TPU v7x, 32 devices: a whole 2x2x4 slice. The times are simulated.
32 devices in a mesh: tile: 16 (over z, y, core), freq: 2 (over x).
Axes of the slice: x: 2, y: 2, z: 4, core: 2. Of those that a mesh axis runs over, the one named last changes fastest.
Arguments:
- wavefield: bfloat16 [8, 2, 16384, 256], P('freq', None, 'tile'), may hold values from -6 to 6
- row_factors: bfloat16 [8, 2, 32768, 1024], P('freq', None, 'tile'), may hold values from -0.125 to 0.125
- col_factors: bfloat16 [8, 2, 16384, 2048], P('freq', None, 'tile'), may hold values from -0.1875 to 0.1875
- window_index: int32 [256], replicated, may hold values from 1 to 15
Outputs:
- adjoint_field: float32 [8, 2, 16384, 256], P('freq', None, 'tile')
All inputs are finite; a program needn't handle non-finite values.
Results may differ from a plain program's by a relative error of at most 0.0038.
Values may be sent and summed in bfloat16 or wider, within the bound.
No kernel may reach another device: no remote copies, remote signals or barrier semaphores. Data moves between devices by JAX's collectives and lax.ppermute only.
A program may use at most 256 MiB of HBM per device.

v0:
```python
import functools
import math

import jax
import jax.numpy as jnp
from jax import lax
from jax.experimental import pallas as pl
from jax.experimental.pallas import tpu as pltpu
from jax.sharding import PartitionSpec as P


TS = 512
RANK = 32
NT = 16
CHUNKS = 2
GROUP = 4
VMEM_BYTES = 67043328


def angles(freq_ids):
    times = lax.broadcasted_iota(jnp.int32, (NT, freq_ids.shape[0]), 0)
    return math.pi / NT * ((2 * freq_ids[None, :] + 1) * times).astype(jnp.float32)


def call(kernel, grid, prefetch, in_specs, out_specs, out_shape, scratch, flops, nbytes, after, **kw):
    count = prefetch + len(in_specs)
    inner = kernel
    if after is not None:
        in_specs = in_specs + [pl.BlockSpec(memory_space=pl.ANY)]

        def inner(*refs):
            kernel(*refs[:count], *refs[count + 1 :])

    made = pl.pallas_call(
        inner,
        grid_spec=pltpu.PrefetchScalarGridSpec(
            num_scalar_prefetch=prefetch,
            grid=grid,
            in_specs=in_specs,
            out_specs=out_specs,
            scratch_shapes=scratch,
        ),
        out_shape=out_shape,
        cost_estimate=pl.CostEstimate(flops=flops, bytes_accessed=nbytes, transcendentals=0),
        compiler_params=pltpu.CompilerParams(vmem_limit_bytes=VMEM_BYTES),
        **kw,
    )
    return made if after is None else lambda *args: made(*args, after)


def dot(left, right):
    return jnp.dot(left, right, preferred_element_type=jnp.float32)


def turned(left, right):
    return lax.dot_general(left, right, (((0,), (0,)), ((), ())), preferred_element_type=jnp.float32)


def project_kernel(dims, pos, v_ref, w_ref, *refs):
    groups, col_local, row_local, width, split = dims
    span = row_local * RANK
    outs = refs[: groups * GROUP if split else 1]
    wave = refs[len(outs)]

    @pl.when(pl.program_id(1) == 0)
    def _():
        wave[:width] = w_ref[0, 0].T
        wave[width:] = w_ref[0, 1].T

    for c in range(col_local):
        rows = slice(c * TS, (c + 1) * TS)
        to = slice(c * RANK, (c + 1) * RANK)
        with_real = dot(wave[:, rows], v_ref[0, 0, rows])
        with_imag = dot(wave[:, rows], v_ref[0, 1, rows])
        real = with_real[:width] + with_imag[width:]
        imag = with_real[width:] - with_imag[:width]
        both = jnp.concatenate([real, imag], 0).astype(jnp.bfloat16).T
        if not split:
            for d in range(GROUP):
                for i in range(row_local):
                    start = d * span + i * RANK
                    outs[0][d, 0, i, to] = both[start : start + RANK]
            continue
        stage = refs[-1]
        stage[...] = both
        for high in range(groups):

            @pl.when(pl.program_id(1) == high)
            def _():
                for low in range(GROUP):
                    base = ((pos[0] % GROUP) ^ low) * span
                    for i in range(row_local):
                        start = pl.multiple_of(base + i * RANK, RANK)
                        outs[high * GROUP + low][0, i, to] = stage[pl.ds(start, RANK)]


def project(pos, col_factors, wavefield, piece, chunk, width, tiles, split, base, groups, after):
    first, freqs = piece
    _, _, src_rows, cols = col_factors.shape
    col_local = src_rows // TS
    row_local = cols // RANK // tiles
    lanes = GROUP * row_local * RANK
    shape = (freqs, row_local, col_local * RANK, 2 * width)
    if split:
        out_specs = [pl.BlockSpec((1,) + shape[1:], lambda f, g, s: (f, 0, 0, 0))] * (groups * GROUP)
        out_shape = [jax.ShapeDtypeStruct(shape, jnp.bfloat16)] * (groups * GROUP)
    else:
        out_specs = pl.BlockSpec((GROUP, 1) + shape[1:], lambda f, g, s: (g, f, 0, 0, 0))
        out_shape = jax.ShapeDtypeStruct((tiles,) + shape, jnp.bfloat16)
    return call(
        functools.partial(project_kernel, (groups, col_local, row_local, width, split)),
        (freqs, groups),
        1,
        [
            pl.BlockSpec(
                (1, 2, src_rows, lanes),
                lambda f, g, s: (first + f, 0, 0, (s[0] // GROUP) ^ (base + g) if split else g),
            ),
            pl.BlockSpec((1, 2, src_rows, width), lambda f, g, s: (first + f, 0, 0, chunk)),
        ],
        out_specs,
        out_shape,
        [pltpu.VMEM((2 * width, src_rows), jnp.bfloat16)]
        + [pltpu.VMEM((lanes, 2 * width), jnp.bfloat16)] * split,
        8 * freqs * src_rows * groups * lanes * width,
        freqs * 4 * src_rows * (groups * lanes + 2 * width),
        after,
    )(pos, col_factors, wavefield)


def gather(pos, got, step, stage):
    if stage is None:
        return got[0][:, 0, 0].reshape(-1, got[0].shape[-1])
    for m, ref in enumerate(got):
        stage[pl.ds(pl.multiple_of((pos[0] ^ m) * step, step), step)] = ref[0, 0]
    return stage[...]


def expand_kernel(dims, pos, u_ref, *refs):
    count, shares, step, width = dims
    got, outs, stage = refs[:count], refs[count : count + shares], refs[count + shares]
    coeffs = gather(pos, got, step, refs[-1] if count > 1 else None)
    with_real = dot(u_ref[0, 0], coeffs)
    with_imag = dot(u_ref[0, 1], coeffs)
    stage[:, :width] = (with_real[:, :width] - with_imag[:, width:]).astype(jnp.bfloat16)
    stage[:, width:] = (with_real[:, width:] + with_imag[:, :width]).astype(jnp.bfloat16)
    share = TS // shares
    for g in range(shares):
        rows = pl.ds(pl.multiple_of((pos[1] ^ g) * share, share), share)
        outs[g][0, 0] = stage[rows]


def gather_specs(got, index):
    step, both = got[0].shape[-2:]
    if len(got) == 1:
        return [pl.BlockSpec((got[0].shape[0], 1, 1, step, both), lambda *n: (0,) + index(*n))], []
    stage = pltpu.VMEM((len(got) * step, both), got[0].dtype)
    return [pl.BlockSpec((1, 1, step, both), index)] * len(got), [stage]


def expand(pos, row_factors, piece, got, shares, after):
    first, freqs = piece
    _, _, rec_rows, cols = row_factors.shape
    row_local = rec_rows // TS
    step, both = got[0].shape[-2:]
    shape = (freqs, row_local, TS // shares, both)
    specs, scratch = gather_specs(got, lambda f, i, s: (f, i, 0, 0))
    return call(
        functools.partial(expand_kernel, (len(got), shares, step, both // 2)),
        (freqs, row_local),
        1,
        [pl.BlockSpec((1, 2, TS, cols), lambda f, i, s: (first + f, 0, i, 0))] + specs,
        [pl.BlockSpec((1, 1, TS // shares, both), lambda f, i, s: (f, i, 0, 0))] * shares,
        [jax.ShapeDtypeStruct(shape, jnp.bfloat16)] * shares,
        [pltpu.VMEM((TS, both), jnp.bfloat16)] + scratch,
        4 * freqs * rec_rows * cols * both,
        freqs * 2 * (rec_rows * (2 * cols + both) + row_local * cols * both),
        after,
    )(pos, row_factors, *got)


def window_kernel(dims, cosine, sine, index_ref, *refs):
    shares, took, gave, rows, slab, width = dims
    ins, outs = refs[: shares * len(took)], refs[shares * len(took) :]
    half = NT // 2
    masks = [t < index_ref[...] for t in range(NT)]

    def planes(arrays, pieces):
        return [
            (arrays[p * shares + g], f)
            for g in range(shares)
            for p, (_, freqs) in enumerate(pieces)
            for f in range(freqs)
        ]

    def body(n, carry):
        at = pl.ds(pl.multiple_of(n * slab, slab), slab)
        real = [ref[f, 0, at, :width].astype(jnp.float32) for ref, f in planes(ins, took)]
        imag = [ref[f, 0, at, width:].astype(jnp.float32) for ref, f in planes(ins, took)]
        count = len(real)
        even = [sum(cosine[t, k] * real[k] for k in range(count)) for t in range(half)]
        odd = [None] + [sum(sine[t, k] * imag[k] for k in range(count)) for t in range(1, half + 1)]
        zero = jnp.zeros_like(real[0])

        def keep(t, value):
            return jnp.where(masks[t], value, zero)

        diff = [keep(0, even[0])]
        total = [None]
        for t in range(1, half):
            one = keep(t, even[t] - odd[t])
            other = keep(NT - t, -even[t] - odd[t])
            diff.append(one - other)
            total.append(one + other)
        total.append(keep(half, -odd[half]))
        for k, (ref, f) in enumerate(planes(outs, gave)):
            out = sum(cosine[t, k] * diff[t] for t in range(half))
            ref[f, 0, at, :width] = out.astype(jnp.bfloat16)
            out = -sum(sine[t, k] * total[t] for t in range(1, half + 1))
            ref[f, 0, at, width:] = out.astype(jnp.bfloat16)
        return carry

    lax.fori_loop(0, rows // slab, body, 0)


def window(cosine, sine, index, parts, took, gave, chunk):
    shares = len(parts[0])
    _, row_local, rows, both = parts[0][0].shape

    def spec(freqs):
        return pl.BlockSpec((freqs, 1, rows, both), lambda i, c, s: (0, i, 0, 0))

    size = sum(part.size for group in parts for part in group)
    made = call(
        functools.partial(window_kernel, (shares, took, gave, rows, 16, both // 2)),
        (row_local,),
        2,
        [pl.BlockSpec((1, both // 2), lambda i, c, s: (0, chunk))]
        + [spec(freqs) for _, freqs in took for _ in range(shares)],
        [spec(freqs) for _, freqs in gave for _ in range(shares)],
        [
            jax.ShapeDtypeStruct((freqs, row_local, rows, both), jnp.bfloat16)
            for _, freqs in gave
            for _ in range(shares)
        ],
        [],
        2 * NT * size,
        4 * size,
        None,
    )(cosine, sine, index, *[part for group in parts for part in group])
    return [made[p * shares : (p + 1) * shares] for p in range(len(gave))]


def contract_kernel(dims, pos, u_ref, *refs):
    tiles, shares, col_local, width, split = dims
    ins, outs = refs[:shares], refs[shares : shares + (tiles if split else 1)]
    stage = refs[shares + len(outs)]
    share = TS // shares
    for g in range(shares):
        stage[pl.ds(pl.multiple_of((pos[1] ^ g) * share, share), share)] = ins[g][0, 0]
    with_real = turned(stage[...], u_ref[0, 0])
    with_imag = turned(stage[...], u_ref[0, 1])
    real = with_real[:width] + with_imag[width:]
    imag = with_real[width:] - with_imag[:width]
    both = jnp.concatenate([real, imag], 0).astype(jnp.bfloat16).T
    if not split:
        outs[0][:, 0] = both.reshape(tiles, col_local, RANK, 2 * width)
        return
    rows = refs[-1]
    rows[...] = both
    for m in range(tiles):
        for c in range(col_local):
            start = ((pos[0] ^ m) * col_local + c) * RANK
            outs[m][0, c] = rows[pl.ds(pl.multiple_of(start, RANK), RANK)]


def contract(pos, row_factors, piece, parts, tiles, split, after):
    first, freqs = piece
    _, _, rec_rows, cols = row_factors.shape
    row_local = rec_rows // TS
    shares = len(parts)
    share, both = parts[0].shape[2:]
    col_local = cols // RANK // tiles
    shape = (freqs, col_local, row_local * RANK, both)
    if split:
        out_specs = [pl.BlockSpec((1, col_local, RANK, both), lambda f, i, s: (f, 0, i, 0))] * tiles
        out_shape = [jax.ShapeDtypeStruct(shape, jnp.bfloat16)] * tiles
    else:
        out_specs = pl.BlockSpec((tiles, 1, col_local, RANK, both), lambda f, i, s: (0, f, 0, i, 0))
        out_shape = jax.ShapeDtypeStruct((tiles,) + shape, jnp.bfloat16)
    return call(
        functools.partial(contract_kernel, (tiles, shares, col_local, both // 2, split)),
        (freqs, row_local),
        1,
        [pl.BlockSpec((1, 2, TS, cols), lambda f, i, s: (first + f, 0, i, 0))]
        + [pl.BlockSpec((1, 1, share, both), lambda f, i, s: (f, i, 0, 0))] * shares,
        out_specs,
        out_shape,
        [pltpu.VMEM((TS, both), jnp.bfloat16)] + [pltpu.VMEM((cols, both), jnp.bfloat16)] * split,
        4 * freqs * rec_rows * cols * both,
        freqs * 2 * (rec_rows * (2 * cols + both) + row_local * cols * both),
        after,
    )(pos, row_factors, *parts)


def spread_kernel(dims, pos, v_ref, *refs):
    count, carried, step, width = dims
    got, out = refs[:count], refs[count + carried]
    coeffs = gather(pos, got, step, refs[-1] if count > 1 else None)
    with_real = dot(v_ref[0, 0], coeffs)
    with_imag = dot(v_ref[0, 1], coeffs)
    out[0, 0] = with_real[:, :width] - with_imag[:, width:]
    out[0, 1] = with_real[:, width:] + with_imag[:, :width]


def spread(pos, col_factors, piece, got, chunk, points, before, after):
    first, freqs = piece
    total, _, src_rows, cols = col_factors.shape
    step, both = got[0].shape[-2:]
    carried = 0 if before is None else 1
    specs, scratch = gather_specs(got, lambda f, c, s: (f, c, 0, 0))
    return call(
        functools.partial(spread_kernel, (len(got), carried, step, both // 2)),
        (freqs, src_rows // TS),
        1,
        [pl.BlockSpec((1, 2, TS, cols), lambda f, c, s: (first + f, 0, c, 0))]
        + specs
        + [pl.BlockSpec(memory_space=pl.ANY)] * carried,
        pl.BlockSpec((1, 2, TS, both // 2), lambda f, c, s: (first + f, 0, c, chunk)),
        jax.ShapeDtypeStruct((total, 2, src_rows, points), jnp.float32),
        scratch,
        4 * freqs * src_rows * cols * both,
        freqs * 4 * (src_rows * (cols + both) + cols * both),
        after,
        input_output_aliases={2 + len(got): 0} if carried else {},
    )(pos, col_factors, *got, *([before] if carried else []))


def send(array, axis, size, mask):
    if mask == 0:
        return array
    return lax.ppermute(array, axis, [(n, n ^ mask) for n in range(size)])


def trade(made, tiles, split):
    if not split:
        return [lax.all_to_all(made, "tile", 0, 0, tiled=True)]
    got = list(made)
    for m in reversed(range(tiles)):
        got[m] = send(made[m], "tile", tiles, m)
    return got


def local(tiles, shares, wavefield, row_factors, col_factors, window_index):
    freqs = wavefield.shape[0]
    points = wavefield.shape[3]
    width = points // CHUNKS
    share = lax.axis_index("freq")
    pos = jnp.stack([lax.axis_index("tile"), share]).astype(jnp.int32)
    owners = share ^ lax.iota(jnp.int32, shares)
    ids = (owners[:, None] * freqs + lax.iota(jnp.int32, freqs)[None, :]).reshape(-1)
    phases = angles(ids)
    cosine = 0.25 * jnp.cos(phases)
    sine = 0.25 * jnp.sin(phases)
    index = window_index.reshape(1, points)

    took = gave = [((0, freqs, False),)] * CHUNKS
    if freqs > 2:
        took = [((0, 1, True), (1, freqs - 1, False))] + took[1:]
        gave = gave[:-1] + [((0, 1, True), (1, freqs - 2, False), (freqs - 1, 1, True))]

    def runs(pieces):
        return tuple(piece[:2] for piece in pieces)

    sent = []
    token = None
    for h in range(CHUNKS):
        sent.append([])
        for *piece, split in took[h]:
            groups = tiles // GROUP
            half = groups // 2 if split else groups
            made = []
            for base in reversed(range(0, groups, half)):
                part = project(
                    pos, col_factors, wavefield, piece, h, width, tiles, split, base, half, token
                )
                token = part[0] if split else part
                made = [part] + made
            made = [*made[0], *made[1]] if split else made[0]
            sent[h].append(trade(made, tiles, split))
    back = []
    for h in range(CHUNKS):
        parts = []
        for n, (*piece, split) in enumerate(took[h]):
            made = expand(pos, row_factors, piece, sent[h][n], shares, token)
            token = made[0]
            parts.append([send(part, "freq", shares, m) for m, part in enumerate(made)])
        parts = window(cosine, sine, index, parts, runs(took[h]), runs(gave[h]), h)
        parts = [[send(part, "freq", shares, m) for m, part in enumerate(group)] for group in parts]
        back.append([])
        token = None
        for n, (*piece, split) in enumerate(gave[h]):
            if n == 2:
                token = back[h - 1][0][0]
            made = contract(pos, row_factors, piece, parts[n], tiles, split, token)
            token = made[0] if split else made
            back[h].append(trade(made, tiles, split))
    result = None
    for h in range(CHUNKS):
        for n, (*piece, split) in enumerate(gave[h]):
            result = spread(pos, col_factors, piece, back[h][n], h, points, result, token)
            token = None
    return result


def solution(mesh):
    spec = P("freq", None, "tile", None)
    body = functools.partial(local, mesh.shape["tile"], mesh.shape["freq"])
    return jax.shard_map(
        body, mesh=mesh, in_specs=(spec, spec, spec, P()), out_specs=spec, check_vma=False
    )
```

profile of v0, /device:TPU:1, one launch (start us, length us, event | category | flops | bytes accessed | tf_op | source)
XLA Modules:
  0.0 985.7 jit_solution(6815738407858050161)
XLA Ops:
  0.7 5.8 shard_map.46
  6.4 5.8 shard_map.47
  12.3 18.9 %shard_map.48.refs_3_ = bf16[16,3,4,64,256]{4,3,2,1,0:T(8,128)(2,1)} custom-call(s32[2]{0:T(128)} %pad_add_fusion.pos.refs_0_, bf16[4,2,1024,2048]{3,2,1,0:T(8,128)(2,1)} %v_ref.7, bf16[4,2,1024,256]{3,2,1,0:T(8,128)(2,1)} %refs_2_.5, bf16[1,4,64,256]{3,2,1,0:T(8,128)(2,1)} %get-tuple-element.68.refs_3_.refs_2_), custom_call_target="tpu_custom_call" | custom-call | flops 6442450944 | bytes 28311552 | tf_op jit(solution)/shard_map/pallas_call | solution.py:48
  31.1 7.3 all-to-all-start.1
  38.5 24.4 %shard_map.49.refs_18_ = bf16[16,4,4,64,256]{4,3,2,1,0:T(8,128)(2,1)} custom-call(s32[2]{0:T(128)} %pad_add_fusion.pos.refs_0_, bf16[4,2,1024,2048]{3,2,1,0:T(8,128)(2,1)} %v_ref.7, bf16[4,2,1024,256]{3,2,1,0:T(8,128)(2,1)} %refs_2_.5, bf16[16,3,4,64,256]{4,3,2,1,0:T(8,128)(2,1)} %shard_map.48.refs_3_), custom_call_target="tpu_custom_call" | custom-call | flops 8589934592 | bytes 37748736 | tf_op jit(solution)/shard_map/pallas_call | solution.py:48
  63.0 90.1 %all-to-all-done.1.refs_2_ = bf16[16,3,4,64,256]{4,3,2,1,0:T(8,128)(2,1)} async-done(((bf16[16,3,4,64,256]{4,3,2,1,0:T(8,128)(2,1)}), bf16[16,3,4,64,256]{4,3,2,1,0:T(8,128)(2,1)}, u32[]{:S(2)}, u32[]{:S(2)}) %all-to-all-start.1) | async-done | bytes 6291488 | tf_op jit(solution)/shard_map/all_to_all | solution.py:347
  153.1 27.5 %all-to-all-start = ((bf16[16,4,4,64,256]{4,3,2,1,0:T(8,128)(2,1)}), bf16[16,4,4,64,256]{4,3,2,1,0:T(8,128)(2,1)}, u32[]{:S(2)}, u32[]{:S(2)}) async-start(bf16[16,4,4,64,256]{4,3,2,1,0:T(8,128)(2,1)} %shard_map.49.refs_18_), calls=%async_computation | async-start | bytes 16777216 | tf_op jit(solution)/shard_map/all_to_all | solution.py:347
  180.7 2.7 collective-permute-start.8
  190.4 191.1 %collective-permute-done.8.refs_11_ = bf16[1,4,64,256]{3,2,1,0:T(8,128)(2,1)} collective-permute-done((bf16[1,4,64,256]{3,2,1,0:T(8,128)(2,1)S(1)}, bf16[1,4,64,256]{3,2,1,0:T(8,128)(2,1)}, u32[]{:S(2)}, u32[]{:S(2)}) %collective-permute-start.8) | collective-permute-done | bytes 131104 | tf_op jit(solution)/shard_map/ppermute | solution.py:342
  386.9 8.1 collective-permute-done.10.refs_13_
  397.3 10.6 %collective-permute-start.3 = (bf16[1,4,64,256]{3,2,1,0:T(8,128)(2,1)S(1)}, bf16[1,4,64,256]{3,2,1,0:T(8,128)(2,1)}, u32[]{:S(2)}, u32[]{:S(2)}) collective-permute-start(bf16[1,4,64,256]{3,2,1,0:T(8,128)(2,1)S(1)} %copy-done.9), channel_id=1, source_target_pairs={{0,8},{2,10},{4,12},{6,14},{8,0},{10,2},{12,4},{14,6},{16,24},{18,... | collective-permute-start | bytes 393224 | tf_op jit(solution)/shard_map/ppermute | solution.py:342
  410.0 2.7 collective-permute-start.5
  414.7 4.1 collective-permute-done.5.refs_8_
  421.1 7.4 shard_map.50
  428.5 18.1 %shard_map.51 = (bf16[3,4,256,256]{3,2,1,0:T(8,128)(2,1)}, bf16[3,4,256,256]{3,2,1,0:T(8,128)(2,1)}) custom-call(s32[2]{0:T(128)} %pad_add_fusion.pos.refs_0_, bf16[4,2,2048,1024]{3,2,1,0:T(8,128)(2,1)} %refs_1_.16, bf16[16,3,4,64,256]{4,3,2,1,0:T(8,128)(2,1)} %all-to-all-done.1.refs_2_, bf16[1,4,256,256]{3,2,1,0:T(8,128)(2,1)} %get-tuple-element.83.refs_3_.refs_0_), custom_call_target="tpu_custom_call" | custom-call | flops 6442450944 | bytes 34603008 | tf_op jit(solution)/shard_map/pallas_call | solution.py:48
  448.9 44.5 %collective-permute-done.15.refs_1_ = bf16[1,4,256,256]{3,2,1,0:T(8,128)(2,1)} collective-permute-done((bf16[1,4,256,256]{3,2,1,0:T(8,128)(2,1)}, bf16[1,4,256,256]{3,2,1,0:T(8,128)(2,1)}, u32[]{:S(2)}, u32[]{:S(2)}) %collective-permute-start.15) | collective-permute-done | bytes 524320 | tf_op jit(solution)/shard_map/ppermute | solution.py:342
  493.4 16.0 %shard_map.52 = (bf16[4,4,256,256]{3,2,1,0:T(8,128)(2,1)}, bf16[4,4,256,256]{3,2,1,0:T(8,128)(2,1)}) custom-call(f32[16,8]{1,0:T(8,128)} %get-tuple-element.130.cosine, f32[16,8]{1,0:T(8,128)} %get-tuple-element.129.sine, s32[1,256]{1,0:T(1,128)} %bitcast.3, bf16[1,4,256,256]{3,2,1,0:T(8,128)(2,1)} %get-tuple-element.83.refs_3_.refs_0_, ...), custom_call_target="tpu_custom_call" | custom-call | flops 67108864 | bytes 8388608 | tf_op jit(solution)/shard_map/pallas_call | solution.py:234
  510.6 44.7 %collective-permute-done.17.refs_1_ = bf16[4,4,256,256]{3,2,1,0:T(8,128)(2,1)} collective-permute-done((bf16[4,4,256,256]{3,2,1,0:T(8,128)(2,1)}, bf16[4,4,256,256]{3,2,1,0:T(8,128)(2,1)}, u32[]{:S(2)}, u32[]{:S(2)}) %collective-permute-start.17) | collective-permute-done | bytes 2097184 | tf_op jit(solution)/shard_map/ppermute | solution.py:342
  555.3 24.6 %shard_map.53.refs_3_ = bf16[16,4,2,128,256]{4,3,2,1,0:T(8,128)(2,1)} custom-call(s32[2]{0:T(128)} %pad_add_fusion.pos.refs_0_, bf16[4,2,2048,1024]{3,2,1,0:T(8,128)(2,1)} %refs_1_.16, bf16[4,4,256,256]{3,2,1,0:T(8,128)(2,1)} %get-tuple-element.87.refs_0_, bf16[4,4,256,256]{3,2,1,0:T(8,128)(2,1)} %collective-permute-done.17.refs_1_), custom_call_target="tpu_custom_call" | custom-call | flops 8589934592 | bytes 46137344 | tf_op jit(solution)/shard_map/pallas_call | solution.py:291
  579.9 6.9 all-to-all-start.2
  586.8 23.5 %shard_map.54 = (bf16[4,4,256,256]{3,2,1,0:T(8,128)(2,1)}, bf16[4,4,256,256]{3,2,1,0:T(8,128)(2,1)}) custom-call(s32[2]{0:T(128)} %pad_add_fusion.pos.refs_0_, bf16[4,2,2048,1024]{3,2,1,0:T(8,128)(2,1)} %refs_1_.16, bf16[16,4,4,64,256]{4,3,2,1,0:T(8,128)(2,1)} %all-to-all-done.refs_2_, bf16[16,4,2,128,256]{4,3,2,1,0:T(8,128)(2,1)} %shard_map.53.refs_3_), custom_call_target="tpu_custom_call" | custom-call | flops 8589934592 | bytes 46137344 | tf_op jit(solution)/shard_map/pallas_call | solution.py:48
  611.5 46.0 %collective-permute-done.18.refs_1_ = bf16[4,4,256,256]{3,2,1,0:T(8,128)(2,1)} collective-permute-done((bf16[4,4,256,256]{3,2,1,0:T(8,128)(2,1)}, bf16[4,4,256,256]{3,2,1,0:T(8,128)(2,1)}, u32[]{:S(2)}, u32[]{:S(2)}) %collective-permute-start.18) | collective-permute-done | bytes 2097184 | tf_op jit(solution)/shard_map/ppermute | solution.py:342
  657.5 16.0 %shard_map.55 = (bf16[1,4,256,256]{3,2,1,0:T(8,128)(2,1)}, bf16[1,4,256,256]{3,2,1,0:T(8,128)(2,1)}, bf16[2,4,256,256]{3,2,1,0:T(8,128)(2,1)}, bf16[2,4,256,256]...) custom-call(f32[16,8]{1,0:T(8,128)} %get-tuple-element.130.cosine, ...), custom_call_target="tpu_custom_call" | custom-call | flops 67108864 | bytes 8388608 | tf_op jit(solution)/shard_map/pallas_call | solution.py:234
  675.0 33.7 %collective-permute-done.36.refs_1_ = bf16[1,4,256,256]{3,2,1,0:T(8,128)(2,1)} collective-permute-done((bf16[1,4,256,256]{3,2,1,0:T(8,128)(2,1)}, bf16[1,4,256,256]{3,2,1,0:T(8,128)(2,1)}, u32[]{:S(2)}, u32[]{:S(2)}) %collective-permute-start.36) | collective-permute-done | bytes 524320 | tf_op jit(solution)/shard_map/ppermute | solution.py:342
  708.6 7.8 shard_map.57
  716.5 13.4 %shard_map.58 = bf16[16,2,2,128,256]{4,3,2,1,0:T(8,128)(2,1)} custom-call(s32[2]{0:T(128)} %pad_add_fusion.pos.refs_0_, bf16[4,2,2048,1024]{3,2,1,0:T(8,128)(2,1)} %refs_1_.16, bf16[2,4,256,256]{3,2,1,0:T(8,128)(2,1)} %get-tuple-element.109.refs_2_, bf16[2,4,256,256]{3,2,1,0:T(8,128)(2,1)} %collective-permute-done.35.refs_3_, ...), custom_call_target="tpu_custom_call" | custom-call | flops 4294967296 | bytes 23068672 | tf_op jit(solution)/shard_map/pallas_call | solution.py:48
  730.0 8.1 all-to-all-done.2.refs_4_.refs_2_
  738.1 35.9 %all-to-all-start.3 = ((bf16[16,2,2,128,256]{4,3,2,1,0:T(8,128)(2,1)}), bf16[16,2,2,128,256]{4,3,2,1,0:T(8,128)(2,1)}, u32[]{:S(2)}, u32[]{:S(2)}) async-start(bf16[16,2,2,128,256]{4,3,2,1,0:T(8,128)(2,1)} %shard_map.58), calls=%async_computation.3 | async-start | bytes 8388608 | tf_op jit(solution)/shard_map/all_to_all | solution.py:347
  779.0 8.5 collective-permute-done.19.refs_3_
  790.9 11.7 %collective-permute-done.38.refs_2_ = bf16[1,2,128,256]{3,2,1,0:T(8,128)(2,1)} collective-permute-done((bf16[1,2,128,256]{3,2,1,0:T(8,128)(2,1)S(1)}, bf16[1,2,128,256]{3,2,1,0:T(8,128)(2,1)}, u32[]{:S(2)}, u32[]{:S(2)}) %collective-permute-start.38) | collective-permute-done | bytes 131104 | tf_op jit(solution)/shard_map/ppermute | solution.py:342
  807.1 37.9 %collective-permute-done.40.refs_4_ = bf16[1,2,128,256]{3,2,1,0:T(8,128)(2,1)} collective-permute-done((bf16[1,2,128,256]{3,2,1,0:T(8,128)(2,1)S(1)}, bf16[1,2,128,256]{3,2,1,0:T(8,128)(2,1)}, u32[]{:S(2)}, u32[]{:S(2)}) %collective-permute-start.40) | collective-permute-done | bytes 131104 | tf_op jit(solution)/shard_map/ppermute | solution.py:342
  845.0 5.3 collective-permute-start.45
  850.3 3.5 collective-permute-start.46
  853.8 5.7 collective-permute-start.47
  859.6 24.5 %collective-permute-done.44.refs_8_ = bf16[1,2,128,256]{3,2,1,0:T(8,128)(2,1)} collective-permute-done((bf16[1,2,128,256]{3,2,1,0:T(8,128)(2,1)S(1)}, bf16[1,2,128,256]{3,2,1,0:T(8,128)(2,1)}, u32[]{:S(2)}, u32[]{:S(2)}) %collective-permute-start.44) | collective-permute-done | bytes 131104 | tf_op jit(solution)/shard_map/ppermute | solution.py:342
  884.1 4.3 collective-permute-start.49
  889.7 3.7 collective-permute-done.46.refs_10_
  893.4 7.1 collective-permute-start.51
  900.5 7.9 shard_map.56
  910.7 3.1 collective-permute-start.24
  913.8 19.3 %shard_map.59.refs_16_ = f32[4,2,1024,256]{3,2,1,0:T(8,128)} custom-call(s32[2]{0:T(128)} %pad_add_fusion.pos.refs_0_, bf16[4,2,1024,2048]{3,2,1,0:T(8,128)(2,1)} %v_ref.7, bf16[16,4,2,128,256]{4,3,2,1,0:T(8,128)(2,1)} %all-to-all-done.2.refs_4_.refs_2_, bf16[1,2,128,256]{3,2,1,0:T(8,128)(2,1)} %get-tuple-element.93.refs_3_.refs_0_), custom_call_target="tpu_custom_call" | custom-call | flops 8589934592 | bytes 46137344 | tf_op jit(solution)/shard_map/pallas_call | solution.py:48
  933.1 2.8 collective-permute-start.26
  940.1 6.7 shard_map.60.refs_1_
  950.0 2.8 collective-permute-start.32
  952.8 9.9 %collective-permute-done.28.refs_9_ = bf16[1,2,128,256]{3,2,1,0:T(8,128)(2,1)} collective-permute-done((bf16[1,2,128,256]{3,2,1,0:T(8,128)(2,1)}, bf16[1,2,128,256]{3,2,1,0:T(8,128)(2,1)}, u32[]{:S(2)}, u32[]{:S(2)}) %collective-permute-start.28) | collective-permute-done | bytes 131104 | tf_op jit(solution)/shard_map/ppermute | solution.py:342
  963.9 3.9 collective-permute-start.34
  967.8 11.0 %shard_map.61.refs_16_ = f32[4,2,1024,256]{3,2,1,0:T(8,128)} custom-call(s32[2]{0:T(128)} %pad_add_fusion.pos.refs_0_, bf16[4,2,1024,2048]{3,2,1,0:T(8,128)(2,1)} %v_ref.7, bf16[16,2,2,128,256]{4,3,2,1,0:T(8,128)(2,1)} %all-to-all-done.3.refs_0_, f32[4,2,1024,256]{3,2,1,0:T(8,128)} %shard_map.60.refs_1_), custom_call_target="tpu_custom_call", output_to_operand_aliasing={{}: (3, {})} | custom-call | flops 4294967296 | bytes 23068672 | tf_op jit(solution)/shard_map/pallas_call | solution.py:322
  978.8 6.7 shard_map.62
  (146 shorter events, 53.2 us)
Async XLA Ops:
  31.1 122.0 %all-to-all-start.1 = ((bf16[16,3,4,64,256]{4,3,2,1,0:T(8,128)(2,1)}), bf16[16,3,4,64,256]{4,3,2,1,0:T(8,128)(2,1)}, u32[]{:S(2)}, u32[]{:S(2)}) async-start(bf16[16,3,4,64,256]{4,3,2,1,0:T(8,128)(2,1)} %shard_map.48.refs_3_), calls=%async_computation.1 | async-start | bytes 12582912 | tf_op jit(solution)/shard_map/all_to_all | solution.py:347
  153.1 426.8 %all-to-all-start = ((bf16[16,4,4,64,256]{4,3,2,1,0:T(8,128)(2,1)}), bf16[16,4,4,64,256]{4,3,2,1,0:T(8,128)(2,1)}, u32[]{:S(2)}, u32[]{:S(2)}) async-start(bf16[16,4,4,64,256]{4,3,2,1,0:T(8,128)(2,1)} %shard_map.49.refs_18_), calls=%async_computation | async-start | bytes 16777216 | tf_op jit(solution)/shard_map/all_to_all | solution.py:347
  180.7 200.8 %collective-permute-start.8 = (bf16[1,4,64,256]{3,2,1,0:T(8,128)(2,1)S(1)}, bf16[1,4,64,256]{3,2,1,0:T(8,128)(2,1)}, u32[]{:S(2)}, u32[]{:S(2)}) collective-permute-start(bf16[1,4,64,256]{3,2,1,0:T(8,128)(2,1)S(1)} %copy-done.29), channel_id=1, source_target_pairs={{0,18},{2,16},{4,22},{6,20},{8,26},{10,24},{12,30},{14,28},{16,2},... | collective-permute-start | bytes 393224 | tf_op jit(solution)/shard_map/ppermute | solution.py:342
  183.3 201.0 %collective-permute-start.9 = (bf16[1,4,64,256]{3,2,1,0:T(8,128)(2,1)S(1)}, bf16[1,4,64,256]{3,2,1,0:T(8,128)(2,1)}, u32[]{:S(2)}, u32[]{:S(2)}) collective-permute-start(bf16[1,4,64,256]{3,2,1,0:T(8,128)(2,1)S(1)} %copy-done.28), channel_id=1, source_target_pairs={{0,20},{2,22},{4,16},{6,18},{8,28},{10,30},{12,24},{14,26},{16,4},... | collective-permute-start | bytes 393224 | tf_op jit(solution)/shard_map/ppermute | solution.py:342
  184.4 210.6 %collective-permute-start.10 = (bf16[1,4,64,256]{3,2,1,0:T(8,128)(2,1)S(1)}, bf16[1,4,64,256]{3,2,1,0:T(8,128)(2,1)}, u32[]{:S(2)}, u32[]{:S(2)}) collective-permute-start(bf16[1,4,64,256]{3,2,1,0:T(8,128)(2,1)S(1)} %copy-done.26), channel_id=1, source_target_pairs={{0,22},{2,20},{4,18},{6,16},{8,30},{10,28},{12,26},{14,24},{16,6},... | collective-permute-start | bytes 393224 | tf_op jit(solution)/shard_map/ppermute | solution.py:342
  186.8 208.2 %collective-permute-start.11 = (bf16[1,4,64,256]{3,2,1,0:T(8,128)(2,1)S(1)}, bf16[1,4,64,256]{3,2,1,0:T(8,128)(2,1)}, u32[]{:S(2)}, u32[]{:S(2)}) collective-permute-start(bf16[1,4,64,256]{3,2,1,0:T(8,128)(2,1)S(1)} %copy-done.24), channel_id=1, source_target_pairs={{0,24},{2,26},{4,28},{6,30},{8,16},{10,18},{12,20},{14,22},{16,8},... | collective-permute-start | bytes 393224 | tf_op jit(solution)/shard_map/ppermute | solution.py:342
  188.0 207.1 %collective-permute-start.12 = (bf16[1,4,64,256]{3,2,1,0:T(8,128)(2,1)S(1)}, bf16[1,4,64,256]{3,2,1,0:T(8,128)(2,1)}, u32[]{:S(2)}, u32[]{:S(2)}) collective-permute-start(bf16[1,4,64,256]{3,2,1,0:T(8,128)(2,1)S(1)} %copy-done.22), channel_id=1, source_target_pairs={{0,26},{2,24},{4,30},{6,28},{8,18},{10,16},{12,22},{14,20},{16,10}... | collective-permute-start | bytes 393224 | tf_op jit(solution)/shard_map/ppermute | solution.py:342
  395.1 14.3 %collective-permute-start = (bf16[1,4,64,256]{3,2,1,0:T(8,128)(2,1)S(1)}, bf16[1,4,64,256]{3,2,1,0:T(8,128)(2,1)S(1)}, u32[]{:S(2)}, u32[]{:S(2)}) collective-permute-start(bf16[1,4,64,256]{3,2,1,0:T(8,128)(2,1)S(1)} %copy-done.15), channel_id=1, source_target_pairs={{0,2},{2,0},{4,6},{6,4},{8,10},{10,8},{12,14},{14,12},{16,18},{18,... | collective-permute-start | bytes 393224 | tf_op jit(solution)/shard_map/ppermute | solution.py:342
  395.2 17.6 %collective-permute-start.1 = (bf16[1,4,64,256]{3,2,1,0:T(8,128)(2,1)S(1)}, bf16[1,4,64,256]{3,2,1,0:T(8,128)(2,1)}, u32[]{:S(2)}, u32[]{:S(2)}) collective-permute-start(bf16[1,4,64,256]{3,2,1,0:T(8,128)(2,1)S(1)} %copy-done.13), channel_id=1, source_target_pairs={{0,4},{2,6},{4,0},{6,2},{8,12},{10,14},{12,8},{14,10},{16,20},{18,... | collective-permute-start | bytes 393224 | tf_op jit(solution)/shard_map/ppermute | solution.py:342
  395.5 18.0 %collective-permute-start.2 = (bf16[1,4,64,256]{3,2,1,0:T(8,128)(2,1)S(1)}, bf16[1,4,64,256]{3,2,1,0:T(8,128)(2,1)}, u32[]{:S(2)}, u32[]{:S(2)}) collective-permute-start(bf16[1,4,64,256]{3,2,1,0:T(8,128)(2,1)S(1)} %copy-done.11), channel_id=1, source_target_pairs={{0,6},{2,4},{4,2},{6,0},{8,14},{10,12},{12,10},{14,8},{16,22},{18,... | collective-permute-start | bytes 393224 | tf_op jit(solution)/shard_map/ppermute | solution.py:342
  397.3 16.2 %collective-permute-start.3 = (bf16[1,4,64,256]{3,2,1,0:T(8,128)(2,1)S(1)}, bf16[1,4,64,256]{3,2,1,0:T(8,128)(2,1)}, u32[]{:S(2)}, u32[]{:S(2)}) collective-permute-start(bf16[1,4,64,256]{3,2,1,0:T(8,128)(2,1)S(1)} %copy-done.9), channel_id=1, source_target_pairs={{0,8},{2,10},{4,12},{6,14},{8,0},{10,2},{12,4},{14,6},{16,24},{18,... | collective-permute-start | bytes 393224 | tf_op jit(solution)/shard_map/ppermute | solution.py:342
  446.6 46.8 %collective-permute-start.16 = (bf16[3,4,256,256]{3,2,1,0:T(8,128)(2,1)}, bf16[3,4,256,256]{3,2,1,0:T(8,128)(2,1)}, u32[]{:S(2)}, u32[]{:S(2)}) collective-permute-start(bf16[3,4,256,256]{3,2,1,0:T(8,128)(2,1)} %get-tuple-element.86), channel_id=1, source_target_pairs={{0,1},{1,0},{2,3},{3,2},{4,5},{5,4},{6,7},{7,6},{8,9},{9,8},{10,11... | collective-permute-start | bytes 4718600 | tf_op jit(solution)/shard_map/ppermute | solution.py:342
  447.8 45.5 %collective-permute-start.15 = (bf16[1,4,256,256]{3,2,1,0:T(8,128)(2,1)}, bf16[1,4,256,256]{3,2,1,0:T(8,128)(2,1)}, u32[]{:S(2)}, u32[]{:S(2)}) collective-permute-start(bf16[1,4,256,256]{3,2,1,0:T(8,128)(2,1)} %get-tuple-element.84), channel_id=1, source_target_pairs={{0,1},{1,0},{2,3},{3,2},{4,5},{5,4},{6,7},{7,6},{8,9},{9,8},{10,11... | collective-permute-start | bytes 1572872 | tf_op jit(solution)/shard_map/ppermute | solution.py:342
  509.4 45.9 %collective-permute-start.17 = (bf16[4,4,256,256]{3,2,1,0:T(8,128)(2,1)}, bf16[4,4,256,256]{3,2,1,0:T(8,128)(2,1)}, u32[]{:S(2)}, u32[]{:S(2)}) collective-permute-start(bf16[4,4,256,256]{3,2,1,0:T(8,128)(2,1)} %get-tuple-element.88), channel_id=1, source_target_pairs={{0,1},{1,0},{2,3},{3,2},{4,5},{5,4},{6,7},{7,6},{8,9},{9,8},{10,11... | collective-permute-start | bytes 6291464 | tf_op jit(solution)/shard_map/ppermute | solution.py:342
  579.9 158.2 %all-to-all-start.2 = ((bf16[16,4,2,128,256]{4,3,2,1,0:T(8,128)(2,1)}), bf16[16,4,2,128,256]{4,3,2,1,0:T(8,128)(2,1)}, u32[]{:S(2)}, u32[]{:S(2)}) async-start(bf16[16,4,2,128,256]{4,3,2,1,0:T(8,128)(2,1)} %shard_map.53.refs_3_), calls=%async_computation.2 | async-start | bytes 16777216 | tf_op jit(solution)/shard_map/all_to_all | solution.py:347
  610.3 47.2 %collective-permute-start.18 = (bf16[4,4,256,256]{3,2,1,0:T(8,128)(2,1)}, bf16[4,4,256,256]{3,2,1,0:T(8,128)(2,1)}, u32[]{:S(2)}, u32[]{:S(2)}) collective-permute-start(bf16[4,4,256,256]{3,2,1,0:T(8,128)(2,1)} %get-tuple-element.90), channel_id=1, source_target_pairs={{0,1},{1,0},{2,3},{3,2},{4,5},{5,4},{6,7},{7,6},{8,9},{9,8},{10,11... | collective-permute-start | bytes 6291464 | tf_op jit(solution)/shard_map/ppermute | solution.py:342
  673.5 43.0 %collective-permute-start.35 = (bf16[2,4,256,256]{3,2,1,0:T(8,128)(2,1)}, bf16[2,4,256,256]{3,2,1,0:T(8,128)(2,1)}, u32[]{:S(2)}, u32[]{:S(2)}) collective-permute-start(bf16[2,4,256,256]{3,2,1,0:T(8,128)(2,1)} %get-tuple-element.110), channel_id=1, source_target_pairs={{0,1},{1,0},{2,3},{3,2},{4,5},{5,4},{6,7},{7,6},{8,9},{9,8},{10,11... | collective-permute-start | bytes 3145736 | tf_op jit(solution)/shard_map/ppermute | solution.py:342
  674.7 33.9 %collective-permute-start.36 = (bf16[1,4,256,256]{3,2,1,0:T(8,128)(2,1)}, bf16[1,4,256,256]{3,2,1,0:T(8,128)(2,1)}, u32[]{:S(2)}, u32[]{:S(2)}) collective-permute-start(bf16[1,4,256,256]{3,2,1,0:T(8,128)(2,1)} %get-tuple-element.112), channel_id=1, source_target_pairs={{0,1},{1,0},{2,3},{3,2},{4,5},{5,4},{6,7},{7,6},{8,9},{9,8},{10,11... | collective-permute-start | bytes 1572872 | tf_op jit(solution)/shard_map/ppermute | solution.py:342
  738.1 229.7 %all-to-all-start.3 = ((bf16[16,2,2,128,256]{4,3,2,1,0:T(8,128)(2,1)}), bf16[16,2,2,128,256]{4,3,2,1,0:T(8,128)(2,1)}, u32[]{:S(2)}, u32[]{:S(2)}) async-start(bf16[16,2,2,128,256]{4,3,2,1,0:T(8,128)(2,1)} %shard_map.58), calls=%async_computation.3 | async-start | bytes 8388608 | tf_op jit(solution)/shard_map/all_to_all | solution.py:347
  775.3 14.5 %collective-permute-start.37 = (bf16[1,2,128,256]{3,2,1,0:T(8,128)(2,1)S(1)}, bf16[1,2,128,256]{3,2,1,0:T(8,128)(2,1)}, u32[]{:S(2)}, u32[]{:S(2)}) collective-permute-start(bf16[1,2,128,256]{3,2,1,0:T(8,128)(2,1)S(1)} %copy-done.27), channel_id=1, source_target_pairs={{0,2},{2,0},{4,6},{6,4},{8,10},{10,8},{12,14},{14,12},{16,18},{18,... | collective-permute-start | bytes 393224 | tf_op jit(solution)/shard_map/ppermute | solution.py:342
  775.7 26.9 %collective-permute-start.38 = (bf16[1,2,128,256]{3,2,1,0:T(8,128)(2,1)S(1)}, bf16[1,2,128,256]{3,2,1,0:T(8,128)(2,1)}, u32[]{:S(2)}, u32[]{:S(2)}) collective-permute-start(bf16[1,2,128,256]{3,2,1,0:T(8,128)(2,1)S(1)} %copy-done.25), channel_id=1, source_target_pairs={{0,4},{2,6},{4,0},{6,2},{8,12},{10,14},{12,8},{14,10},{16,20},{18,... | collective-permute-start | bytes 393224 | tf_op jit(solution)/shard_map/ppermute | solution.py:342
  777.3 28.7 %collective-permute-start.39 = (bf16[1,2,128,256]{3,2,1,0:T(8,128)(2,1)S(1)}, bf16[1,2,128,256]{3,2,1,0:T(8,128)(2,1)}, u32[]{:S(2)}, u32[]{:S(2)}) collective-permute-start(bf16[1,2,128,256]{3,2,1,0:T(8,128)(2,1)S(1)} %copy-done.23), channel_id=1, source_target_pairs={{0,6},{2,4},{4,2},{6,0},{8,14},{10,12},{12,10},{14,8},{16,22},{18,... | collective-permute-start | bytes 393224 | tf_op jit(solution)/shard_map/ppermute | solution.py:342
  777.4 67.5 %collective-permute-start.40 = (bf16[1,2,128,256]{3,2,1,0:T(8,128)(2,1)S(1)}, bf16[1,2,128,256]{3,2,1,0:T(8,128)(2,1)}, u32[]{:S(2)}, u32[]{:S(2)}) collective-permute-start(bf16[1,2,128,256]{3,2,1,0:T(8,128)(2,1)S(1)} %copy-done.21), channel_id=1, source_target_pairs={{0,8},{2,10},{4,12},{6,14},{8,0},{10,2},{12,4},{14,6},{16,24},{18,... | collective-permute-start | bytes 393224 | tf_op jit(solution)/shard_map/ppermute | solution.py:342
  787.5 62.8 %collective-permute-start.41 = (bf16[1,2,128,256]{3,2,1,0:T(8,128)(2,1)S(1)}, bf16[1,2,128,256]{3,2,1,0:T(8,128)(2,1)}, u32[]{:S(2)}, u32[]{:S(2)}) collective-permute-start(bf16[1,2,128,256]{3,2,1,0:T(8,128)(2,1)S(1)} %copy-done.19), channel_id=1, source_target_pairs={{0,10},{2,8},{4,14},{6,12},{8,2},{10,0},{12,6},{14,4},{16,26},{18,... | collective-permute-start | bytes 393224 | tf_op jit(solution)/shard_map/ppermute | solution.py:342
  789.8 64.1 %collective-permute-start.42 = (bf16[1,2,128,256]{3,2,1,0:T(8,128)(2,1)S(1)}, bf16[1,2,128,256]{3,2,1,0:T(8,128)(2,1)}, u32[]{:S(2)}, u32[]{:S(2)}) collective-permute-start(bf16[1,2,128,256]{3,2,1,0:T(8,128)(2,1)S(1)} %copy-done.17), channel_id=1, source_target_pairs={{0,12},{2,14},{4,8},{6,10},{8,4},{10,6},{12,0},{14,2},{16,28},{18,... | collective-permute-start | bytes 393224 | tf_op jit(solution)/shard_map/ppermute | solution.py:342
  802.6 57.0 %collective-permute-start.43 = (bf16[1,2,128,256]{3,2,1,0:T(8,128)(2,1)S(1)}, bf16[1,2,128,256]{3,2,1,0:T(8,128)(2,1)}, u32[]{:S(2)}, u32[]{:S(2)}) collective-permute-start(bf16[1,2,128,256]{3,2,1,0:T(8,128)(2,1)S(1)} %copy-done.16), channel_id=1, source_target_pairs={{0,14},{2,12},{4,10},{6,8},{8,6},{10,4},{12,2},{14,0},{16,30},{18,... | collective-permute-start | bytes 393224 | tf_op jit(solution)/shard_map/ppermute | solution.py:342
  806.0 78.1 %collective-permute-start.44 = (bf16[1,2,128,256]{3,2,1,0:T(8,128)(2,1)S(1)}, bf16[1,2,128,256]{3,2,1,0:T(8,128)(2,1)}, u32[]{:S(2)}, u32[]{:S(2)}) collective-permute-start(bf16[1,2,128,256]{3,2,1,0:T(8,128)(2,1)S(1)} %copy-done.14), channel_id=1, source_target_pairs={{0,16},{2,18},{4,20},{6,22},{8,24},{10,26},{12,28},{14,30},{16,0},... | collective-permute-start | bytes 393224 | tf_op jit(solution)/shard_map/ppermute | solution.py:342
  845.0 43.4 %collective-permute-start.45 = (bf16[1,2,128,256]{3,2,1,0:T(8,128)(2,1)S(1)}, bf16[1,2,128,256]{3,2,1,0:T(8,128)(2,1)}, u32[]{:S(2)}, u32[]{:S(2)}) collective-permute-start(bf16[1,2,128,256]{3,2,1,0:T(8,128)(2,1)S(1)} %copy-done.12), channel_id=1, source_target_pairs={{0,18},{2,16},{4,22},{6,20},{8,26},{10,24},{12,30},{14,28},{16,2},... | collective-permute-start | bytes 393224 | tf_op jit(solution)/shard_map/ppermute | solution.py:342
  850.3 43.1 %collective-permute-start.46 = (bf16[1,2,128,256]{3,2,1,0:T(8,128)(2,1)S(1)}, bf16[1,2,128,256]{3,2,1,0:T(8,128)(2,1)}, u32[]{:S(2)}, u32[]{:S(2)}) collective-permute-start(bf16[1,2,128,256]{3,2,1,0:T(8,128)(2,1)S(1)} %copy-done.10), channel_id=1, source_target_pairs={{0,20},{2,22},{4,16},{6,18},{8,28},{10,30},{12,24},{14,26},{16,4},... | collective-permute-start | bytes 393224 | tf_op jit(solution)/shard_map/ppermute | solution.py:342
  853.8 54.6 %collective-permute-start.47 = (bf16[1,2,128,256]{3,2,1,0:T(8,128)(2,1)}, bf16[1,2,128,256]{3,2,1,0:T(8,128)(2,1)}, u32[]{:S(2)}, u32[]{:S(2)}) collective-permute-start(bf16[1,2,128,256]{3,2,1,0:T(8,128)(2,1)} %get-tuple-element.124), channel_id=1, source_target_pairs={{0,22},{2,20},{4,18},{6,16},{8,30},{10,28},{12,26},{14,24},{16,6},... | collective-permute-start | bytes 393224 | tf_op jit(solution)/shard_map/ppermute | solution.py:342
  859.6 49.0 %collective-permute-start.48 = (bf16[1,2,128,256]{3,2,1,0:T(8,128)(2,1)}, bf16[1,2,128,256]{3,2,1,0:T(8,128)(2,1)}, u32[]{:S(2)}, u32[]{:S(2)}) collective-permute-start(bf16[1,2,128,256]{3,2,1,0:T(8,128)(2,1)} %get-tuple-element.125), channel_id=1, source_target_pairs={{0,24},{2,26},{4,28},{6,30},{8,16},{10,18},{12,20},{14,22},{16,8},... | collective-permute-start | bytes 393224 | tf_op jit(solution)/shard_map/ppermute | solution.py:342
  884.1 24.5 %collective-permute-start.49 = (bf16[1,2,128,256]{3,2,1,0:T(8,128)(2,1)}, bf16[1,2,128,256]{3,2,1,0:T(8,128)(2,1)}, u32[]{:S(2)}, u32[]{:S(2)}) collective-permute-start(bf16[1,2,128,256]{3,2,1,0:T(8,128)(2,1)} %get-tuple-element.126), channel_id=1, source_target_pairs={{0,26},{2,24},{4,30},{6,28},{8,18},{10,16},{12,22},{14,20},{16,10}... | collective-permute-start | bytes 393224 | tf_op jit(solution)/shard_map/ppermute | solution.py:342
  888.4 22.3 %collective-permute-start.50 = (bf16[1,2,128,256]{3,2,1,0:T(8,128)(2,1)}, bf16[1,2,128,256]{3,2,1,0:T(8,128)(2,1)}, u32[]{:S(2)}, u32[]{:S(2)}) collective-permute-start(bf16[1,2,128,256]{3,2,1,0:T(8,128)(2,1)} %get-tuple-element.127), channel_id=1, source_target_pairs={{0,28},{2,30},{4,24},{6,26},{8,20},{10,22},{12,16},{14,18},{16,12}... | collective-permute-start | bytes 393224 | tf_op jit(solution)/shard_map/ppermute | solution.py:342
  893.4 17.2 %collective-permute-start.51 = (bf16[1,2,128,256]{3,2,1,0:T(8,128)(2,1)}, bf16[1,2,128,256]{3,2,1,0:T(8,128)(2,1)}, u32[]{:S(2)}, u32[]{:S(2)}) collective-permute-start(bf16[1,2,128,256]{3,2,1,0:T(8,128)(2,1)} %get-tuple-element.128), channel_id=1, source_target_pairs={{0,30},{2,28},{4,26},{6,24},{8,22},{10,20},{12,18},{14,16},{16,14}... | collective-permute-start | bytes 393224 | tf_op jit(solution)/shard_map/ppermute | solution.py:342
  908.4 24.6 %collective-permute-start.20 = (bf16[1,2,128,256]{3,2,1,0:T(8,128)(2,1)}, bf16[1,2,128,256]{3,2,1,0:T(8,128)(2,1)}, u32[]{:S(2)}, u32[]{:S(2)}) collective-permute-start(bf16[1,2,128,256]{3,2,1,0:T(8,128)(2,1)} %get-tuple-element.94), channel_id=1, source_target_pairs={{0,2},{2,0},{4,6},{6,4},{8,10},{10,8},{12,14},{14,12},{16,18},{18,... | collective-permute-start | bytes 393224 | tf_op jit(solution)/shard_map/ppermute | solution.py:342
  908.5 24.6 %collective-permute-start.21 = (bf16[1,2,128,256]{3,2,1,0:T(8,128)(2,1)}, bf16[1,2,128,256]{3,2,1,0:T(8,128)(2,1)}, u32[]{:S(2)}, u32[]{:S(2)}) collective-permute-start(bf16[1,2,128,256]{3,2,1,0:T(8,128)(2,1)} %get-tuple-element.95), channel_id=1, source_target_pairs={{0,4},{2,6},{4,0},{6,2},{8,12},{10,14},{12,8},{14,10},{16,20},{18,... | collective-permute-start | bytes 393224 | tf_op jit(solution)/shard_map/ppermute | solution.py:342
  908.6 27.3 %collective-permute-start.22 = (bf16[1,2,128,256]{3,2,1,0:T(8,128)(2,1)}, bf16[1,2,128,256]{3,2,1,0:T(8,128)(2,1)}, u32[]{:S(2)}, u32[]{:S(2)}) collective-permute-start(bf16[1,2,128,256]{3,2,1,0:T(8,128)(2,1)} %get-tuple-element.96), channel_id=1, source_target_pairs={{0,6},{2,4},{4,2},{6,0},{8,14},{10,12},{12,10},{14,8},{16,22},{18,... | collective-permute-start | bytes 393224 | tf_op jit(solution)/shard_map/ppermute | solution.py:342
  910.7 25.9 %collective-permute-start.23 = (bf16[1,2,128,256]{3,2,1,0:T(8,128)(2,1)}, bf16[1,2,128,256]{3,2,1,0:T(8,128)(2,1)}, u32[]{:S(2)}, u32[]{:S(2)}) collective-permute-start(bf16[1,2,128,256]{3,2,1,0:T(8,128)(2,1)} %get-tuple-element.97), channel_id=1, source_target_pairs={{0,8},{2,10},{4,12},{6,14},{8,0},{10,2},{12,4},{14,6},{16,24},{18,... | collective-permute-start | bytes 393224 | tf_op jit(solution)/shard_map/ppermute | solution.py:342
  910.7 27.6 %collective-permute-start.24 = (bf16[1,2,128,256]{3,2,1,0:T(8,128)(2,1)}, bf16[1,2,128,256]{3,2,1,0:T(8,128)(2,1)}, u32[]{:S(2)}, u32[]{:S(2)}) collective-permute-start(bf16[1,2,128,256]{3,2,1,0:T(8,128)(2,1)} %get-tuple-element.98), channel_id=1, source_target_pairs={{0,10},{2,8},{4,14},{6,12},{8,2},{10,0},{12,6},{14,4},{16,26},{18,... | collective-permute-start | bytes 393224 | tf_op jit(solution)/shard_map/ppermute | solution.py:342
  933.1 15.8 %collective-permute-start.26 = (bf16[1,2,128,256]{3,2,1,0:T(8,128)(2,1)}, bf16[1,2,128,256]{3,2,1,0:T(8,128)(2,1)}, u32[]{:S(2)}, u32[]{:S(2)}) collective-permute-start(bf16[1,2,128,256]{3,2,1,0:T(8,128)(2,1)} %get-tuple-element.100), channel_id=1, source_target_pairs={{0,14},{2,12},{4,10},{6,8},{8,6},{10,4},{12,2},{14,0},{16,30},{18,... | collective-permute-start | bytes 393224 | tf_op jit(solution)/shard_map/ppermute | solution.py:342
  935.9 14.1 %collective-permute-start.27 = (bf16[1,2,128,256]{3,2,1,0:T(8,128)(2,1)}, bf16[1,2,128,256]{3,2,1,0:T(8,128)(2,1)}, u32[]{:S(2)}, u32[]{:S(2)}) collective-permute-start(bf16[1,2,128,256]{3,2,1,0:T(8,128)(2,1)} %get-tuple-element.101), channel_id=1, source_target_pairs={{0,16},{2,18},{4,20},{6,22},{8,24},{10,26},{12,28},{14,30},{16,0},... | collective-permute-start | bytes 393224 | tf_op jit(solution)/shard_map/ppermute | solution.py:342
  936.5 26.1 %collective-permute-start.28 = (bf16[1,2,128,256]{3,2,1,0:T(8,128)(2,1)}, bf16[1,2,128,256]{3,2,1,0:T(8,128)(2,1)}, u32[]{:S(2)}, u32[]{:S(2)}) collective-permute-start(bf16[1,2,128,256]{3,2,1,0:T(8,128)(2,1)} %get-tuple-element.102), channel_id=1, source_target_pairs={{0,18},{2,16},{4,22},{6,20},{8,26},{10,24},{12,30},{14,28},{16,2},... | collective-permute-start | bytes 393224 | tf_op jit(solution)/shard_map/ppermute | solution.py:342
  938.3 25.5 %collective-permute-start.29 = (bf16[1,2,128,256]{3,2,1,0:T(8,128)(2,1)}, bf16[1,2,128,256]{3,2,1,0:T(8,128)(2,1)}, u32[]{:S(2)}, u32[]{:S(2)}) collective-permute-start(bf16[1,2,128,256]{3,2,1,0:T(8,128)(2,1)} %get-tuple-element.103), channel_id=1, source_target_pairs={{0,20},{2,22},{4,16},{6,18},{8,28},{10,30},{12,24},{14,26},{16,4},... | collective-permute-start | bytes 393224 | tf_op jit(solution)/shard_map/ppermute | solution.py:342
  946.8 32.0 %collective-permute-start.30 = (bf16[1,2,128,256]{3,2,1,0:T(8,128)(2,1)}, bf16[1,2,128,256]{3,2,1,0:T(8,128)(2,1)}, u32[]{:S(2)}, u32[]{:S(2)}) collective-permute-start(bf16[1,2,128,256]{3,2,1,0:T(8,128)(2,1)} %get-tuple-element.104), channel_id=1, source_target_pairs={{0,22},{2,20},{4,18},{6,16},{8,30},{10,28},{12,26},{14,24},{16,6},... | collective-permute-start | bytes 393224 | tf_op jit(solution)/shard_map/ppermute | solution.py:342
  948.9 29.8 %collective-permute-start.31 = (bf16[1,2,128,256]{3,2,1,0:T(8,128)(2,1)}, bf16[1,2,128,256]{3,2,1,0:T(8,128)(2,1)}, u32[]{:S(2)}, u32[]{:S(2)}) collective-permute-start(bf16[1,2,128,256]{3,2,1,0:T(8,128)(2,1)} %get-tuple-element.105), channel_id=1, source_target_pairs={{0,24},{2,26},{4,28},{6,30},{8,16},{10,18},{12,20},{14,22},{16,8},... | collective-permute-start | bytes 393224 | tf_op jit(solution)/shard_map/ppermute | solution.py:342
  950.0 28.8 %collective-permute-start.32 = (bf16[1,2,128,256]{3,2,1,0:T(8,128)(2,1)}, bf16[1,2,128,256]{3,2,1,0:T(8,128)(2,1)}, u32[]{:S(2)}, u32[]{:S(2)}) collective-permute-start(bf16[1,2,128,256]{3,2,1,0:T(8,128)(2,1)} %get-tuple-element.106), channel_id=1, source_target_pairs={{0,26},{2,24},{4,30},{6,28},{8,18},{10,16},{12,22},{14,20},{16,10}... | collective-permute-start | bytes 393224 | tf_op jit(solution)/shard_map/ppermute | solution.py:342
  962.7 16.1 %collective-permute-start.33 = (bf16[1,2,128,256]{3,2,1,0:T(8,128)(2,1)}, bf16[1,2,128,256]{3,2,1,0:T(8,128)(2,1)}, u32[]{:S(2)}, u32[]{:S(2)}) collective-permute-start(bf16[1,2,128,256]{3,2,1,0:T(8,128)(2,1)} %get-tuple-element.107), channel_id=1, source_target_pairs={{0,28},{2,30},{4,24},{6,26},{8,20},{10,22},{12,16},{14,18},{16,12}... | collective-permute-start | bytes 393224 | tf_op jit(solution)/shard_map/ppermute | solution.py:342
  963.9 14.9 %collective-permute-start.34 = (bf16[1,2,128,256]{3,2,1,0:T(8,128)(2,1)}, bf16[1,2,128,256]{3,2,1,0:T(8,128)(2,1)}, u32[]{:S(2)}, u32[]{:S(2)}) collective-permute-start(bf16[1,2,128,256]{3,2,1,0:T(8,128)(2,1)} %get-tuple-element.108), channel_id=1, source_target_pairs={{0,30},{2,28},{4,26},{6,24},{8,22},{10,20},{12,18},{14,16},{16,14}... | collective-permute-start | bytes 393224 | tf_op jit(solution)/shard_map/ppermute | solution.py:342
  (38 other events, 4803.2 us)
where the time goes:
time: 993 us; the launch traced here: 986 us
  waiting for transfers between devices  573 us (58%)
  Pallas kernels  233 us (23%)
  starting transfers between devices  176 us (18%)
    ppermute x52, waiting for transfers between devices, send(): return lax.ppermute(array, axis, [(n, n ^ mask) for n in range(size)])  475 us
    pallas_call x9, Pallas kernels, call(): return made if after is None else lambda *args: made(*args, after)  139 us
    all_to_all x4, waiting for transfers between devices, trade(): return [lax.all_to_all(made, 'tile', 0, 0, tiled=True)]  98.2 us
    ppermute x52, starting transfers between devices, send(): return lax.ppermute(array, axis, [(n, n ^ mask) for n in range(size)])  97.9 us
    all_to_all x4, starting transfers between devices, trade(): return [lax.all_to_all(made, 'tile', 0, 0, tiled=True)]  77.7 us
    pallas_call x2, Pallas kernels, contract(): call(functools.partial(contract_kernel, (tiles, shares, col_local, both /...  32.4 us
    pallas_call x2, Pallas kernels, window(): call(functools.partial(window_kernel, (shares, took, gave, rows, 16, both...  32 us
    pallas_call x3, Pallas kernels, spread(): call(functools.partial(spread_kernel, (len(got), carried, step, both // 2...  24.4 us
  transfers between devices with their start and end apart: 56, of which 20 were waited for; matrix products, arithmetic and copies ran while one was open for 0% of the time, Pallas kernels for 20%

commit v1 on v0

--- a/solution.py
+++ b/solution.py
@@ -336,6 +336,59 @@
     )(pos, col_factors, *got, *([before] if carried else []))
 
 
+def finish_kernel(dims, pos, *refs):
+    groups, step, width, adds = dims
+    held, got = refs[:groups], refs[groups : groups * (1 + GROUP)]
+    out, stage = refs[-2:]
+    with_real = with_imag = 0.0
+    for n, v_ref in enumerate(held):
+        for seat in range(GROUP):
+            row = ((pos[0] % GROUP) ^ seat) * step
+            stage[n, pl.ds(pl.multiple_of(row, step), step)] = got[n * GROUP + seat][0, 0]
+        with_real = with_real + dot(v_ref[0, 0], stage[n])
+        with_imag = with_imag + dot(v_ref[0, 1], stage[n])
+    real = with_real[:, :width] - with_imag[:, width:]
+    imag = with_real[:, width:] + with_imag[:, :width]
+    if adds:
+        part = refs[groups * (1 + GROUP)]
+        real, imag = part[0, 0] + real, part[0, 1] + imag
+    out[0, 0] = real
+    out[0, 1] = imag
+
+
+def finish(pos, col_factors, piece, got, highs, chunk, points, part, before, after):
+    first, freqs = piece
+    total, _, src_rows, _ = col_factors.shape
+    step, both = got[0].shape[-2:]
+    width, groups = both // 2, len(highs)
+    own = pl.BlockSpec((1, 2, TS, width), lambda f, c, s: (f, 0, c, 0))
+    last = before is not None
+    adds = part is not None
+    shape = (total, 2, src_rows, points) if last else (freqs, 2, src_rows, width)
+
+    def held(high):
+        return pl.BlockSpec(
+            (1, 2, TS, GROUP * step), lambda f, c, s: (first + f, 0, c, (s[0] // GROUP) ^ high)
+        )
+
+    return call(
+        functools.partial(finish_kernel, (groups, step, width, adds)),
+        (freqs, src_rows // TS),
+        1,
+        [held(high) for high in highs]
+        + [pl.BlockSpec((1, 1, step, both), lambda f, c, s: (f, c, 0, 0))] * len(got)
+        + [own] * adds
+        + [pl.BlockSpec(memory_space=pl.ANY)] * last,
+        pl.BlockSpec((1, 2, TS, width), lambda f, c, s: (first + f, 0, c, chunk)) if last else own,
+        jax.ShapeDtypeStruct(shape, jnp.float32),
+        [pltpu.VMEM((groups, GROUP * step, both), got[0].dtype)],
+        4 * freqs * src_rows * len(got) * step * both,
+        freqs * 4 * (src_rows * (len(got) * step + both) + len(got) * step * both),
+        after,
+        input_output_aliases={1 + groups + len(got) + adds: 0} if last else {},
+    )(pos, *[col_factors] * groups, *got, *([part] if adds else []), *([before] if last else []))
+
+
 def send(array, axis, size, mask):
     if mask == 0:
         return array
@@ -366,7 +419,8 @@
 
     took = gave = [((0, freqs, False),)] * CHUNKS
     if freqs > 2:
-        took = [((0, 1, True), (1, freqs - 1, False))] + took[1:]
+        took = [((0, freqs - 1, False), (freqs - 1, 1, True))] * CHUNKS
+        took = [((0, 1, True), (1, freqs - 2, False), (freqs - 1, 1, True))] + took[1:]
         gave = gave[:-1] + [((0, 1, True), (1, freqs - 2, False), (freqs - 1, 1, True))]
 
     def runs(pieces):
@@ -376,17 +430,16 @@
     token = None
     for h in range(CHUNKS):
         sent.append([])
-        for *piece, split in took[h]:
+        for n, (*piece, split) in enumerate(took[h]):
             groups = tiles // GROUP
-            half = groups // 2 if split else groups
+            some = 1 if split and h == n == 0 else groups
             made = []
-            for base in reversed(range(0, groups, half)):
+            for base in reversed(range(0, groups, some)):
                 part = project(
-                    pos, col_factors, wavefield, piece, h, width, tiles, split, base, half, token
+                    pos, col_factors, wavefield, piece, h, width, tiles, split, base, some, token
                 )
                 token = part[0] if split else part
-                made = [part] + made
-            made = [*made[0], *made[1]] if split else made[0]
+                made = [*part, *made] if split else part
             sent[h].append(trade(made, tiles, split))
     back = []
     for h in range(CHUNKS):
@@ -396,7 +449,9 @@
             token = made[0]
             parts.append([send(part, "freq", shares, m) for m, part in enumerate(made)])
         parts = window(cosine, sine, index, parts, runs(took[h]), runs(gave[h]), h)
-        parts = [[send(part, "freq", shares, m) for m, part in enumerate(group)] for group in parts]
+        parts = [
+            [send(part, "freq", shares, m) for m, part in enumerate(group)] for group in parts
+        ]
         back.append([])
         token = None
         for n, (*piece, split) in enumerate(gave[h]):
@@ -408,6 +463,19 @@
     result = None
     for h in range(CHUNKS):
         for n, (*piece, split) in enumerate(gave[h]):
+            if n == 2:
+                slow = tiles // GROUP // 2
+                most = tuple(high for high in range(tiles // GROUP) if high != slow)
+                part = None
+                for highs in (most, (slow,)):
+                    group = [back[h][n][high * GROUP + seat] for high in highs for seat in range(GROUP)]
+                    ends = part is not None
+                    part = finish(
+                        pos, col_factors, piece, group, highs, h, points, part,
+                        result if ends else None, None if ends else result,
+                    )
+                result = part
+                continue
             result = spread(pos, col_factors, piece, back[h][n], h, points, result, token)
             token = None
     return result

time: 993 us -> 1060 us (1.067)
  starting transfers between devices: 176 us -> 240 us
  Pallas kernels: 233 us -> 252 us
    ppermute x52 -> x84, starting transfers between devices: 97.9 us -> 188 us  [send(): return lax.ppermute(array, axis, [(n, n ^ mask) for n in range(size)])]
    all_to_all x4, waiting for transfers between devices: 98.2 us -> 50 us  [trade(): return [lax.all_to_all(made, 'tile', 0, 0, tiled=True)]]
    ppermute x52 -> x84, waiting for transfers between devices: 475 us -> 516 us  [send(): return lax.ppermute(array, axis, [(n, n ^ mask) for n in range(size)])]
    all_to_all x4, starting transfers between devices: 77.7 us -> 51.2 us  [trade(): return [lax.all_to_all(made, 'tile', 0, 0, tiled=True)]]
    pallas_call x9 -> x16, Pallas kernels: 139 us -> 162 us  [call(): return made if after is None else lambda *args: made(*args, after)]
    pallas_call x3 -> x2, Pallas kernels: 24.4 us -> 17.7 us  [spread(): call(functools.partial(spread_kernel, (len(got), carried, step, both // 2...]
  transfers between devices with their start and end apart: 56 -> 88, of which waited for: 20 -> 35; matrix products, arithmetic and copies ran while one was open for 0% -> 0% of each run, Pallas kernels for 20% -> 21%
where the time goes in v1:
time: 1060 us
  waiting for transfers between devices  566 us (53%)
  Pallas kernels  252 us (24%)
  starting transfers between devices  240 us (23%)
    ppermute x84, waiting for transfers between devices, send(): return lax.ppermute(array, axis, [(n, n ^ mask) for n in range(size)])  516 us
    ppermute x84, starting transfers between devices, send(): return lax.ppermute(array, axis, [(n, n ^ mask) for n in range(size)])  188 us
    pallas_call x16, Pallas kernels, call(): return made if after is None else lambda *args: made(*args, after)  162 us
    all_to_all x4, starting transfers between devices, trade(): return [lax.all_to_all(made, 'tile', 0, 0, tiled=True)]  51.2 us
    all_to_all x4, waiting for transfers between devices, trade(): return [lax.all_to_all(made, 'tile', 0, 0, tiled=True)]  50 us
    pallas_call x2, Pallas kernels, contract(): call(functools.partial(contract_kernel, (tiles, shares, col_local, both /...  32.5 us
    pallas_call x2, Pallas kernels, window(): call(functools.partial(window_kernel, (shares, took, gave, rows, 16, both...  31.9 us
  transfers between devices with their start and end apart: 88, of which 35 were waited for; matrix products, arithmetic and copies ran while one was open for 0% of the time, Pallas kernels for 21%

profile of v1, /device:TPU:1, one launch (start us, length us, event | category | flops | bytes accessed | tf_op | source)
XLA Modules:
  0.0 1059.3 jit_solution(3057858730244019523)
XLA Ops:
  16.8 13.3 %shard_map.50.refs_3_ = bf16[16,2,4,64,256]{4,3,2,1,0:T(8,128)(2,1)} custom-call(s32[2]{0:T(128)} %pad_add_fusion.pos.refs_0_, bf16[4,2,1024,2048]{3,2,1,0:T(8,128)(2,1)} %refs_0_.1, bf16[4,2,1024,256]{3,2,1,0:T(8,128)(2,1)} %refs_2_.14, bf16[1,4,64,256]{3,2,1,0:T(8,128)(2,1)} %get-tuple-element.106.refs_3_.refs_2_), custom_call_target="tpu_custom_call" | custom-call | flops 4294967296 | bytes 18874368 | tf_op jit(solution)/shard_map/pallas_call | solution.py:48
  30.1 7.3 all-to-all-start.1
  37.4 9.2 shard_map.51
  46.6 18.9 %shard_map.52.refs_3_ = bf16[16,3,4,64,256]{4,3,2,1,0:T(8,128)(2,1)} custom-call(s32[2]{0:T(128)} %pad_add_fusion.pos.refs_0_, bf16[4,2,1024,2048]{3,2,1,0:T(8,128)(2,1)} %refs_0_.1, bf16[4,2,1024,256]{3,2,1,0:T(8,128)(2,1)} %refs_2_.14, bf16[1,4,64,256]{3,2,1,0:T(8,128)(2,1)} %get-tuple-element.107.refs_3_.refs_2_), custom_call_target="tpu_custom_call" | custom-call | flops 6442450944 | bytes 28311552 | tf_op jit(solution)/shard_map/pallas_call | solution.py:48
  65.6 50.0 %all-to-all-done.1.refs_2_ = bf16[16,2,4,64,256]{4,3,2,1,0:T(8,128)(2,1)} async-done(((bf16[16,2,4,64,256]{4,3,2,1,0:T(8,128)(2,1)}), bf16[16,2,4,64,256]{4,3,2,1,0:T(8,128)(2,1)}, u32[]{:S(2)}, u32[]{:S(2)}) %all-to-all-start.1) | async-done | bytes 4194336 | tf_op jit(solution)/shard_map/all_to_all | solution.py:400
  115.6 19.1 %all-to-all-start = ((bf16[16,3,4,64,256]{4,3,2,1,0:T(8,128)(2,1)}), bf16[16,3,4,64,256]{4,3,2,1,0:T(8,128)(2,1)}, u32[]{:S(2)}, u32[]{:S(2)}) async-start(bf16[16,3,4,64,256]{4,3,2,1,0:T(8,128)(2,1)} %shard_map.52.refs_3_), calls=%async_computation | async-start | bytes 12582912 | tf_op jit(solution)/shard_map/all_to_all | solution.py:400
  142.8 101.4 %collective-permute-done.12.refs_15_ = bf16[1,4,64,256]{3,2,1,0:T(8,128)(2,1)} collective-permute-done((bf16[1,4,64,256]{3,2,1,0:T(8,128)(2,1)S(1)}, bf16[1,4,64,256]{3,2,1,0:T(8,128)(2,1)}, u32[]{:S(2)}, u32[]{:S(2)}) %collective-permute-start.12) | collective-permute-done | bytes 131104 | tf_op jit(solution)/shard_map/ppermute | solution.py:395
  244.1 47.5 %collective-permute-start.9 = (bf16[1,4,64,256]{3,2,1,0:T(8,128)(2,1)S(1)}, bf16[1,4,64,256]{3,2,1,0:T(8,128)(2,1)}, u32[]{:S(2)}, u32[]{:S(2)}) collective-permute-start(bf16[1,4,64,256]{3,2,1,0:T(8,128)(2,1)S(1)} %copy-done.6), channel_id=1, source_target_pairs={{0,20},{2,22},{4,16},{6,18},{8,28},{10,30},{12,24},{14,26},{16,4},... | collective-permute-start | bytes 393224 | tf_op jit(solution)/shard_map/ppermute | solution.py:395
  295.1 7.8 collective-permute-start.7
  305.5 4.8 collective-permute-done.8.refs_11_
  322.7 9.1 shard_map.53
  335.7 7.4 shard_map.54
  345.8 12.7 %shard_map.55 = (bf16[2,4,256,256]{3,2,1,0:T(8,128)(2,1)}, bf16[2,4,256,256]{3,2,1,0:T(8,128)(2,1)}) custom-call(s32[2]{0:T(128)} %pad_add_fusion.pos.refs_0_, bf16[4,2,2048,1024]{3,2,1,0:T(8,128)(2,1)} %refs_1_.29, bf16[16,2,4,64,256]{4,3,2,1,0:T(8,128)(2,1)} %all-to-all-done.1.refs_2_, bf16[1,4,256,256]{3,2,1,0:T(8,128)(2,1)} %get-tuple-element.121.refs_3_.refs_0_), custom_call_target="tpu_custom_call" | custom-call | flops 4294967296 | bytes 23068672 | tf_op jit(solution)/shard_map/pallas_call | solution.py:48
  366.0 11.5 %collective-permute-done.24.refs_10_ = bf16[1,4,64,256]{3,2,1,0:T(8,128)(2,1)} collective-permute-done((bf16[1,4,64,256]{3,2,1,0:T(8,128)(2,1)}, bf16[1,4,64,256]{3,2,1,0:T(8,128)(2,1)}, u32[]{:S(2)}, u32[]{:S(2)}) %collective-permute-start.24) | collective-permute-done | bytes 131104 | tf_op jit(solution)/shard_map/ppermute | solution.py:395
  381.8 8.0 collective-permute-done.26.refs_12_
  401.1 7.4 shard_map.56
  409.7 12.3 %collective-permute-done.32.refs_5_ = bf16[1,4,256,256]{3,2,1,0:T(8,128)(2,1)} collective-permute-done((bf16[1,4,256,256]{3,2,1,0:T(8,128)(2,1)}, bf16[1,4,256,256]{3,2,1,0:T(8,128)(2,1)}, u32[]{:S(2)}, u32[]{:S(2)}) %collective-permute-start.32) | collective-permute-done | bytes 524320 | tf_op jit(solution)/shard_map/ppermute | solution.py:395
  422.0 16.0 %shard_map.57 = (bf16[4,4,256,256]{3,2,1,0:T(8,128)(2,1)}, bf16[4,4,256,256]{3,2,1,0:T(8,128)(2,1)}) custom-call(f32[16,8]{1,0:T(8,128)} %get-tuple-element.202.cosine, f32[16,8]{1,0:T(8,128)} %get-tuple-element.201.sine, s32[1,256]{1,0:T(1,128)} %bitcast.3, bf16[1,4,256,256]{3,2,1,0:T(8,128)(2,1)} %get-tuple-element.121.refs_3_.refs_0_, ...), custom_call_target="tpu_custom_call" | custom-call | flops 67108864 | bytes 8388608 | tf_op jit(solution)/shard_map/pallas_call | solution.py:234
  438.2 46.0 %collective-permute-done.33.refs_1_ = bf16[4,4,256,256]{3,2,1,0:T(8,128)(2,1)} collective-permute-done((bf16[4,4,256,256]{3,2,1,0:T(8,128)(2,1)}, bf16[4,4,256,256]{3,2,1,0:T(8,128)(2,1)}, u32[]{:S(2)}, u32[]{:S(2)}) %collective-permute-start.33) | collective-permute-done | bytes 2097184 | tf_op jit(solution)/shard_map/ppermute | solution.py:395
  484.2 24.5 %shard_map.58.refs_3_ = bf16[16,4,2,128,256]{4,3,2,1,0:T(8,128)(2,1)} custom-call(s32[2]{0:T(128)} %pad_add_fusion.pos.refs_0_, bf16[4,2,2048,1024]{3,2,1,0:T(8,128)(2,1)} %refs_1_.29, bf16[4,4,256,256]{3,2,1,0:T(8,128)(2,1)} %get-tuple-element.142.refs_0_, bf16[4,4,256,256]{3,2,1,0:T(8,128)(2,1)} %collective-permute-done.33.refs_1_), custom_call_target="tpu_custom_call" | custom-call | flops 8589934592 | bytes 46137344 | tf_op jit(solution)/shard_map/pallas_call | solution.py:291
  508.7 12.3 %all-to-all-start.2 = ((bf16[16,4,2,128,256]{4,3,2,1,0:T(8,128)(2,1)}), bf16[16,4,2,128,256]{4,3,2,1,0:T(8,128)(2,1)}, u32[]{:S(2)}, u32[]{:S(2)}) async-start(bf16[16,4,2,128,256]{4,3,2,1,0:T(8,128)(2,1)} %shard_map.58.refs_3_), calls=%async_computation.2 | async-start | bytes 16777216 | tf_op jit(solution)/shard_map/all_to_all | solution.py:400
  521.0 18.1 %shard_map.59 = (bf16[3,4,256,256]{3,2,1,0:T(8,128)(2,1)}, bf16[3,4,256,256]{3,2,1,0:T(8,128)(2,1)}) custom-call(s32[2]{0:T(128)} %pad_add_fusion.pos.refs_0_, bf16[4,2,2048,1024]{3,2,1,0:T(8,128)(2,1)} %refs_1_.29, bf16[16,3,4,64,256]{4,3,2,1,0:T(8,128)(2,1)} %all-to-all-done.refs_2_, bf16[16,4,2,128,256]{4,3,2,1,0:T(8,128)(2,1)} %shard_map.58.refs_3_), custom_call_target="tpu_custom_call" | custom-call | flops 6442450944 | bytes 34603008 | tf_op jit(solution)/shard_map/pallas_call | solution.py:48
  544.5 27.6 %collective-permute-done.36.refs_4_ = bf16[1,4,64,256]{3,2,1,0:T(8,128)(2,1)} collective-permute-done((bf16[1,4,64,256]{3,2,1,0:T(8,128)(2,1)}, bf16[1,4,64,256]{3,2,1,0:T(8,128)(2,1)}, u32[]{:S(2)}, u32[]{:S(2)}) %collective-permute-start.36) | collective-permute-done | bytes 131104 | tf_op jit(solution)/shard_map/ppermute | solution.py:395
  576.2 83.3 %collective-permute-done.38.refs_6_ = bf16[1,4,64,256]{3,2,1,0:T(8,128)(2,1)} collective-permute-done((bf16[1,4,64,256]{3,2,1,0:T(8,128)(2,1)}, bf16[1,4,64,256]{3,2,1,0:T(8,128)(2,1)}, u32[]{:S(2)}, u32[]{:S(2)}) %collective-permute-start.38) | collective-permute-done | bytes 131104 | tf_op jit(solution)/shard_map/ppermute | solution.py:395
  673.8 44.2 %collective-permute-done.42.refs_10_ = bf16[1,4,64,256]{3,2,1,0:T(8,128)(2,1)} collective-permute-done((bf16[1,4,64,256]{3,2,1,0:T(8,128)(2,1)}, bf16[1,4,64,256]{3,2,1,0:T(8,128)(2,1)}, u32[]{:S(2)}, u32[]{:S(2)}) %collective-permute-start.42) | collective-permute-done | bytes 131104 | tf_op jit(solution)/shard_map/ppermute | solution.py:395
  723.4 6.9 collective-permute-done.44.refs_12_
  737.3 5.5 collective-permute-done.49.refs_17_
  742.8 7.4 shard_map.60
  750.4 13.1 %collective-permute-done.50.refs_3_ = bf16[1,4,256,256]{3,2,1,0:T(8,128)(2,1)} collective-permute-done((bf16[1,4,256,256]{3,2,1,0:T(8,128)(2,1)}, bf16[1,4,256,256]{3,2,1,0:T(8,128)(2,1)}, u32[]{:S(2)}, u32[]{:S(2)}) %collective-permute-start.50) | collective-permute-done | bytes 524320 | tf_op jit(solution)/shard_map/ppermute | solution.py:395
  763.5 16.0 %shard_map.61 = (bf16[1,4,256,256]{3,2,1,0:T(8,128)(2,1)}, bf16[1,4,256,256]{3,2,1,0:T(8,128)(2,1)}, bf16[2,4,256,256]{3,2,1,0:T(8,128)(2,1)}, bf16[2,4,256,256]...) custom-call(f32[16,8]{1,0:T(8,128)} %get-tuple-element.202.cosine, ...), custom_call_target="tpu_custom_call" | custom-call | flops 67108864 | bytes 8388608 | tf_op jit(solution)/shard_map/pallas_call | solution.py:234
  781.0 33.5 %collective-permute-done.68.refs_1_ = bf16[1,4,256,256]{3,2,1,0:T(8,128)(2,1)} collective-permute-done((bf16[1,4,256,256]{3,2,1,0:T(8,128)(2,1)}, bf16[1,4,256,256]{3,2,1,0:T(8,128)(2,1)}, u32[]{:S(2)}, u32[]{:S(2)}) %collective-permute-start.68) | collective-permute-done | bytes 524320 | tf_op jit(solution)/shard_map/ppermute | solution.py:395
  814.5 7.9 shard_map.63
  822.5 13.4 %shard_map.64 = bf16[16,2,2,128,256]{4,3,2,1,0:T(8,128)(2,1)} custom-call(s32[2]{0:T(128)} %pad_add_fusion.pos.refs_0_, bf16[4,2,2048,1024]{3,2,1,0:T(8,128)(2,1)} %refs_1_.29, bf16[2,4,256,256]{3,2,1,0:T(8,128)(2,1)} %get-tuple-element.181.refs_2_, bf16[2,4,256,256]{3,2,1,0:T(8,128)(2,1)} %collective-permute-done.67.refs_3_, ...), custom_call_target="tpu_custom_call" | custom-call | flops 4294967296 | bytes 23068672 | tf_op jit(solution)/shard_map/pallas_call | solution.py:48
  835.9 12.4 %all-to-all-start.3 = ((bf16[16,2,2,128,256]{4,3,2,1,0:T(8,128)(2,1)}), bf16[16,2,2,128,256]{4,3,2,1,0:T(8,128)(2,1)}, u32[]{:S(2)}, u32[]{:S(2)}) async-start(bf16[16,2,2,128,256]{4,3,2,1,0:T(8,128)(2,1)} %shard_map.64), calls=%async_computation.3 | async-start | bytes 8388608 | tf_op jit(solution)/shard_map/all_to_all | solution.py:400
  853.4 8.5 collective-permute-done.51.refs_3_
  865.3 11.7 %collective-permute-done.70.refs_2_ = bf16[1,2,128,256]{3,2,1,0:T(8,128)(2,1)} collective-permute-done((bf16[1,2,128,256]{3,2,1,0:T(8,128)(2,1)S(1)}, bf16[1,2,128,256]{3,2,1,0:T(8,128)(2,1)}, u32[]{:S(2)}, u32[]{:S(2)}) %collective-permute-start.70) | collective-permute-done | bytes 131104 | tf_op jit(solution)/shard_map/ppermute | solution.py:395
  881.4 37.9 %collective-permute-done.72.refs_4_ = bf16[1,2,128,256]{3,2,1,0:T(8,128)(2,1)} collective-permute-done((bf16[1,2,128,256]{3,2,1,0:T(8,128)(2,1)S(1)}, bf16[1,2,128,256]{3,2,1,0:T(8,128)(2,1)}, u32[]{:S(2)}, u32[]{:S(2)}) %collective-permute-start.72) | collective-permute-done | bytes 131104 | tf_op jit(solution)/shard_map/ppermute | solution.py:395
  919.3 5.3 collective-permute-start.77
  928.2 5.7 collective-permute-start.79
  933.9 7.9 shard_map.62
  941.9 16.6 %collective-permute-done.76.refs_8_ = bf16[1,2,128,256]{3,2,1,0:T(8,128)(2,1)} collective-permute-done((bf16[1,2,128,256]{3,2,1,0:T(8,128)(2,1)}, bf16[1,2,128,256]{3,2,1,0:T(8,128)(2,1)}, u32[]{:S(2)}, u32[]{:S(2)}) %collective-permute-start.76) | collective-permute-done | bytes 131104 | tf_op jit(solution)/shard_map/ppermute | solution.py:395
  958.5 4.8 collective-permute-start.81
  967.8 7.6 collective-permute-start.83
  975.4 19.3 %shard_map.65.refs_16_ = f32[4,2,1024,256]{3,2,1,0:T(8,128)} custom-call(s32[2]{0:T(128)} %pad_add_fusion.pos.refs_0_, bf16[4,2,1024,2048]{3,2,1,0:T(8,128)(2,1)} %refs_0_.1, bf16[16,4,2,128,256]{4,3,2,1,0:T(8,128)(2,1)} %all-to-all-done.2.refs_4_.refs_2_, bf16[1,2,128,256]{3,2,1,0:T(8,128)(2,1)} %get-tuple-element.169.refs_3_.refs_4_), custom_call_target="tpu_custom_call" | custom-call | flops 8589934592 | bytes 46137344 | tf_op jit(solution)/shard_map/pallas_call | solution.py:48
  998.2 6.7 shard_map.66.refs_1_
  1016.0 11.0 %shard_map.67.refs_16_.refs_6_ = f32[4,2,1024,256]{3,2,1,0:T(8,128)} custom-call(s32[2]{0:T(128)} %pad_add_fusion.pos.refs_0_, bf16[4,2,1024,2048]{3,2,1,0:T(8,128)(2,1)} %refs_0_.1, bf16[16,2,2,128,256]{4,3,2,1,0:T(8,128)(2,1)} %all-to-all-done.3.refs_0_, f32[4,2,1024,256]{3,2,1,0:T(8,128)} %shard_map.66.refs_1_), custom_call_target="tpu_custom_call", output_to_operand_aliasing={{}: (3, {})} | custom-call | flops 4294967296 | bytes 23068672 | tf_op jit(solution)/shard_map/pallas_call | solution.py:322
  1029.3 13.2 %collective-permute-start.55 = (bf16[1,2,128,256]{3,2,1,0:T(8,128)(2,1)}, bf16[1,2,128,256]{3,2,1,0:T(8,128)(2,1)}, u32[]{:S(2)}, u32[]{:S(2)}) collective-permute-start(bf16[1,2,128,256]{3,2,1,0:T(8,128)(2,1)} %get-tuple-element.168), channel_id=1, source_target_pairs={{0,22},{2,20},{4,18},{6,16},{8,30},{10,28},{12,26},{14,24},{16,6},... | collective-permute-start | bytes 393224 | tf_op jit(solution)/shard_map/ppermute | solution.py:395
  1042.5 5.7 shard_map.68.refs_5_
  (191 shorter events, 161.3 us)
Async XLA Ops:
  30.1 85.5 %all-to-all-start.1 = ((bf16[16,2,4,64,256]{4,3,2,1,0:T(8,128)(2,1)}), bf16[16,2,4,64,256]{4,3,2,1,0:T(8,128)(2,1)}, u32[]{:S(2)}, u32[]{:S(2)}) async-start(bf16[16,2,4,64,256]{4,3,2,1,0:T(8,128)(2,1)} %shard_map.50.refs_3_), calls=%async_computation.1 | async-start | bytes 8388608 | tf_op jit(solution)/shard_map/all_to_all | solution.py:400
  115.6 393.1 %all-to-all-start = ((bf16[16,3,4,64,256]{4,3,2,1,0:T(8,128)(2,1)}), bf16[16,3,4,64,256]{4,3,2,1,0:T(8,128)(2,1)}, u32[]{:S(2)}, u32[]{:S(2)}) async-start(bf16[16,3,4,64,256]{4,3,2,1,0:T(8,128)(2,1)} %shard_map.52.refs_3_), calls=%async_computation | async-start | bytes 12582912 | tf_op jit(solution)/shard_map/all_to_all | solution.py:400
  134.7 109.4 %collective-permute-start.12 = (bf16[1,4,64,256]{3,2,1,0:T(8,128)(2,1)S(1)}, bf16[1,4,64,256]{3,2,1,0:T(8,128)(2,1)}, u32[]{:S(2)}, u32[]{:S(2)}) collective-permute-start(bf16[1,4,64,256]{3,2,1,0:T(8,128)(2,1)S(1)} %copy-done.14), channel_id=1, source_target_pairs={{0,26},{2,24},{4,30},{6,28},{8,18},{10,16},{12,22},{14,20},{16,10}... | collective-permute-start | bytes 393224 | tf_op jit(solution)/shard_map/ppermute | solution.py:395
  138.2 153.5 %collective-permute-start.13 = (bf16[1,4,64,256]{3,2,1,0:T(8,128)(2,1)S(1)}, bf16[1,4,64,256]{3,2,1,0:T(8,128)(2,1)}, u32[]{:S(2)}, u32[]{:S(2)}) collective-permute-start(bf16[1,4,64,256]{3,2,1,0:T(8,128)(2,1)S(1)} %copy-done.12), channel_id=1, source_target_pairs={{0,28},{2,30},{4,24},{6,26},{8,20},{10,22},{12,16},{14,18},{16,12}... | collective-permute-start | bytes 393224 | tf_op jit(solution)/shard_map/ppermute | solution.py:395
  139.4 155.7 %collective-permute-start.14 = (bf16[1,4,64,256]{3,2,1,0:T(8,128)(2,1)S(1)}, bf16[1,4,64,256]{3,2,1,0:T(8,128)(2,1)}, u32[]{:S(2)}, u32[]{:S(2)}) collective-permute-start(bf16[1,4,64,256]{3,2,1,0:T(8,128)(2,1)S(1)} %copy-done.10), channel_id=1, source_target_pairs={{0,30},{2,28},{4,26},{6,24},{8,22},{10,20},{12,18},{14,16},{16,14}... | collective-permute-start | bytes 393224 | tf_op jit(solution)/shard_map/ppermute | solution.py:395
  142.6 160.3 %collective-permute-start.11 = (bf16[1,4,64,256]{3,2,1,0:T(8,128)(2,1)S(1)}, bf16[1,4,64,256]{3,2,1,0:T(8,128)(2,1)}, u32[]{:S(2)}, u32[]{:S(2)}) collective-permute-start(bf16[1,4,64,256]{3,2,1,0:T(8,128)(2,1)S(1)} %copy-done.1), channel_id=1, source_target_pairs={{0,24},{2,26},{4,28},{6,30},{8,16},{10,18},{12,20},{14,22},{16,8},... | collective-permute-start | bytes 393224 | tf_op jit(solution)/shard_map/ppermute | solution.py:395
  142.8 167.5 %collective-permute-start.8 = (bf16[1,4,64,256]{3,2,1,0:T(8,128)(2,1)S(1)}, bf16[1,4,64,256]{3,2,1,0:T(8,128)(2,1)}, u32[]{:S(2)}, u32[]{:S(2)}) collective-permute-start(bf16[1,4,64,256]{3,2,1,0:T(8,128)(2,1)S(1)} %copy-done.7), channel_id=1, source_target_pairs={{0,18},{2,16},{4,22},{6,20},{8,26},{10,24},{12,30},{14,28},{16,2},... | collective-permute-start | bytes 393224 | tf_op jit(solution)/shard_map/ppermute | solution.py:395
  244.1 69.0 %collective-permute-start.9 = (bf16[1,4,64,256]{3,2,1,0:T(8,128)(2,1)S(1)}, bf16[1,4,64,256]{3,2,1,0:T(8,128)(2,1)}, u32[]{:S(2)}, u32[]{:S(2)}) collective-permute-start(bf16[1,4,64,256]{3,2,1,0:T(8,128)(2,1)S(1)} %copy-done.6), channel_id=1, source_target_pairs={{0,20},{2,22},{4,16},{6,18},{8,28},{10,30},{12,24},{14,26},{16,4},... | collective-permute-start | bytes 393224 | tf_op jit(solution)/shard_map/ppermute | solution.py:395
  291.7 25.2 %collective-permute-start.10 = (bf16[1,4,64,256]{3,2,1,0:T(8,128)(2,1)S(1)}, bf16[1,4,64,256]{3,2,1,0:T(8,128)(2,1)}, u32[]{:S(2)}, u32[]{:S(2)}) collective-permute-start(bf16[1,4,64,256]{3,2,1,0:T(8,128)(2,1)S(1)} %copy-done.5), channel_id=1, source_target_pairs={{0,22},{2,20},{4,18},{6,16},{8,30},{10,28},{12,26},{14,24},{16,6},... | collective-permute-start | bytes 393224 | tf_op jit(solution)/shard_map/ppermute | solution.py:395
  333.2 25.3 %collective-permute-start.19 = (bf16[1,4,64,256]{3,2,1,0:T(8,128)(2,1)}, bf16[1,4,64,256]{3,2,1,0:T(8,128)(2,1)}, u32[]{:S(2)}, u32[]{:S(2)}) collective-permute-start(bf16[1,4,64,256]{3,2,1,0:T(8,128)(2,1)} %get-tuple-element.127), channel_id=1, source_target_pairs={{0,6},{2,4},{4,2},{6,0},{8,14},{10,12},{12,10},{14,8},{16,22},{18,... | collective-permute-start | bytes 393224 | tf_op jit(solution)/shard_map/ppermute | solution.py:395
  334.0 25.9 %collective-permute-start.20 = (bf16[1,4,64,256]{3,2,1,0:T(8,128)(2,1)}, bf16[1,4,64,256]{3,2,1,0:T(8,128)(2,1)}, u32[]{:S(2)}, u32[]{:S(2)}) collective-permute-start(bf16[1,4,64,256]{3,2,1,0:T(8,128)(2,1)} %get-tuple-element.128), channel_id=1, source_target_pairs={{0,8},{2,10},{4,12},{6,14},{8,0},{10,2},{12,4},{14,6},{16,24},{18,... | collective-permute-start | bytes 393224 | tf_op jit(solution)/shard_map/ppermute | solution.py:395
  334.0 25.9 %collective-permute-start.21 = (bf16[1,4,64,256]{3,2,1,0:T(8,128)(2,1)}, bf16[1,4,64,256]{3,2,1,0:T(8,128)(2,1)}, u32[]{:S(2)}, u32[]{:S(2)}) collective-permute-start(bf16[1,4,64,256]{3,2,1,0:T(8,128)(2,1)} %get-tuple-element.129), channel_id=1, source_target_pairs={{0,10},{2,8},{4,14},{6,12},{8,2},{10,0},{12,6},{14,4},{16,26},{18,... | collective-permute-start | bytes 393224 | tf_op jit(solution)/shard_map/ppermute | solution.py:395
  358.6 63.4 %collective-permute-start.16 = (bf16[2,4,256,256]{3,2,1,0:T(8,128)(2,1)}, bf16[2,4,256,256]{3,2,1,0:T(8,128)(2,1)}, u32[]{:S(2)}, u32[]{:S(2)}) collective-permute-start(bf16[2,4,256,256]{3,2,1,0:T(8,128)(2,1)} %get-tuple-element.124), channel_id=1, source_target_pairs={{0,1},{1,0},{2,3},{3,2},{4,5},{5,4},{6,7},{7,6},{8,9},{9,8},{10,11... | collective-permute-start | bytes 3145736 | tf_op jit(solution)/shard_map/ppermute | solution.py:395
  362.7 27.1 %collective-permute-start.26 = (bf16[1,4,64,256]{3,2,1,0:T(8,128)(2,1)}, bf16[1,4,64,256]{3,2,1,0:T(8,128)(2,1)}, u32[]{:S(2)}, u32[]{:S(2)}) collective-permute-start(bf16[1,4,64,256]{3,2,1,0:T(8,128)(2,1)} %get-tuple-element.134), channel_id=1, source_target_pairs={{0,20},{2,22},{4,16},{6,18},{8,28},{10,30},{12,24},{14,26},{16,4},... | collective-permute-start | bytes 393224 | tf_op jit(solution)/shard_map/ppermute | solution.py:395
  363.4 29.2 %collective-permute-start.27 = (bf16[1,4,64,256]{3,2,1,0:T(8,128)(2,1)}, bf16[1,4,64,256]{3,2,1,0:T(8,128)(2,1)}, u32[]{:S(2)}, u32[]{:S(2)}) collective-permute-start(bf16[1,4,64,256]{3,2,1,0:T(8,128)(2,1)} %get-tuple-element.135), channel_id=1, source_target_pairs={{0,22},{2,20},{4,18},{6,16},{8,30},{10,28},{12,26},{14,24},{16,6},... | collective-permute-start | bytes 393224 | tf_op jit(solution)/shard_map/ppermute | solution.py:395
  437.9 46.3 %collective-permute-start.33 = (bf16[4,4,256,256]{3,2,1,0:T(8,128)(2,1)}, bf16[4,4,256,256]{3,2,1,0:T(8,128)(2,1)}, u32[]{:S(2)}, u32[]{:S(2)}) collective-permute-start(bf16[4,4,256,256]{3,2,1,0:T(8,128)(2,1)} %get-tuple-element.143), channel_id=1, source_target_pairs={{0,1},{1,0},{2,3},{3,2},{4,5},{5,4},{6,7},{7,6},{8,9},{9,8},{10,11... | collective-permute-start | bytes 6291464 | tf_op jit(solution)/shard_map/ppermute | solution.py:395
  508.7 327.2 %all-to-all-start.2 = ((bf16[16,4,2,128,256]{4,3,2,1,0:T(8,128)(2,1)}), bf16[16,4,2,128,256]{4,3,2,1,0:T(8,128)(2,1)}, u32[]{:S(2)}, u32[]{:S(2)}) async-start(bf16[16,4,2,128,256]{4,3,2,1,0:T(8,128)(2,1)} %shard_map.58.refs_3_), calls=%async_computation.2 | async-start | bytes 16777216 | tf_op jit(solution)/shard_map/all_to_all | solution.py:400
  539.2 224.4 %collective-permute-start.34 = (bf16[3,4,256,256]{3,2,1,0:T(8,128)(2,1)}, bf16[3,4,256,256]{3,2,1,0:T(8,128)(2,1)}, u32[]{:S(2)}, u32[]{:S(2)}) collective-permute-start(bf16[3,4,256,256]{3,2,1,0:T(8,128)(2,1)} %get-tuple-element.145), channel_id=1, source_target_pairs={{0,1},{1,0},{2,3},{3,2},{4,5},{5,4},{6,7},{7,6},{8,9},{9,8},{10,11... | collective-permute-start | bytes 4718600 | tf_op jit(solution)/shard_map/ppermute | solution.py:395
  539.9 32.3 %collective-permute-start.36 = (bf16[1,4,64,256]{3,2,1,0:T(8,128)(2,1)}, bf16[1,4,64,256]{3,2,1,0:T(8,128)(2,1)}, u32[]{:S(2)}, u32[]{:S(2)}) collective-permute-start(bf16[1,4,64,256]{3,2,1,0:T(8,128)(2,1)} %get-tuple-element.147), channel_id=1, source_target_pairs={{0,4},{2,6},{4,0},{6,2},{8,12},{10,14},{12,8},{14,10},{16,20},{18,... | collective-permute-start | bytes 393224 | tf_op jit(solution)/shard_map/ppermute | solution.py:395
  541.5 34.0 %collective-permute-start.37 = (bf16[1,4,64,256]{3,2,1,0:T(8,128)(2,1)}, bf16[1,4,64,256]{3,2,1,0:T(8,128)(2,1)}, u32[]{:S(2)}, u32[]{:S(2)}) collective-permute-start(bf16[1,4,64,256]{3,2,1,0:T(8,128)(2,1)} %get-tuple-element.148), channel_id=1, source_target_pairs={{0,6},{2,4},{4,2},{6,0},{8,14},{10,12},{12,10},{14,8},{16,22},{18,... | collective-permute-start | bytes 393224 | tf_op jit(solution)/shard_map/ppermute | solution.py:395
  541.6 117.9 %collective-permute-start.38 = (bf16[1,4,64,256]{3,2,1,0:T(8,128)(2,1)}, bf16[1,4,64,256]{3,2,1,0:T(8,128)(2,1)}, u32[]{:S(2)}, u32[]{:S(2)}) collective-permute-start(bf16[1,4,64,256]{3,2,1,0:T(8,128)(2,1)} %get-tuple-element.149), channel_id=1, source_target_pairs={{0,8},{2,10},{4,12},{6,14},{8,0},{10,2},{12,4},{14,6},{16,24},{18,... | collective-permute-start | bytes 393224 | tf_op jit(solution)/shard_map/ppermute | solution.py:395
  544.4 118.9 %collective-permute-start.39 = (bf16[1,4,64,256]{3,2,1,0:T(8,128)(2,1)}, bf16[1,4,64,256]{3,2,1,0:T(8,128)(2,1)}, u32[]{:S(2)}, u32[]{:S(2)}) collective-permute-start(bf16[1,4,64,256]{3,2,1,0:T(8,128)(2,1)} %get-tuple-element.150), channel_id=1, source_target_pairs={{0,10},{2,8},{4,14},{6,12},{8,2},{10,0},{12,6},{14,4},{16,26},{18,... | collective-permute-start | bytes 393224 | tf_op jit(solution)/shard_map/ppermute | solution.py:395
  572.1 94.3 %collective-permute-start.40 = (bf16[1,4,64,256]{3,2,1,0:T(8,128)(2,1)}, bf16[1,4,64,256]{3,2,1,0:T(8,128)(2,1)}, u32[]{:S(2)}, u32[]{:S(2)}) collective-permute-start(bf16[1,4,64,256]{3,2,1,0:T(8,128)(2,1)} %get-tuple-element.151), channel_id=1, source_target_pairs={{0,12},{2,14},{4,8},{6,10},{8,4},{10,6},{12,0},{14,2},{16,28},{18,... | collective-permute-start | bytes 393224 | tf_op jit(solution)/shard_map/ppermute | solution.py:395
  575.5 94.3 %collective-permute-start.41 = (bf16[1,4,64,256]{3,2,1,0:T(8,128)(2,1)}, bf16[1,4,64,256]{3,2,1,0:T(8,128)(2,1)}, u32[]{:S(2)}, u32[]{:S(2)}) collective-permute-start(bf16[1,4,64,256]{3,2,1,0:T(8,128)(2,1)} %get-tuple-element.152), channel_id=1, source_target_pairs={{0,14},{2,12},{4,10},{6,8},{8,6},{10,4},{12,2},{14,0},{16,30},{18,... | collective-permute-start | bytes 393224 | tf_op jit(solution)/shard_map/ppermute | solution.py:395
  659.5 58.5 %collective-permute-start.42 = (bf16[1,4,64,256]{3,2,1,0:T(8,128)(2,1)}, bf16[1,4,64,256]{3,2,1,0:T(8,128)(2,1)}, u32[]{:S(2)}, u32[]{:S(2)}) collective-permute-start(bf16[1,4,64,256]{3,2,1,0:T(8,128)(2,1)} %get-tuple-element.153), channel_id=1, source_target_pairs={{0,16},{2,18},{4,20},{6,22},{8,24},{10,26},{12,28},{14,30},{16,0},... | collective-permute-start | bytes 393224 | tf_op jit(solution)/shard_map/ppermute | solution.py:395
  663.3 58.8 %collective-permute-start.43 = (bf16[1,4,64,256]{3,2,1,0:T(8,128)(2,1)}, bf16[1,4,64,256]{3,2,1,0:T(8,128)(2,1)}, u32[]{:S(2)}, u32[]{:S(2)}) collective-permute-start(bf16[1,4,64,256]{3,2,1,0:T(8,128)(2,1)} %get-tuple-element.154), channel_id=1, source_target_pairs={{0,18},{2,16},{4,22},{6,20},{8,26},{10,24},{12,30},{14,28},{16,2},... | collective-permute-start | bytes 393224 | tf_op jit(solution)/shard_map/ppermute | solution.py:395
  666.4 63.9 %collective-permute-start.44 = (bf16[1,4,64,256]{3,2,1,0:T(8,128)(2,1)}, bf16[1,4,64,256]{3,2,1,0:T(8,128)(2,1)}, u32[]{:S(2)}, u32[]{:S(2)}) collective-permute-start(bf16[1,4,64,256]{3,2,1,0:T(8,128)(2,1)} %get-tuple-element.155), channel_id=1, source_target_pairs={{0,20},{2,22},{4,16},{6,18},{8,28},{10,30},{12,24},{14,26},{16,4},... | collective-permute-start | bytes 393224 | tf_op jit(solution)/shard_map/ppermute | solution.py:395
  669.8 64.2 %collective-permute-start.45 = (bf16[1,4,64,256]{3,2,1,0:T(8,128)(2,1)}, bf16[1,4,64,256]{3,2,1,0:T(8,128)(2,1)}, u32[]{:S(2)}, u32[]{:S(2)}) collective-permute-start(bf16[1,4,64,256]{3,2,1,0:T(8,128)(2,1)} %get-tuple-element.156), channel_id=1, source_target_pairs={{0,22},{2,20},{4,18},{6,16},{8,30},{10,28},{12,26},{14,24},{16,6},... | collective-permute-start | bytes 393224 | tf_op jit(solution)/shard_map/ppermute | solution.py:395
  779.5 43.0 %collective-permute-start.67 = (bf16[2,4,256,256]{3,2,1,0:T(8,128)(2,1)}, bf16[2,4,256,256]{3,2,1,0:T(8,128)(2,1)}, u32[]{:S(2)}, u32[]{:S(2)}) collective-permute-start(bf16[2,4,256,256]{3,2,1,0:T(8,128)(2,1)} %get-tuple-element.182), channel_id=1, source_target_pairs={{0,1},{1,0},{2,3},{3,2},{4,5},{5,4},{6,7},{7,6},{8,9},{9,8},{10,11... | collective-permute-start | bytes 3145736 | tf_op jit(solution)/shard_map/ppermute | solution.py:395
  779.8 34.7 %collective-permute-start.68 = (bf16[1,4,256,256]{3,2,1,0:T(8,128)(2,1)}, bf16[1,4,256,256]{3,2,1,0:T(8,128)(2,1)}, u32[]{:S(2)}, u32[]{:S(2)}) collective-permute-start(bf16[1,4,256,256]{3,2,1,0:T(8,128)(2,1)} %get-tuple-element.184), channel_id=1, source_target_pairs={{0,1},{1,0},{2,3},{3,2},{4,5},{5,4},{6,7},{7,6},{8,9},{9,8},{10,11... | collective-permute-start | bytes 1572872 | tf_op jit(solution)/shard_map/ppermute | solution.py:395
  835.9 180.1 %all-to-all-start.3 = ((bf16[16,2,2,128,256]{4,3,2,1,0:T(8,128)(2,1)}), bf16[16,2,2,128,256]{4,3,2,1,0:T(8,128)(2,1)}, u32[]{:S(2)}, u32[]{:S(2)}) async-start(bf16[16,2,2,128,256]{4,3,2,1,0:T(8,128)(2,1)} %shard_map.64), calls=%async_computation.3 | async-start | bytes 8388608 | tf_op jit(solution)/shard_map/all_to_all | solution.py:400
  849.1 27.8 %collective-permute-start.70 = (bf16[1,2,128,256]{3,2,1,0:T(8,128)(2,1)S(1)}, bf16[1,2,128,256]{3,2,1,0:T(8,128)(2,1)}, u32[]{:S(2)}, u32[]{:S(2)}) collective-permute-start(bf16[1,2,128,256]{3,2,1,0:T(8,128)(2,1)S(1)} %copy-done.15), channel_id=1, source_target_pairs={{0,4},{2,6},{4,0},{6,2},{8,12},{10,14},{12,8},{14,10},{16,20},{18,... | collective-permute-start | bytes 393224 | tf_op jit(solution)/shard_map/ppermute | solution.py:395
  850.7 29.6 %collective-permute-start.71 = (bf16[1,2,128,256]{3,2,1,0:T(8,128)(2,1)S(1)}, bf16[1,2,128,256]{3,2,1,0:T(8,128)(2,1)}, u32[]{:S(2)}, u32[]{:S(2)}) collective-permute-start(bf16[1,2,128,256]{3,2,1,0:T(8,128)(2,1)S(1)} %copy-done.13), channel_id=1, source_target_pairs={{0,6},{2,4},{4,2},{6,0},{8,14},{10,12},{12,10},{14,8},{16,22},{18,... | collective-permute-start | bytes 393224 | tf_op jit(solution)/shard_map/ppermute | solution.py:395
  850.8 68.5 %collective-permute-start.72 = (bf16[1,2,128,256]{3,2,1,0:T(8,128)(2,1)S(1)}, bf16[1,2,128,256]{3,2,1,0:T(8,128)(2,1)}, u32[]{:S(2)}, u32[]{:S(2)}) collective-permute-start(bf16[1,2,128,256]{3,2,1,0:T(8,128)(2,1)S(1)} %copy-done.11), channel_id=1, source_target_pairs={{0,8},{2,10},{4,12},{6,14},{8,0},{10,2},{12,4},{14,6},{16,24},{18,... | collective-permute-start | bytes 393224 | tf_op jit(solution)/shard_map/ppermute | solution.py:395
  861.8 62.8 %collective-permute-start.73 = (bf16[1,2,128,256]{3,2,1,0:T(8,128)(2,1)S(1)}, bf16[1,2,128,256]{3,2,1,0:T(8,128)(2,1)}, u32[]{:S(2)}, u32[]{:S(2)}) collective-permute-start(bf16[1,2,128,256]{3,2,1,0:T(8,128)(2,1)S(1)} %copy-done.9), channel_id=1, source_target_pairs={{0,10},{2,8},{4,14},{6,12},{8,2},{10,0},{12,6},{14,4},{16,26},{18,... | collective-permute-start | bytes 393224 | tf_op jit(solution)/shard_map/ppermute | solution.py:395
  864.1 64.1 %collective-permute-start.74 = (bf16[1,2,128,256]{3,2,1,0:T(8,128)(2,1)S(1)}, bf16[1,2,128,256]{3,2,1,0:T(8,128)(2,1)}, u32[]{:S(2)}, u32[]{:S(2)}) collective-permute-start(bf16[1,2,128,256]{3,2,1,0:T(8,128)(2,1)S(1)} %copy-done.8), channel_id=1, source_target_pairs={{0,12},{2,14},{4,8},{6,10},{8,4},{10,6},{12,0},{14,2},{16,28},{18,... | collective-permute-start | bytes 393224 | tf_op jit(solution)/shard_map/ppermute | solution.py:395
  877.0 64.9 %collective-permute-start.75 = (bf16[1,2,128,256]{3,2,1,0:T(8,128)(2,1)}, bf16[1,2,128,256]{3,2,1,0:T(8,128)(2,1)}, u32[]{:S(2)}, u32[]{:S(2)}) collective-permute-start(bf16[1,2,128,256]{3,2,1,0:T(8,128)(2,1)} %get-tuple-element.192), channel_id=1, source_target_pairs={{0,14},{2,12},{4,10},{6,8},{8,6},{10,4},{12,2},{14,0},{16,30},{18,... | collective-permute-start | bytes 393224 | tf_op jit(solution)/shard_map/ppermute | solution.py:395
  880.3 78.1 %collective-permute-start.76 = (bf16[1,2,128,256]{3,2,1,0:T(8,128)(2,1)}, bf16[1,2,128,256]{3,2,1,0:T(8,128)(2,1)}, u32[]{:S(2)}, u32[]{:S(2)}) collective-permute-start(bf16[1,2,128,256]{3,2,1,0:T(8,128)(2,1)} %get-tuple-element.193), channel_id=1, source_target_pairs={{0,16},{2,18},{4,20},{6,22},{8,24},{10,26},{12,28},{14,30},{16,0},... | collective-permute-start | bytes 393224 | tf_op jit(solution)/shard_map/ppermute | solution.py:395
  919.3 44.0 %collective-permute-start.77 = (bf16[1,2,128,256]{3,2,1,0:T(8,128)(2,1)}, bf16[1,2,128,256]{3,2,1,0:T(8,128)(2,1)}, u32[]{:S(2)}, u32[]{:S(2)}) collective-permute-start(bf16[1,2,128,256]{3,2,1,0:T(8,128)(2,1)} %get-tuple-element.194), channel_id=1, source_target_pairs={{0,18},{2,16},{4,22},{6,20},{8,26},{10,24},{12,30},{14,28},{16,2},... | collective-permute-start | bytes 393224 | tf_op jit(solution)/shard_map/ppermute | solution.py:395
  924.6 43.1 %collective-permute-start.78 = (bf16[1,2,128,256]{3,2,1,0:T(8,128)(2,1)}, bf16[1,2,128,256]{3,2,1,0:T(8,128)(2,1)}, u32[]{:S(2)}, u32[]{:S(2)}) collective-permute-start(bf16[1,2,128,256]{3,2,1,0:T(8,128)(2,1)} %get-tuple-element.195), channel_id=1, source_target_pairs={{0,20},{2,22},{4,16},{6,18},{8,28},{10,30},{12,24},{14,26},{16,4},... | collective-permute-start | bytes 393224 | tf_op jit(solution)/shard_map/ppermute | solution.py:395
  928.2 47.2 %collective-permute-start.79 = (bf16[1,2,128,256]{3,2,1,0:T(8,128)(2,1)}, bf16[1,2,128,256]{3,2,1,0:T(8,128)(2,1)}, u32[]{:S(2)}, u32[]{:S(2)}) collective-permute-start(bf16[1,2,128,256]{3,2,1,0:T(8,128)(2,1)} %get-tuple-element.196), channel_id=1, source_target_pairs={{0,22},{2,20},{4,18},{6,16},{8,30},{10,28},{12,26},{14,24},{16,6},... | collective-permute-start | bytes 393224 | tf_op jit(solution)/shard_map/ppermute | solution.py:395
  941.8 52.8 %collective-permute-start.80 = (bf16[1,2,128,256]{3,2,1,0:T(8,128)(2,1)}, bf16[1,2,128,256]{3,2,1,0:T(8,128)(2,1)}, u32[]{:S(2)}, u32[]{:S(2)}) collective-permute-start(bf16[1,2,128,256]{3,2,1,0:T(8,128)(2,1)} %get-tuple-element.197), channel_id=1, source_target_pairs={{0,24},{2,26},{4,28},{6,30},{8,16},{10,18},{12,20},{14,22},{16,8},... | collective-permute-start | bytes 393224 | tf_op jit(solution)/shard_map/ppermute | solution.py:395
  958.5 36.2 %collective-permute-start.81 = (bf16[1,2,128,256]{3,2,1,0:T(8,128)(2,1)}, bf16[1,2,128,256]{3,2,1,0:T(8,128)(2,1)}, u32[]{:S(2)}, u32[]{:S(2)}) collective-permute-start(bf16[1,2,128,256]{3,2,1,0:T(8,128)(2,1)} %get-tuple-element.198), channel_id=1, source_target_pairs={{0,26},{2,24},{4,30},{6,28},{8,18},{10,16},{12,22},{14,20},{16,10}... | collective-permute-start | bytes 393224 | tf_op jit(solution)/shard_map/ppermute | solution.py:395
  963.3 33.5 %collective-permute-start.82 = (bf16[1,2,128,256]{3,2,1,0:T(8,128)(2,1)}, bf16[1,2,128,256]{3,2,1,0:T(8,128)(2,1)}, u32[]{:S(2)}, u32[]{:S(2)}) collective-permute-start(bf16[1,2,128,256]{3,2,1,0:T(8,128)(2,1)} %get-tuple-element.199), channel_id=1, source_target_pairs={{0,28},{2,30},{4,24},{6,26},{8,20},{10,22},{12,16},{14,18},{16,12}... | collective-permute-start | bytes 393224 | tf_op jit(solution)/shard_map/ppermute | solution.py:395
  967.8 29.0 %collective-permute-start.83 = (bf16[1,2,128,256]{3,2,1,0:T(8,128)(2,1)}, bf16[1,2,128,256]{3,2,1,0:T(8,128)(2,1)}, u32[]{:S(2)}, u32[]{:S(2)}) collective-permute-start(bf16[1,2,128,256]{3,2,1,0:T(8,128)(2,1)} %get-tuple-element.200), channel_id=1, source_target_pairs={{0,30},{2,28},{4,26},{6,24},{8,22},{10,20},{12,18},{14,16},{16,14}... | collective-permute-start | bytes 393224 | tf_op jit(solution)/shard_map/ppermute | solution.py:395
  1013.4 29.1 %collective-permute-start.66 = (bf16[1,2,128,256]{3,2,1,0:T(8,128)(2,1)}, bf16[1,2,128,256]{3,2,1,0:T(8,128)(2,1)}, u32[]{:S(2)}, u32[]{:S(2)}) collective-permute-start(bf16[1,2,128,256]{3,2,1,0:T(8,128)(2,1)} %get-tuple-element.180), channel_id=1, source_target_pairs={{0,30},{2,28},{4,26},{6,24},{8,22},{10,20},{12,18},{14,16},{16,14}... | collective-permute-start | bytes 393224 | tf_op jit(solution)/shard_map/ppermute | solution.py:395
  1027.0 23.1 %collective-permute-start.53 = (bf16[1,2,128,256]{3,2,1,0:T(8,128)(2,1)}, bf16[1,2,128,256]{3,2,1,0:T(8,128)(2,1)}, u32[]{:S(2)}, u32[]{:S(2)}) collective-permute-start(bf16[1,2,128,256]{3,2,1,0:T(8,128)(2,1)} %get-tuple-element.166), channel_id=1, source_target_pairs={{0,18},{2,16},{4,22},{6,20},{8,26},{10,24},{12,30},{14,28},{16,2},... | collective-permute-start | bytes 393224 | tf_op jit(solution)/shard_map/ppermute | solution.py:395
  1029.3 26.0 %collective-permute-start.55 = (bf16[1,2,128,256]{3,2,1,0:T(8,128)(2,1)}, bf16[1,2,128,256]{3,2,1,0:T(8,128)(2,1)}, u32[]{:S(2)}, u32[]{:S(2)}) collective-permute-start(bf16[1,2,128,256]{3,2,1,0:T(8,128)(2,1)} %get-tuple-element.168), channel_id=1, source_target_pairs={{0,22},{2,20},{4,18},{6,16},{8,30},{10,28},{12,26},{14,24},{16,6},... | collective-permute-start | bytes 393224 | tf_op jit(solution)/shard_map/ppermute | solution.py:395
  (57 other events, 2219.7 us)

commit v2 on v1

--- a/solution.py
+++ b/solution.py
@@ -418,7 +418,7 @@
     index = window_index.reshape(1, points)
 
     took = gave = [((0, freqs, False),)] * CHUNKS
-    if freqs > 2:
+    if freqs > 2 and tiles > GROUP:
         took = [((0, freqs - 1, False), (freqs - 1, 1, True))] * CHUNKS
         took = [((0, 1, True), (1, freqs - 2, False), (freqs - 1, 1, True))] + took[1:]
         gave = gave[:-1] + [((0, 1, True), (1, freqs - 2, False), (freqs - 1, 1, True))]
@@ -428,19 +428,22 @@
 
     sent = []
     token = None
+    groups = tiles // GROUP
     for h in range(CHUNKS):
-        sent.append([])
-        for n, (*piece, split) in enumerate(took[h]):
-            groups = tiles // GROUP
-            some = 1 if split and h == n == 0 else groups
-            made = []
-            for base in reversed(range(0, groups, some)):
-                part = project(
-                    pos, col_factors, wavefield, piece, h, width, tiles, split, base, some, token
-                )
-                token = part[0] if split else part
-                made = [*part, *made] if split else part
-            sent[h].append(trade(made, tiles, split))
+        jobs = [(n, 0, groups) for n in range(len(took[h]))]
+        if h == 0 and took[h][0][2]:
+            near = [(0, base, 1) for base in reversed(range(groups))]
+            jobs[1:2] = [jobs[1]] + near[groups - groups // 2 :]
+            jobs[:1] = near[: groups - groups // 2]
+        made = [[] for _ in took[h]]
+        for n, base, some in jobs:
+            *piece, split = took[h][n]
+            part = project(
+                pos, col_factors, wavefield, piece, h, width, tiles, split, base, some, token
+            )
+            token = part[0] if split else part
+            made[n] = [*part, *made[n]] if split else part
+        sent.append([trade(made[n], tiles, took[h][n][2]) for n in range(len(took[h]))])
     back = []
     for h in range(CHUNKS):
         parts = []

time: 1060 us -> 1050 us (level)
  transfers between devices with their start and end apart: 88 -> 88, of which waited for: 35 -> 35; matrix products, arithmetic and copies ran while one was open for 0% -> 0% of each run, Pallas kernels for 21% -> 22%
where the time goes in v2:
time: 1050 us
  waiting for transfers between devices  558 us (53%)
  Pallas kernels  252 us (24%)
  starting transfers between devices  240 us (23%)
    ppermute x84, waiting for transfers between devices, send(): return lax.ppermute(array, axis, [(n, n ^ mask) for n in range(size)])  516 us
    ppermute x84, starting transfers between devices, send(): return lax.ppermute(array, axis, [(n, n ^ mask) for n in range(size)])  188 us
    pallas_call x16, Pallas kernels, call(): return made if after is None else lambda *args: made(*args, after)  162 us
    all_to_all x4, starting transfers between devices, trade(): return [lax.all_to_all(made, 'tile', 0, 0, tiled=True)]  51.2 us
    all_to_all x4, waiting for transfers between devices, trade(): return [lax.all_to_all(made, 'tile', 0, 0, tiled=True)]  41.9 us
    pallas_call x2, Pallas kernels, contract(): call(functools.partial(contract_kernel, (tiles, shares, col_local, both /...  32.5 us
    pallas_call x2, Pallas kernels, window(): call(functools.partial(window_kernel, (shares, took, gave, rows, 16, both...  31.9 us
  transfers between devices with their start and end apart: 88, of which 35 were waited for; matrix products, arithmetic and copies ran while one was open for 0% of the time, Pallas kernels for 22%

profile of v2, /device:TPU:1, one launch (start us, length us, event | category | flops | bytes accessed | tf_op | source)
XLA Modules:
  0.0 1051.2 jit_solution(4284573012992987978)
XLA Ops:
  8.7 13.3 %shard_map.48.refs_3_ = bf16[16,2,4,64,256]{4,3,2,1,0:T(8,128)(2,1)} custom-call(s32[2]{0:T(128)} %pad_add_fusion.pos.refs_0_, bf16[4,2,1024,2048]{3,2,1,0:T(8,128)(2,1)} %refs_0_.1, bf16[4,2,1024,256]{3,2,1,0:T(8,128)(2,1)} %refs_2_.14, bf16[1,4,64,256]{3,2,1,0:T(8,128)(2,1)} %get-tuple-element.104.refs_3_), custom_call_target="tpu_custom_call" | custom-call | flops 4294967296 | bytes 18874368 | tf_op jit(solution)/shard_map/pallas_call | solution.py:48
  22.0 7.3 all-to-all-start.1
  37.4 9.2 shard_map.51
  46.6 18.9 %shard_map.52.refs_3_ = bf16[16,3,4,64,256]{4,3,2,1,0:T(8,128)(2,1)} custom-call(s32[2]{0:T(128)} %pad_add_fusion.pos.refs_0_, bf16[4,2,1024,2048]{3,2,1,0:T(8,128)(2,1)} %refs_0_.1, bf16[4,2,1024,256]{3,2,1,0:T(8,128)(2,1)} %refs_2_.14, bf16[1,4,64,256]{3,2,1,0:T(8,128)(2,1)} %get-tuple-element.107.refs_3_.refs_2_), custom_call_target="tpu_custom_call" | custom-call | flops 6442450944 | bytes 28311552 | tf_op jit(solution)/shard_map/pallas_call | solution.py:48
  65.5 41.9 %all-to-all-done.1.refs_2_ = bf16[16,2,4,64,256]{4,3,2,1,0:T(8,128)(2,1)} async-done(((bf16[16,2,4,64,256]{4,3,2,1,0:T(8,128)(2,1)}), bf16[16,2,4,64,256]{4,3,2,1,0:T(8,128)(2,1)}, u32[]{:S(2)}, u32[]{:S(2)}) %all-to-all-start.1) | async-done | bytes 4194336 | tf_op jit(solution)/shard_map/all_to_all | solution.py:400
  107.5 19.1 %all-to-all-start = ((bf16[16,3,4,64,256]{4,3,2,1,0:T(8,128)(2,1)}), bf16[16,3,4,64,256]{4,3,2,1,0:T(8,128)(2,1)}, u32[]{:S(2)}, u32[]{:S(2)}) async-start(bf16[16,3,4,64,256]{4,3,2,1,0:T(8,128)(2,1)} %shard_map.52.refs_3_), calls=%async_computation | async-start | bytes 12582912 | tf_op jit(solution)/shard_map/all_to_all | solution.py:400
  134.6 101.4 %collective-permute-done.12.refs_15_ = bf16[1,4,64,256]{3,2,1,0:T(8,128)(2,1)} collective-permute-done((bf16[1,4,64,256]{3,2,1,0:T(8,128)(2,1)S(1)}, bf16[1,4,64,256]{3,2,1,0:T(8,128)(2,1)}, u32[]{:S(2)}, u32[]{:S(2)}) %collective-permute-start.12) | collective-permute-done | bytes 131104 | tf_op jit(solution)/shard_map/ppermute | solution.py:395
  236.0 47.5 %collective-permute-start.9 = (bf16[1,4,64,256]{3,2,1,0:T(8,128)(2,1)S(1)}, bf16[1,4,64,256]{3,2,1,0:T(8,128)(2,1)}, u32[]{:S(2)}, u32[]{:S(2)}) collective-permute-start(bf16[1,4,64,256]{3,2,1,0:T(8,128)(2,1)S(1)} %copy-done.6), channel_id=1, source_target_pairs={{0,20},{2,22},{4,16},{6,18},{8,28},{10,30},{12,24},{14,26},{16,4},... | collective-permute-start | bytes 393224 | tf_op jit(solution)/shard_map/ppermute | solution.py:395
  287.0 7.8 collective-permute-start.7
  297.4 4.8 collective-permute-done.8.refs_11_
  314.5 9.1 shard_map.53
  327.5 7.4 shard_map.54
  337.7 12.7 %shard_map.55 = (bf16[2,4,256,256]{3,2,1,0:T(8,128)(2,1)}, bf16[2,4,256,256]{3,2,1,0:T(8,128)(2,1)}) custom-call(s32[2]{0:T(128)} %pad_add_fusion.pos.refs_0_, bf16[4,2,2048,1024]{3,2,1,0:T(8,128)(2,1)} %refs_1_.29, bf16[16,2,4,64,256]{4,3,2,1,0:T(8,128)(2,1)} %all-to-all-done.1.refs_2_, bf16[1,4,256,256]{3,2,1,0:T(8,128)(2,1)} %get-tuple-element.121.refs_3_.refs_0_), custom_call_target="tpu_custom_call" | custom-call | flops 4294967296 | bytes 23068672 | tf_op jit(solution)/shard_map/pallas_call | solution.py:48
  357.9 11.5 %collective-permute-done.24.refs_10_ = bf16[1,4,64,256]{3,2,1,0:T(8,128)(2,1)} collective-permute-done((bf16[1,4,64,256]{3,2,1,0:T(8,128)(2,1)}, bf16[1,4,64,256]{3,2,1,0:T(8,128)(2,1)}, u32[]{:S(2)}, u32[]{:S(2)}) %collective-permute-start.24) | collective-permute-done | bytes 131104 | tf_op jit(solution)/shard_map/ppermute | solution.py:395
  373.6 8.0 collective-permute-done.26.refs_12_
  393.0 7.4 shard_map.56
  401.5 12.3 %collective-permute-done.32.refs_5_ = bf16[1,4,256,256]{3,2,1,0:T(8,128)(2,1)} collective-permute-done((bf16[1,4,256,256]{3,2,1,0:T(8,128)(2,1)}, bf16[1,4,256,256]{3,2,1,0:T(8,128)(2,1)}, u32[]{:S(2)}, u32[]{:S(2)}) %collective-permute-start.32) | collective-permute-done | bytes 524320 | tf_op jit(solution)/shard_map/ppermute | solution.py:395
  413.9 16.0 %shard_map.57 = (bf16[4,4,256,256]{3,2,1,0:T(8,128)(2,1)}, bf16[4,4,256,256]{3,2,1,0:T(8,128)(2,1)}) custom-call(f32[16,8]{1,0:T(8,128)} %get-tuple-element.202.cosine, f32[16,8]{1,0:T(8,128)} %get-tuple-element.201.sine, s32[1,256]{1,0:T(1,128)} %bitcast.3, bf16[1,4,256,256]{3,2,1,0:T(8,128)(2,1)} %get-tuple-element.121.refs_3_.refs_0_, ...), custom_call_target="tpu_custom_call" | custom-call | flops 67108864 | bytes 8388608 | tf_op jit(solution)/shard_map/pallas_call | solution.py:234
  430.1 46.0 %collective-permute-done.33.refs_1_ = bf16[4,4,256,256]{3,2,1,0:T(8,128)(2,1)} collective-permute-done((bf16[4,4,256,256]{3,2,1,0:T(8,128)(2,1)}, bf16[4,4,256,256]{3,2,1,0:T(8,128)(2,1)}, u32[]{:S(2)}, u32[]{:S(2)}) %collective-permute-start.33) | collective-permute-done | bytes 2097184 | tf_op jit(solution)/shard_map/ppermute | solution.py:395
  476.1 24.5 %shard_map.58.refs_3_ = bf16[16,4,2,128,256]{4,3,2,1,0:T(8,128)(2,1)} custom-call(s32[2]{0:T(128)} %pad_add_fusion.pos.refs_0_, bf16[4,2,2048,1024]{3,2,1,0:T(8,128)(2,1)} %refs_1_.29, bf16[4,4,256,256]{3,2,1,0:T(8,128)(2,1)} %get-tuple-element.142.refs_0_, bf16[4,4,256,256]{3,2,1,0:T(8,128)(2,1)} %collective-permute-done.33.refs_1_), custom_call_target="tpu_custom_call" | custom-call | flops 8589934592 | bytes 46137344 | tf_op jit(solution)/shard_map/pallas_call | solution.py:291
  500.6 12.3 %all-to-all-start.2 = ((bf16[16,4,2,128,256]{4,3,2,1,0:T(8,128)(2,1)}), bf16[16,4,2,128,256]{4,3,2,1,0:T(8,128)(2,1)}, u32[]{:S(2)}, u32[]{:S(2)}) async-start(bf16[16,4,2,128,256]{4,3,2,1,0:T(8,128)(2,1)} %shard_map.58.refs_3_), calls=%async_computation.2 | async-start | bytes 16777216 | tf_op jit(solution)/shard_map/all_to_all | solution.py:400
  512.9 18.1 %shard_map.59 = (bf16[3,4,256,256]{3,2,1,0:T(8,128)(2,1)}, bf16[3,4,256,256]{3,2,1,0:T(8,128)(2,1)}) custom-call(s32[2]{0:T(128)} %pad_add_fusion.pos.refs_0_, bf16[4,2,2048,1024]{3,2,1,0:T(8,128)(2,1)} %refs_1_.29, bf16[16,3,4,64,256]{4,3,2,1,0:T(8,128)(2,1)} %all-to-all-done.refs_2_, bf16[16,4,2,128,256]{4,3,2,1,0:T(8,128)(2,1)} %shard_map.58.refs_3_), custom_call_target="tpu_custom_call" | custom-call | flops 6442450944 | bytes 34603008 | tf_op jit(solution)/shard_map/pallas_call | solution.py:48
  536.4 27.6 %collective-permute-done.36.refs_4_ = bf16[1,4,64,256]{3,2,1,0:T(8,128)(2,1)} collective-permute-done((bf16[1,4,64,256]{3,2,1,0:T(8,128)(2,1)}, bf16[1,4,64,256]{3,2,1,0:T(8,128)(2,1)}, u32[]{:S(2)}, u32[]{:S(2)}) %collective-permute-start.36) | collective-permute-done | bytes 131104 | tf_op jit(solution)/shard_map/ppermute | solution.py:395
  568.1 83.3 %collective-permute-done.38.refs_6_ = bf16[1,4,64,256]{3,2,1,0:T(8,128)(2,1)} collective-permute-done((bf16[1,4,64,256]{3,2,1,0:T(8,128)(2,1)}, bf16[1,4,64,256]{3,2,1,0:T(8,128)(2,1)}, u32[]{:S(2)}, u32[]{:S(2)}) %collective-permute-start.38) | collective-permute-done | bytes 131104 | tf_op jit(solution)/shard_map/ppermute | solution.py:395
  665.7 44.2 %collective-permute-done.42.refs_10_ = bf16[1,4,64,256]{3,2,1,0:T(8,128)(2,1)} collective-permute-done((bf16[1,4,64,256]{3,2,1,0:T(8,128)(2,1)}, bf16[1,4,64,256]{3,2,1,0:T(8,128)(2,1)}, u32[]{:S(2)}, u32[]{:S(2)}) %collective-permute-start.42) | collective-permute-done | bytes 131104 | tf_op jit(solution)/shard_map/ppermute | solution.py:395
  715.3 6.9 collective-permute-done.44.refs_12_
  729.2 5.5 collective-permute-done.49.refs_17_
  734.6 7.4 shard_map.60
  742.3 13.1 %collective-permute-done.50.refs_3_ = bf16[1,4,256,256]{3,2,1,0:T(8,128)(2,1)} collective-permute-done((bf16[1,4,256,256]{3,2,1,0:T(8,128)(2,1)}, bf16[1,4,256,256]{3,2,1,0:T(8,128)(2,1)}, u32[]{:S(2)}, u32[]{:S(2)}) %collective-permute-start.50) | collective-permute-done | bytes 524320 | tf_op jit(solution)/shard_map/ppermute | solution.py:395
  755.4 16.0 %shard_map.61 = (bf16[1,4,256,256]{3,2,1,0:T(8,128)(2,1)}, bf16[1,4,256,256]{3,2,1,0:T(8,128)(2,1)}, bf16[2,4,256,256]{3,2,1,0:T(8,128)(2,1)}, bf16[2,4,256,256]...) custom-call(f32[16,8]{1,0:T(8,128)} %get-tuple-element.202.cosine, ...), custom_call_target="tpu_custom_call" | custom-call | flops 67108864 | bytes 8388608 | tf_op jit(solution)/shard_map/pallas_call | solution.py:234
  772.9 33.5 %collective-permute-done.68.refs_1_ = bf16[1,4,256,256]{3,2,1,0:T(8,128)(2,1)} collective-permute-done((bf16[1,4,256,256]{3,2,1,0:T(8,128)(2,1)}, bf16[1,4,256,256]{3,2,1,0:T(8,128)(2,1)}, u32[]{:S(2)}, u32[]{:S(2)}) %collective-permute-start.68) | collective-permute-done | bytes 524320 | tf_op jit(solution)/shard_map/ppermute | solution.py:395
  806.4 7.9 shard_map.63
  814.4 13.4 %shard_map.64 = bf16[16,2,2,128,256]{4,3,2,1,0:T(8,128)(2,1)} custom-call(s32[2]{0:T(128)} %pad_add_fusion.pos.refs_0_, bf16[4,2,2048,1024]{3,2,1,0:T(8,128)(2,1)} %refs_1_.29, bf16[2,4,256,256]{3,2,1,0:T(8,128)(2,1)} %get-tuple-element.181.refs_2_, bf16[2,4,256,256]{3,2,1,0:T(8,128)(2,1)} %collective-permute-done.67.refs_3_, ...), custom_call_target="tpu_custom_call" | custom-call | flops 4294967296 | bytes 23068672 | tf_op jit(solution)/shard_map/pallas_call | solution.py:48
  827.8 12.4 %all-to-all-start.3 = ((bf16[16,2,2,128,256]{4,3,2,1,0:T(8,128)(2,1)}), bf16[16,2,2,128,256]{4,3,2,1,0:T(8,128)(2,1)}, u32[]{:S(2)}, u32[]{:S(2)}) async-start(bf16[16,2,2,128,256]{4,3,2,1,0:T(8,128)(2,1)} %shard_map.64), calls=%async_computation.3 | async-start | bytes 8388608 | tf_op jit(solution)/shard_map/all_to_all | solution.py:400
  845.2 8.5 collective-permute-done.51.refs_3_
  857.2 11.7 %collective-permute-done.70.refs_2_ = bf16[1,2,128,256]{3,2,1,0:T(8,128)(2,1)} collective-permute-done((bf16[1,2,128,256]{3,2,1,0:T(8,128)(2,1)S(1)}, bf16[1,2,128,256]{3,2,1,0:T(8,128)(2,1)}, u32[]{:S(2)}, u32[]{:S(2)}) %collective-permute-start.70) | collective-permute-done | bytes 131104 | tf_op jit(solution)/shard_map/ppermute | solution.py:395
  873.3 37.9 %collective-permute-done.72.refs_4_ = bf16[1,2,128,256]{3,2,1,0:T(8,128)(2,1)} collective-permute-done((bf16[1,2,128,256]{3,2,1,0:T(8,128)(2,1)S(1)}, bf16[1,2,128,256]{3,2,1,0:T(8,128)(2,1)}, u32[]{:S(2)}, u32[]{:S(2)}) %collective-permute-start.72) | collective-permute-done | bytes 131104 | tf_op jit(solution)/shard_map/ppermute | solution.py:395
  911.2 5.3 collective-permute-start.77
  920.0 5.7 collective-permute-start.79
  925.8 7.9 shard_map.62
  933.8 16.6 %collective-permute-done.76.refs_8_ = bf16[1,2,128,256]{3,2,1,0:T(8,128)(2,1)} collective-permute-done((bf16[1,2,128,256]{3,2,1,0:T(8,128)(2,1)}, bf16[1,2,128,256]{3,2,1,0:T(8,128)(2,1)}, u32[]{:S(2)}, u32[]{:S(2)}) %collective-permute-start.76) | collective-permute-done | bytes 131104 | tf_op jit(solution)/shard_map/ppermute | solution.py:395
  950.3 4.8 collective-permute-start.81
  959.7 7.6 collective-permute-start.83
  967.3 19.3 %shard_map.65.refs_16_ = f32[4,2,1024,256]{3,2,1,0:T(8,128)} custom-call(s32[2]{0:T(128)} %pad_add_fusion.pos.refs_0_, bf16[4,2,1024,2048]{3,2,1,0:T(8,128)(2,1)} %refs_0_.1, bf16[16,4,2,128,256]{4,3,2,1,0:T(8,128)(2,1)} %all-to-all-done.2.refs_4_.refs_2_, bf16[1,2,128,256]{3,2,1,0:T(8,128)(2,1)} %get-tuple-element.169.refs_3_.refs_4_), custom_call_target="tpu_custom_call" | custom-call | flops 8589934592 | bytes 46137344 | tf_op jit(solution)/shard_map/pallas_call | solution.py:48
  990.1 6.7 shard_map.66.refs_1_
  1007.9 11.0 %shard_map.67.refs_16_.refs_6_ = f32[4,2,1024,256]{3,2,1,0:T(8,128)} custom-call(s32[2]{0:T(128)} %pad_add_fusion.pos.refs_0_, bf16[4,2,1024,2048]{3,2,1,0:T(8,128)(2,1)} %refs_0_.1, bf16[16,2,2,128,256]{4,3,2,1,0:T(8,128)(2,1)} %all-to-all-done.3.refs_0_, f32[4,2,1024,256]{3,2,1,0:T(8,128)} %shard_map.66.refs_1_), custom_call_target="tpu_custom_call", output_to_operand_aliasing={{}: (3, {})} | custom-call | flops 4294967296 | bytes 23068672 | tf_op jit(solution)/shard_map/pallas_call | solution.py:322
  1021.1 13.2 %collective-permute-start.55 = (bf16[1,2,128,256]{3,2,1,0:T(8,128)(2,1)}, bf16[1,2,128,256]{3,2,1,0:T(8,128)(2,1)}, u32[]{:S(2)}, u32[]{:S(2)}) collective-permute-start(bf16[1,2,128,256]{3,2,1,0:T(8,128)(2,1)} %get-tuple-element.168), channel_id=1, source_target_pairs={{0,22},{2,20},{4,18},{6,16},{8,30},{10,28},{12,26},{14,24},{16,6},... | collective-permute-start | bytes 393224 | tf_op jit(solution)/shard_map/ppermute | solution.py:395
  1034.4 5.7 shard_map.68.refs_5_
  (191 shorter events, 161.3 us)
Async XLA Ops:
  22.0 85.5 %all-to-all-start.1 = ((bf16[16,2,4,64,256]{4,3,2,1,0:T(8,128)(2,1)}), bf16[16,2,4,64,256]{4,3,2,1,0:T(8,128)(2,1)}, u32[]{:S(2)}, u32[]{:S(2)}) async-start(bf16[16,2,4,64,256]{4,3,2,1,0:T(8,128)(2,1)} %shard_map.48.refs_3_), calls=%async_computation.1 | async-start | bytes 8388608 | tf_op jit(solution)/shard_map/all_to_all | solution.py:400
  107.5 393.1 %all-to-all-start = ((bf16[16,3,4,64,256]{4,3,2,1,0:T(8,128)(2,1)}), bf16[16,3,4,64,256]{4,3,2,1,0:T(8,128)(2,1)}, u32[]{:S(2)}, u32[]{:S(2)}) async-start(bf16[16,3,4,64,256]{4,3,2,1,0:T(8,128)(2,1)} %shard_map.52.refs_3_), calls=%async_computation | async-start | bytes 12582912 | tf_op jit(solution)/shard_map/all_to_all | solution.py:400
  126.6 109.4 %collective-permute-start.12 = (bf16[1,4,64,256]{3,2,1,0:T(8,128)(2,1)S(1)}, bf16[1,4,64,256]{3,2,1,0:T(8,128)(2,1)}, u32[]{:S(2)}, u32[]{:S(2)}) collective-permute-start(bf16[1,4,64,256]{3,2,1,0:T(8,128)(2,1)S(1)} %copy-done.14), channel_id=1, source_target_pairs={{0,26},{2,24},{4,30},{6,28},{8,18},{10,16},{12,22},{14,20},{16,10}... | collective-permute-start | bytes 393224 | tf_op jit(solution)/shard_map/ppermute | solution.py:395
  130.1 153.5 %collective-permute-start.13 = (bf16[1,4,64,256]{3,2,1,0:T(8,128)(2,1)S(1)}, bf16[1,4,64,256]{3,2,1,0:T(8,128)(2,1)}, u32[]{:S(2)}, u32[]{:S(2)}) collective-permute-start(bf16[1,4,64,256]{3,2,1,0:T(8,128)(2,1)S(1)} %copy-done.12), channel_id=1, source_target_pairs={{0,28},{2,30},{4,24},{6,26},{8,20},{10,22},{12,16},{14,18},{16,12}... | collective-permute-start | bytes 393224 | tf_op jit(solution)/shard_map/ppermute | solution.py:395
  131.3 155.7 %collective-permute-start.14 = (bf16[1,4,64,256]{3,2,1,0:T(8,128)(2,1)S(1)}, bf16[1,4,64,256]{3,2,1,0:T(8,128)(2,1)}, u32[]{:S(2)}, u32[]{:S(2)}) collective-permute-start(bf16[1,4,64,256]{3,2,1,0:T(8,128)(2,1)S(1)} %copy-done.10), channel_id=1, source_target_pairs={{0,30},{2,28},{4,26},{6,24},{8,22},{10,20},{12,18},{14,16},{16,14}... | collective-permute-start | bytes 393224 | tf_op jit(solution)/shard_map/ppermute | solution.py:395
  134.5 160.3 %collective-permute-start.11 = (bf16[1,4,64,256]{3,2,1,0:T(8,128)(2,1)S(1)}, bf16[1,4,64,256]{3,2,1,0:T(8,128)(2,1)}, u32[]{:S(2)}, u32[]{:S(2)}) collective-permute-start(bf16[1,4,64,256]{3,2,1,0:T(8,128)(2,1)S(1)} %copy-done.1), channel_id=1, source_target_pairs={{0,24},{2,26},{4,28},{6,30},{8,16},{10,18},{12,20},{14,22},{16,8},... | collective-permute-start | bytes 393224 | tf_op jit(solution)/shard_map/ppermute | solution.py:395
  134.6 167.5 %collective-permute-start.8 = (bf16[1,4,64,256]{3,2,1,0:T(8,128)(2,1)S(1)}, bf16[1,4,64,256]{3,2,1,0:T(8,128)(2,1)}, u32[]{:S(2)}, u32[]{:S(2)}) collective-permute-start(bf16[1,4,64,256]{3,2,1,0:T(8,128)(2,1)S(1)} %copy-done.7), channel_id=1, source_target_pairs={{0,18},{2,16},{4,22},{6,20},{8,26},{10,24},{12,30},{14,28},{16,2},... | collective-permute-start | bytes 393224 | tf_op jit(solution)/shard_map/ppermute | solution.py:395
  236.0 69.0 %collective-permute-start.9 = (bf16[1,4,64,256]{3,2,1,0:T(8,128)(2,1)S(1)}, bf16[1,4,64,256]{3,2,1,0:T(8,128)(2,1)}, u32[]{:S(2)}, u32[]{:S(2)}) collective-permute-start(bf16[1,4,64,256]{3,2,1,0:T(8,128)(2,1)S(1)} %copy-done.6), channel_id=1, source_target_pairs={{0,20},{2,22},{4,16},{6,18},{8,28},{10,30},{12,24},{14,26},{16,4},... | collective-permute-start | bytes 393224 | tf_op jit(solution)/shard_map/ppermute | solution.py:395
  283.6 25.2 %collective-permute-start.10 = (bf16[1,4,64,256]{3,2,1,0:T(8,128)(2,1)S(1)}, bf16[1,4,64,256]{3,2,1,0:T(8,128)(2,1)}, u32[]{:S(2)}, u32[]{:S(2)}) collective-permute-start(bf16[1,4,64,256]{3,2,1,0:T(8,128)(2,1)S(1)} %copy-done.5), channel_id=1, source_target_pairs={{0,22},{2,20},{4,18},{6,16},{8,30},{10,28},{12,26},{14,24},{16,6},... | collective-permute-start | bytes 393224 | tf_op jit(solution)/shard_map/ppermute | solution.py:395
  325.1 25.3 %collective-permute-start.19 = (bf16[1,4,64,256]{3,2,1,0:T(8,128)(2,1)}, bf16[1,4,64,256]{3,2,1,0:T(8,128)(2,1)}, u32[]{:S(2)}, u32[]{:S(2)}) collective-permute-start(bf16[1,4,64,256]{3,2,1,0:T(8,128)(2,1)} %get-tuple-element.127), channel_id=1, source_target_pairs={{0,6},{2,4},{4,2},{6,0},{8,14},{10,12},{12,10},{14,8},{16,22},{18,... | collective-permute-start | bytes 393224 | tf_op jit(solution)/shard_map/ppermute | solution.py:395
  325.9 25.8 %collective-permute-start.20 = (bf16[1,4,64,256]{3,2,1,0:T(8,128)(2,1)}, bf16[1,4,64,256]{3,2,1,0:T(8,128)(2,1)}, u32[]{:S(2)}, u32[]{:S(2)}) collective-permute-start(bf16[1,4,64,256]{3,2,1,0:T(8,128)(2,1)} %get-tuple-element.128), channel_id=1, source_target_pairs={{0,8},{2,10},{4,12},{6,14},{8,0},{10,2},{12,4},{14,6},{16,24},{18,... | collective-permute-start | bytes 393224 | tf_op jit(solution)/shard_map/ppermute | solution.py:395
  325.9 25.9 %collective-permute-start.21 = (bf16[1,4,64,256]{3,2,1,0:T(8,128)(2,1)}, bf16[1,4,64,256]{3,2,1,0:T(8,128)(2,1)}, u32[]{:S(2)}, u32[]{:S(2)}) collective-permute-start(bf16[1,4,64,256]{3,2,1,0:T(8,128)(2,1)} %get-tuple-element.129), channel_id=1, source_target_pairs={{0,10},{2,8},{4,14},{6,12},{8,2},{10,0},{12,6},{14,4},{16,26},{18,... | collective-permute-start | bytes 393224 | tf_op jit(solution)/shard_map/ppermute | solution.py:395
  350.5 63.4 %collective-permute-start.16 = (bf16[2,4,256,256]{3,2,1,0:T(8,128)(2,1)}, bf16[2,4,256,256]{3,2,1,0:T(8,128)(2,1)}, u32[]{:S(2)}, u32[]{:S(2)}) collective-permute-start(bf16[2,4,256,256]{3,2,1,0:T(8,128)(2,1)} %get-tuple-element.124), channel_id=1, source_target_pairs={{0,1},{1,0},{2,3},{3,2},{4,5},{5,4},{6,7},{7,6},{8,9},{9,8},{10,11... | collective-permute-start | bytes 3145736 | tf_op jit(solution)/shard_map/ppermute | solution.py:395
  354.6 27.1 %collective-permute-start.26 = (bf16[1,4,64,256]{3,2,1,0:T(8,128)(2,1)}, bf16[1,4,64,256]{3,2,1,0:T(8,128)(2,1)}, u32[]{:S(2)}, u32[]{:S(2)}) collective-permute-start(bf16[1,4,64,256]{3,2,1,0:T(8,128)(2,1)} %get-tuple-element.134), channel_id=1, source_target_pairs={{0,20},{2,22},{4,16},{6,18},{8,28},{10,30},{12,24},{14,26},{16,4},... | collective-permute-start | bytes 393224 | tf_op jit(solution)/shard_map/ppermute | solution.py:395
  355.3 29.2 %collective-permute-start.27 = (bf16[1,4,64,256]{3,2,1,0:T(8,128)(2,1)}, bf16[1,4,64,256]{3,2,1,0:T(8,128)(2,1)}, u32[]{:S(2)}, u32[]{:S(2)}) collective-permute-start(bf16[1,4,64,256]{3,2,1,0:T(8,128)(2,1)} %get-tuple-element.135), channel_id=1, source_target_pairs={{0,22},{2,20},{4,18},{6,16},{8,30},{10,28},{12,26},{14,24},{16,6},... | collective-permute-start | bytes 393224 | tf_op jit(solution)/shard_map/ppermute | solution.py:395
  429.8 46.3 %collective-permute-start.33 = (bf16[4,4,256,256]{3,2,1,0:T(8,128)(2,1)}, bf16[4,4,256,256]{3,2,1,0:T(8,128)(2,1)}, u32[]{:S(2)}, u32[]{:S(2)}) collective-permute-start(bf16[4,4,256,256]{3,2,1,0:T(8,128)(2,1)} %get-tuple-element.143), channel_id=1, source_target_pairs={{0,1},{1,0},{2,3},{3,2},{4,5},{5,4},{6,7},{7,6},{8,9},{9,8},{10,11... | collective-permute-start | bytes 6291464 | tf_op jit(solution)/shard_map/ppermute | solution.py:395
  500.6 327.2 %all-to-all-start.2 = ((bf16[16,4,2,128,256]{4,3,2,1,0:T(8,128)(2,1)}), bf16[16,4,2,128,256]{4,3,2,1,0:T(8,128)(2,1)}, u32[]{:S(2)}, u32[]{:S(2)}) async-start(bf16[16,4,2,128,256]{4,3,2,1,0:T(8,128)(2,1)} %shard_map.58.refs_3_), calls=%async_computation.2 | async-start | bytes 16777216 | tf_op jit(solution)/shard_map/all_to_all | solution.py:400
  531.0 224.4 %collective-permute-start.34 = (bf16[3,4,256,256]{3,2,1,0:T(8,128)(2,1)}, bf16[3,4,256,256]{3,2,1,0:T(8,128)(2,1)}, u32[]{:S(2)}, u32[]{:S(2)}) collective-permute-start(bf16[3,4,256,256]{3,2,1,0:T(8,128)(2,1)} %get-tuple-element.145), channel_id=1, source_target_pairs={{0,1},{1,0},{2,3},{3,2},{4,5},{5,4},{6,7},{7,6},{8,9},{9,8},{10,11... | collective-permute-start | bytes 4718600 | tf_op jit(solution)/shard_map/ppermute | solution.py:395
  531.7 32.3 %collective-permute-start.36 = (bf16[1,4,64,256]{3,2,1,0:T(8,128)(2,1)}, bf16[1,4,64,256]{3,2,1,0:T(8,128)(2,1)}, u32[]{:S(2)}, u32[]{:S(2)}) collective-permute-start(bf16[1,4,64,256]{3,2,1,0:T(8,128)(2,1)} %get-tuple-element.147), channel_id=1, source_target_pairs={{0,4},{2,6},{4,0},{6,2},{8,12},{10,14},{12,8},{14,10},{16,20},{18,... | collective-permute-start | bytes 393224 | tf_op jit(solution)/shard_map/ppermute | solution.py:395
  533.3 34.1 %collective-permute-start.37 = (bf16[1,4,64,256]{3,2,1,0:T(8,128)(2,1)}, bf16[1,4,64,256]{3,2,1,0:T(8,128)(2,1)}, u32[]{:S(2)}, u32[]{:S(2)}) collective-permute-start(bf16[1,4,64,256]{3,2,1,0:T(8,128)(2,1)} %get-tuple-element.148), channel_id=1, source_target_pairs={{0,6},{2,4},{4,2},{6,0},{8,14},{10,12},{12,10},{14,8},{16,22},{18,... | collective-permute-start | bytes 393224 | tf_op jit(solution)/shard_map/ppermute | solution.py:395
  533.4 118.0 %collective-permute-start.38 = (bf16[1,4,64,256]{3,2,1,0:T(8,128)(2,1)}, bf16[1,4,64,256]{3,2,1,0:T(8,128)(2,1)}, u32[]{:S(2)}, u32[]{:S(2)}) collective-permute-start(bf16[1,4,64,256]{3,2,1,0:T(8,128)(2,1)} %get-tuple-element.149), channel_id=1, source_target_pairs={{0,8},{2,10},{4,12},{6,14},{8,0},{10,2},{12,4},{14,6},{16,24},{18,... | collective-permute-start | bytes 393224 | tf_op jit(solution)/shard_map/ppermute | solution.py:395
  536.3 118.9 %collective-permute-start.39 = (bf16[1,4,64,256]{3,2,1,0:T(8,128)(2,1)}, bf16[1,4,64,256]{3,2,1,0:T(8,128)(2,1)}, u32[]{:S(2)}, u32[]{:S(2)}) collective-permute-start(bf16[1,4,64,256]{3,2,1,0:T(8,128)(2,1)} %get-tuple-element.150), channel_id=1, source_target_pairs={{0,10},{2,8},{4,14},{6,12},{8,2},{10,0},{12,6},{14,4},{16,26},{18,... | collective-permute-start | bytes 393224 | tf_op jit(solution)/shard_map/ppermute | solution.py:395
  564.0 94.3 %collective-permute-start.40 = (bf16[1,4,64,256]{3,2,1,0:T(8,128)(2,1)}, bf16[1,4,64,256]{3,2,1,0:T(8,128)(2,1)}, u32[]{:S(2)}, u32[]{:S(2)}) collective-permute-start(bf16[1,4,64,256]{3,2,1,0:T(8,128)(2,1)} %get-tuple-element.151), channel_id=1, source_target_pairs={{0,12},{2,14},{4,8},{6,10},{8,4},{10,6},{12,0},{14,2},{16,28},{18,... | collective-permute-start | bytes 393224 | tf_op jit(solution)/shard_map/ppermute | solution.py:395
  567.4 94.3 %collective-permute-start.41 = (bf16[1,4,64,256]{3,2,1,0:T(8,128)(2,1)}, bf16[1,4,64,256]{3,2,1,0:T(8,128)(2,1)}, u32[]{:S(2)}, u32[]{:S(2)}) collective-permute-start(bf16[1,4,64,256]{3,2,1,0:T(8,128)(2,1)} %get-tuple-element.152), channel_id=1, source_target_pairs={{0,14},{2,12},{4,10},{6,8},{8,6},{10,4},{12,2},{14,0},{16,30},{18,... | collective-permute-start | bytes 393224 | tf_op jit(solution)/shard_map/ppermute | solution.py:395
  651.4 58.5 %collective-permute-start.42 = (bf16[1,4,64,256]{3,2,1,0:T(8,128)(2,1)}, bf16[1,4,64,256]{3,2,1,0:T(8,128)(2,1)}, u32[]{:S(2)}, u32[]{:S(2)}) collective-permute-start(bf16[1,4,64,256]{3,2,1,0:T(8,128)(2,1)} %get-tuple-element.153), channel_id=1, source_target_pairs={{0,16},{2,18},{4,20},{6,22},{8,24},{10,26},{12,28},{14,30},{16,0},... | collective-permute-start | bytes 393224 | tf_op jit(solution)/shard_map/ppermute | solution.py:395
  655.2 58.8 %collective-permute-start.43 = (bf16[1,4,64,256]{3,2,1,0:T(8,128)(2,1)}, bf16[1,4,64,256]{3,2,1,0:T(8,128)(2,1)}, u32[]{:S(2)}, u32[]{:S(2)}) collective-permute-start(bf16[1,4,64,256]{3,2,1,0:T(8,128)(2,1)} %get-tuple-element.154), channel_id=1, source_target_pairs={{0,18},{2,16},{4,22},{6,20},{8,26},{10,24},{12,30},{14,28},{16,2},... | collective-permute-start | bytes 393224 | tf_op jit(solution)/shard_map/ppermute | solution.py:395
  658.3 63.9 %collective-permute-start.44 = (bf16[1,4,64,256]{3,2,1,0:T(8,128)(2,1)}, bf16[1,4,64,256]{3,2,1,0:T(8,128)(2,1)}, u32[]{:S(2)}, u32[]{:S(2)}) collective-permute-start(bf16[1,4,64,256]{3,2,1,0:T(8,128)(2,1)} %get-tuple-element.155), channel_id=1, source_target_pairs={{0,20},{2,22},{4,16},{6,18},{8,28},{10,30},{12,24},{14,26},{16,4},... | collective-permute-start | bytes 393224 | tf_op jit(solution)/shard_map/ppermute | solution.py:395
  661.7 64.2 %collective-permute-start.45 = (bf16[1,4,64,256]{3,2,1,0:T(8,128)(2,1)}, bf16[1,4,64,256]{3,2,1,0:T(8,128)(2,1)}, u32[]{:S(2)}, u32[]{:S(2)}) collective-permute-start(bf16[1,4,64,256]{3,2,1,0:T(8,128)(2,1)} %get-tuple-element.156), channel_id=1, source_target_pairs={{0,22},{2,20},{4,18},{6,16},{8,30},{10,28},{12,26},{14,24},{16,6},... | collective-permute-start | bytes 393224 | tf_op jit(solution)/shard_map/ppermute | solution.py:395
  771.4 43.0 %collective-permute-start.67 = (bf16[2,4,256,256]{3,2,1,0:T(8,128)(2,1)}, bf16[2,4,256,256]{3,2,1,0:T(8,128)(2,1)}, u32[]{:S(2)}, u32[]{:S(2)}) collective-permute-start(bf16[2,4,256,256]{3,2,1,0:T(8,128)(2,1)} %get-tuple-element.182), channel_id=1, source_target_pairs={{0,1},{1,0},{2,3},{3,2},{4,5},{5,4},{6,7},{7,6},{8,9},{9,8},{10,11... | collective-permute-start | bytes 3145736 | tf_op jit(solution)/shard_map/ppermute | solution.py:395
  771.7 34.7 %collective-permute-start.68 = (bf16[1,4,256,256]{3,2,1,0:T(8,128)(2,1)}, bf16[1,4,256,256]{3,2,1,0:T(8,128)(2,1)}, u32[]{:S(2)}, u32[]{:S(2)}) collective-permute-start(bf16[1,4,256,256]{3,2,1,0:T(8,128)(2,1)} %get-tuple-element.184), channel_id=1, source_target_pairs={{0,1},{1,0},{2,3},{3,2},{4,5},{5,4},{6,7},{7,6},{8,9},{9,8},{10,11... | collective-permute-start | bytes 1572872 | tf_op jit(solution)/shard_map/ppermute | solution.py:395
  827.8 180.1 %all-to-all-start.3 = ((bf16[16,2,2,128,256]{4,3,2,1,0:T(8,128)(2,1)}), bf16[16,2,2,128,256]{4,3,2,1,0:T(8,128)(2,1)}, u32[]{:S(2)}, u32[]{:S(2)}) async-start(bf16[16,2,2,128,256]{4,3,2,1,0:T(8,128)(2,1)} %shard_map.64), calls=%async_computation.3 | async-start | bytes 8388608 | tf_op jit(solution)/shard_map/all_to_all | solution.py:400
  841.0 27.8 %collective-permute-start.70 = (bf16[1,2,128,256]{3,2,1,0:T(8,128)(2,1)S(1)}, bf16[1,2,128,256]{3,2,1,0:T(8,128)(2,1)}, u32[]{:S(2)}, u32[]{:S(2)}) collective-permute-start(bf16[1,2,128,256]{3,2,1,0:T(8,128)(2,1)S(1)} %copy-done.15), channel_id=1, source_target_pairs={{0,4},{2,6},{4,0},{6,2},{8,12},{10,14},{12,8},{14,10},{16,20},{18,... | collective-permute-start | bytes 393224 | tf_op jit(solution)/shard_map/ppermute | solution.py:395
  842.6 29.6 %collective-permute-start.71 = (bf16[1,2,128,256]{3,2,1,0:T(8,128)(2,1)S(1)}, bf16[1,2,128,256]{3,2,1,0:T(8,128)(2,1)}, u32[]{:S(2)}, u32[]{:S(2)}) collective-permute-start(bf16[1,2,128,256]{3,2,1,0:T(8,128)(2,1)S(1)} %copy-done.13), channel_id=1, source_target_pairs={{0,6},{2,4},{4,2},{6,0},{8,14},{10,12},{12,10},{14,8},{16,22},{18,... | collective-permute-start | bytes 393224 | tf_op jit(solution)/shard_map/ppermute | solution.py:395
  842.7 68.5 %collective-permute-start.72 = (bf16[1,2,128,256]{3,2,1,0:T(8,128)(2,1)S(1)}, bf16[1,2,128,256]{3,2,1,0:T(8,128)(2,1)}, u32[]{:S(2)}, u32[]{:S(2)}) collective-permute-start(bf16[1,2,128,256]{3,2,1,0:T(8,128)(2,1)S(1)} %copy-done.11), channel_id=1, source_target_pairs={{0,8},{2,10},{4,12},{6,14},{8,0},{10,2},{12,4},{14,6},{16,24},{18,... | collective-permute-start | bytes 393224 | tf_op jit(solution)/shard_map/ppermute | solution.py:395
  853.7 62.8 %collective-permute-start.73 = (bf16[1,2,128,256]{3,2,1,0:T(8,128)(2,1)S(1)}, bf16[1,2,128,256]{3,2,1,0:T(8,128)(2,1)}, u32[]{:S(2)}, u32[]{:S(2)}) collective-permute-start(bf16[1,2,128,256]{3,2,1,0:T(8,128)(2,1)S(1)} %copy-done.9), channel_id=1, source_target_pairs={{0,10},{2,8},{4,14},{6,12},{8,2},{10,0},{12,6},{14,4},{16,26},{18,... | collective-permute-start | bytes 393224 | tf_op jit(solution)/shard_map/ppermute | solution.py:395
  856.0 64.1 %collective-permute-start.74 = (bf16[1,2,128,256]{3,2,1,0:T(8,128)(2,1)S(1)}, bf16[1,2,128,256]{3,2,1,0:T(8,128)(2,1)}, u32[]{:S(2)}, u32[]{:S(2)}) collective-permute-start(bf16[1,2,128,256]{3,2,1,0:T(8,128)(2,1)S(1)} %copy-done.8), channel_id=1, source_target_pairs={{0,12},{2,14},{4,8},{6,10},{8,4},{10,6},{12,0},{14,2},{16,28},{18,... | collective-permute-start | bytes 393224 | tf_op jit(solution)/shard_map/ppermute | solution.py:395
  868.8 64.9 %collective-permute-start.75 = (bf16[1,2,128,256]{3,2,1,0:T(8,128)(2,1)}, bf16[1,2,128,256]{3,2,1,0:T(8,128)(2,1)}, u32[]{:S(2)}, u32[]{:S(2)}) collective-permute-start(bf16[1,2,128,256]{3,2,1,0:T(8,128)(2,1)} %get-tuple-element.192), channel_id=1, source_target_pairs={{0,14},{2,12},{4,10},{6,8},{8,6},{10,4},{12,2},{14,0},{16,30},{18,... | collective-permute-start | bytes 393224 | tf_op jit(solution)/shard_map/ppermute | solution.py:395
  872.2 78.1 %collective-permute-start.76 = (bf16[1,2,128,256]{3,2,1,0:T(8,128)(2,1)}, bf16[1,2,128,256]{3,2,1,0:T(8,128)(2,1)}, u32[]{:S(2)}, u32[]{:S(2)}) collective-permute-start(bf16[1,2,128,256]{3,2,1,0:T(8,128)(2,1)} %get-tuple-element.193), channel_id=1, source_target_pairs={{0,16},{2,18},{4,20},{6,22},{8,24},{10,26},{12,28},{14,30},{16,0},... | collective-permute-start | bytes 393224 | tf_op jit(solution)/shard_map/ppermute | solution.py:395
  911.2 44.0 %collective-permute-start.77 = (bf16[1,2,128,256]{3,2,1,0:T(8,128)(2,1)}, bf16[1,2,128,256]{3,2,1,0:T(8,128)(2,1)}, u32[]{:S(2)}, u32[]{:S(2)}) collective-permute-start(bf16[1,2,128,256]{3,2,1,0:T(8,128)(2,1)} %get-tuple-element.194), channel_id=1, source_target_pairs={{0,18},{2,16},{4,22},{6,20},{8,26},{10,24},{12,30},{14,28},{16,2},... | collective-permute-start | bytes 393224 | tf_op jit(solution)/shard_map/ppermute | solution.py:395
  916.5 43.1 %collective-permute-start.78 = (bf16[1,2,128,256]{3,2,1,0:T(8,128)(2,1)}, bf16[1,2,128,256]{3,2,1,0:T(8,128)(2,1)}, u32[]{:S(2)}, u32[]{:S(2)}) collective-permute-start(bf16[1,2,128,256]{3,2,1,0:T(8,128)(2,1)} %get-tuple-element.195), channel_id=1, source_target_pairs={{0,20},{2,22},{4,16},{6,18},{8,28},{10,30},{12,24},{14,26},{16,4},... | collective-permute-start | bytes 393224 | tf_op jit(solution)/shard_map/ppermute | solution.py:395
  920.0 47.2 %collective-permute-start.79 = (bf16[1,2,128,256]{3,2,1,0:T(8,128)(2,1)}, bf16[1,2,128,256]{3,2,1,0:T(8,128)(2,1)}, u32[]{:S(2)}, u32[]{:S(2)}) collective-permute-start(bf16[1,2,128,256]{3,2,1,0:T(8,128)(2,1)} %get-tuple-element.196), channel_id=1, source_target_pairs={{0,22},{2,20},{4,18},{6,16},{8,30},{10,28},{12,26},{14,24},{16,6},... | collective-permute-start | bytes 393224 | tf_op jit(solution)/shard_map/ppermute | solution.py:395
  933.7 52.8 %collective-permute-start.80 = (bf16[1,2,128,256]{3,2,1,0:T(8,128)(2,1)}, bf16[1,2,128,256]{3,2,1,0:T(8,128)(2,1)}, u32[]{:S(2)}, u32[]{:S(2)}) collective-permute-start(bf16[1,2,128,256]{3,2,1,0:T(8,128)(2,1)} %get-tuple-element.197), channel_id=1, source_target_pairs={{0,24},{2,26},{4,28},{6,30},{8,16},{10,18},{12,20},{14,22},{16,8},... | collective-permute-start | bytes 393224 | tf_op jit(solution)/shard_map/ppermute | solution.py:395
  950.3 36.2 %collective-permute-start.81 = (bf16[1,2,128,256]{3,2,1,0:T(8,128)(2,1)}, bf16[1,2,128,256]{3,2,1,0:T(8,128)(2,1)}, u32[]{:S(2)}, u32[]{:S(2)}) collective-permute-start(bf16[1,2,128,256]{3,2,1,0:T(8,128)(2,1)} %get-tuple-element.198), channel_id=1, source_target_pairs={{0,26},{2,24},{4,30},{6,28},{8,18},{10,16},{12,22},{14,20},{16,10}... | collective-permute-start | bytes 393224 | tf_op jit(solution)/shard_map/ppermute | solution.py:395
  955.1 33.5 %collective-permute-start.82 = (bf16[1,2,128,256]{3,2,1,0:T(8,128)(2,1)}, bf16[1,2,128,256]{3,2,1,0:T(8,128)(2,1)}, u32[]{:S(2)}, u32[]{:S(2)}) collective-permute-start(bf16[1,2,128,256]{3,2,1,0:T(8,128)(2,1)} %get-tuple-element.199), channel_id=1, source_target_pairs={{0,28},{2,30},{4,24},{6,26},{8,20},{10,22},{12,16},{14,18},{16,12}... | collective-permute-start | bytes 393224 | tf_op jit(solution)/shard_map/ppermute | solution.py:395
  959.7 29.0 %collective-permute-start.83 = (bf16[1,2,128,256]{3,2,1,0:T(8,128)(2,1)}, bf16[1,2,128,256]{3,2,1,0:T(8,128)(2,1)}, u32[]{:S(2)}, u32[]{:S(2)}) collective-permute-start(bf16[1,2,128,256]{3,2,1,0:T(8,128)(2,1)} %get-tuple-element.200), channel_id=1, source_target_pairs={{0,30},{2,28},{4,26},{6,24},{8,22},{10,20},{12,18},{14,16},{16,14}... | collective-permute-start | bytes 393224 | tf_op jit(solution)/shard_map/ppermute | solution.py:395
  1005.3 29.1 %collective-permute-start.66 = (bf16[1,2,128,256]{3,2,1,0:T(8,128)(2,1)}, bf16[1,2,128,256]{3,2,1,0:T(8,128)(2,1)}, u32[]{:S(2)}, u32[]{:S(2)}) collective-permute-start(bf16[1,2,128,256]{3,2,1,0:T(8,128)(2,1)} %get-tuple-element.180), channel_id=1, source_target_pairs={{0,30},{2,28},{4,26},{6,24},{8,22},{10,20},{12,18},{14,16},{16,14}... | collective-permute-start | bytes 393224 | tf_op jit(solution)/shard_map/ppermute | solution.py:395
  1018.9 23.1 %collective-permute-start.53 = (bf16[1,2,128,256]{3,2,1,0:T(8,128)(2,1)}, bf16[1,2,128,256]{3,2,1,0:T(8,128)(2,1)}, u32[]{:S(2)}, u32[]{:S(2)}) collective-permute-start(bf16[1,2,128,256]{3,2,1,0:T(8,128)(2,1)} %get-tuple-element.166), channel_id=1, source_target_pairs={{0,18},{2,16},{4,22},{6,20},{8,26},{10,24},{12,30},{14,28},{16,2},... | collective-permute-start | bytes 393224 | tf_op jit(solution)/shard_map/ppermute | solution.py:395
  1021.1 26.0 %collective-permute-start.55 = (bf16[1,2,128,256]{3,2,1,0:T(8,128)(2,1)}, bf16[1,2,128,256]{3,2,1,0:T(8,128)(2,1)}, u32[]{:S(2)}, u32[]{:S(2)}) collective-permute-start(bf16[1,2,128,256]{3,2,1,0:T(8,128)(2,1)} %get-tuple-element.168), channel_id=1, source_target_pairs={{0,22},{2,20},{4,18},{6,16},{8,30},{10,28},{12,26},{14,24},{16,6},... | collective-permute-start | bytes 393224 | tf_op jit(solution)/shard_map/ppermute | solution.py:395
  (57 other events, 2138.5 us)

commit v3 on v2

--- a/solution.py
+++ b/solution.py
@@ -57,9 +57,9 @@
 
 
 def project_kernel(dims, pos, v_ref, w_ref, *refs):
-    groups, col_local, row_local, width, split = dims
+    size, groups, col_local, row_local, width, split = dims
     span = row_local * RANK
-    outs = refs[: groups * GROUP if split else 1]
+    outs = refs[: groups * size if split else 1]
     wave = refs[len(outs)]
 
     @pl.when(pl.program_id(1) == 0)
@@ -76,7 +76,7 @@
         imag = with_real[width:] - with_imag[:width]
         both = jnp.concatenate([real, imag], 0).astype(jnp.bfloat16).T
         if not split:
-            for d in range(GROUP):
+            for d in range(size):
                 for i in range(row_local):
                     start = d * span + i * RANK
                     outs[0][d, 0, i, to] = both[start : start + RANK]
@@ -87,34 +87,34 @@
 
             @pl.when(pl.program_id(1) == high)
             def _():
-                for low in range(GROUP):
-                    base = ((pos[0] % GROUP) ^ low) * span
+                for low in range(size):
+                    base = ((pos[0] % size) ^ low) * span
                     for i in range(row_local):
                         start = pl.multiple_of(base + i * RANK, RANK)
-                        outs[high * GROUP + low][0, i, to] = stage[pl.ds(start, RANK)]
-
-
-def project(pos, col_factors, wavefield, piece, chunk, width, tiles, split, base, groups, after):
+                        outs[high * size + low][0, i, to] = stage[pl.ds(start, RANK)]
+
+
+def project(pos, col_factors, wavefield, piece, chunk, width, tiles, split, size, base, groups, after):
     first, freqs = piece
     _, _, src_rows, cols = col_factors.shape
     col_local = src_rows // TS
     row_local = cols // RANK // tiles
-    lanes = GROUP * row_local * RANK
+    lanes = size * row_local * RANK
     shape = (freqs, row_local, col_local * RANK, 2 * width)
     if split:
-        out_specs = [pl.BlockSpec((1,) + shape[1:], lambda f, g, s: (f, 0, 0, 0))] * (groups * GROUP)
-        out_shape = [jax.ShapeDtypeStruct(shape, jnp.bfloat16)] * (groups * GROUP)
+        out_specs = [pl.BlockSpec((1,) + shape[1:], lambda f, g, s: (f, 0, 0, 0))] * (groups * size)
+        out_shape = [jax.ShapeDtypeStruct(shape, jnp.bfloat16)] * (groups * size)
     else:
-        out_specs = pl.BlockSpec((GROUP, 1) + shape[1:], lambda f, g, s: (g, f, 0, 0, 0))
+        out_specs = pl.BlockSpec((size, 1) + shape[1:], lambda f, g, s: (g, f, 0, 0, 0))
         out_shape = jax.ShapeDtypeStruct((tiles,) + shape, jnp.bfloat16)
     return call(
-        functools.partial(project_kernel, (groups, col_local, row_local, width, split)),
+        functools.partial(project_kernel, (size, groups, col_local, row_local, width, split)),
         (freqs, groups),
         1,
         [
             pl.BlockSpec(
                 (1, 2, src_rows, lanes),
-                lambda f, g, s: (first + f, 0, 0, (s[0] // GROUP) ^ (base + g) if split else g),
+                lambda f, g, s: (first + f, 0, 0, (s[0] // size) ^ (base + g) if split else g),
             ),
             pl.BlockSpec((1, 2, src_rows, width), lambda f, g, s: (first + f, 0, 0, chunk)),
         ],
@@ -430,16 +430,18 @@
     token = None
     groups = tiles // GROUP
     for h in range(CHUNKS):
-        jobs = [(n, 0, groups) for n in range(len(took[h]))]
+        jobs = [(n, GROUP, 0, groups) for n in range(len(took[h]))]
         if h == 0 and took[h][0][2]:
-            near = [(0, base, 1) for base in reversed(range(groups))]
+            near = [(0, GROUP, base, 1) for base in reversed(range(groups))]
             jobs[1:2] = [jobs[1]] + near[groups - groups // 2 :]
-            jobs[:1] = near[: groups - groups // 2]
+            half = GROUP // 2
+            jobs[:1] = [(0, half, 2 * groups - 1, 1), (0, half, 2 * groups - 2, 1)]
+            jobs[2:2] = near[1 : groups - groups // 2]
         made = [[] for _ in took[h]]
-        for n, base, some in jobs:
+        for n, size, base, some in jobs:
             *piece, split = took[h][n]
             part = project(
-                pos, col_factors, wavefield, piece, h, width, tiles, split, base, some, token
+                pos, col_factors, wavefield, piece, h, width, tiles, split, size, base, some, token
             )
             token = part[0] if split else part
             made[n] = [*part, *made[n]] if split else part

time: 1050 us -> 1060 us (level)
    pallas_call x16 -> x17, Pallas kernels: 162 us -> 165 us  [call(): return made if after is None else lambda *args: made(*args, after)]
  transfers between devices with their start and end apart: 88 -> 88, of which waited for: 35 -> 35; matrix products, arithmetic and copies ran while one was open for 0% -> 0% of each run, Pallas kernels for 22% -> 21%
where the time goes in v3:
time: 1060 us; the launch traced here: 1050 us
  waiting for transfers between devices  558 us (53%)
  Pallas kernels  255 us (24%)
  starting transfers between devices  239 us (23%)
    ppermute x84, waiting for transfers between devices, send(): return lax.ppermute(array, axis, [(n, n ^ mask) for n in range(size)])  517 us
    ppermute x84, starting transfers between devices, send(): return lax.ppermute(array, axis, [(n, n ^ mask) for n in range(size)])  188 us
    pallas_call x17, Pallas kernels, call(): return made if after is None else lambda *args: made(*args, after)  165 us
    all_to_all x4, starting transfers between devices, trade(): return [lax.all_to_all(made, 'tile', 0, 0, tiled=True)]  51.1 us
    all_to_all x4, waiting for transfers between devices, trade(): return [lax.all_to_all(made, 'tile', 0, 0, tiled=True)]  41.9 us
    pallas_call x2, Pallas kernels, contract(): call(functools.partial(contract_kernel, (tiles, shares, col_local, both /...  32.4 us
    pallas_call x2, Pallas kernels, window(): call(functools.partial(window_kernel, (shares, took, gave, rows, 16, both...  32 us
  transfers between devices with their start and end apart: 88, of which 35 were waited for; matrix products, arithmetic and copies ran while one was open for 0% of the time, Pallas kernels for 21%

profile of v3, /device:TPU:1, one launch (start us, length us, event | category | flops | bytes accessed | tf_op | source)
XLA Modules:
  0.0 1053.8 jit_solution(12319165832730777078)
XLA Ops:
  11.4 13.3 %shard_map.49.refs_3_ = bf16[16,2,4,64,256]{4,3,2,1,0:T(8,128)(2,1)} custom-call(s32[2]{0:T(128)} %pad_add_fusion.pos.refs_0_, bf16[4,2,1024,2048]{3,2,1,0:T(8,128)(2,1)} %refs_0_.1, bf16[4,2,1024,256]{3,2,1,0:T(8,128)(2,1)} %refs_2_.16, bf16[1,4,64,256]{3,2,1,0:T(8,128)(2,1)} %get-tuple-element.105.refs_3_), custom_call_target="tpu_custom_call" | custom-call | flops 4294967296 | bytes 18874368 | tf_op jit(solution)/shard_map/pallas_call | solution.py:48
  24.7 7.3 all-to-all-start.1
  40.1 9.1 shard_map.52
  49.3 18.9 %shard_map.53.refs_3_ = bf16[16,3,4,64,256]{4,3,2,1,0:T(8,128)(2,1)} custom-call(s32[2]{0:T(128)} %pad_add_fusion.pos.refs_0_, bf16[4,2,1024,2048]{3,2,1,0:T(8,128)(2,1)} %refs_0_.1, bf16[4,2,1024,256]{3,2,1,0:T(8,128)(2,1)} %refs_2_.16, bf16[1,4,64,256]{3,2,1,0:T(8,128)(2,1)} %get-tuple-element.108.refs_3_.refs_2_), custom_call_target="tpu_custom_call" | custom-call | flops 6442450944 | bytes 28311552 | tf_op jit(solution)/shard_map/pallas_call | solution.py:48
  68.2 41.9 %all-to-all-done.1.refs_2_ = bf16[16,2,4,64,256]{4,3,2,1,0:T(8,128)(2,1)} async-done(((bf16[16,2,4,64,256]{4,3,2,1,0:T(8,128)(2,1)}), bf16[16,2,4,64,256]{4,3,2,1,0:T(8,128)(2,1)}, u32[]{:S(2)}, u32[]{:S(2)}) %all-to-all-start.1) | async-done | bytes 4194336 | tf_op jit(solution)/shard_map/all_to_all | solution.py:400
  110.2 19.1 %all-to-all-start = ((bf16[16,3,4,64,256]{4,3,2,1,0:T(8,128)(2,1)}), bf16[16,3,4,64,256]{4,3,2,1,0:T(8,128)(2,1)}, u32[]{:S(2)}, u32[]{:S(2)}) async-start(bf16[16,3,4,64,256]{4,3,2,1,0:T(8,128)(2,1)} %shard_map.53.refs_3_), calls=%async_computation | async-start | bytes 12582912 | tf_op jit(solution)/shard_map/all_to_all | solution.py:400
  137.3 102.1 %collective-permute-done.14.refs_17_ = bf16[1,4,64,256]{3,2,1,0:T(8,128)(2,1)} collective-permute-done((bf16[1,4,64,256]{3,2,1,0:T(8,128)(2,1)S(1)}, bf16[1,4,64,256]{3,2,1,0:T(8,128)(2,1)}, u32[]{:S(2)}, u32[]{:S(2)}) %collective-permute-start.14) | collective-permute-done | bytes 131104 | tf_op jit(solution)/shard_map/ppermute | solution.py:395
  239.4 46.9 %collective-permute-start.9 = (bf16[1,4,64,256]{3,2,1,0:T(8,128)(2,1)S(1)}, bf16[1,4,64,256]{3,2,1,0:T(8,128)(2,1)}, u32[]{:S(2)}, u32[]{:S(2)}) collective-permute-start(bf16[1,4,64,256]{3,2,1,0:T(8,128)(2,1)S(1)} %copy-done.7), channel_id=1, source_target_pairs={{0,20},{2,22},{4,16},{6,18},{8,28},{10,30},{12,24},{14,26},{16,4},... | collective-permute-start | bytes 393224 | tf_op jit(solution)/shard_map/ppermute | solution.py:395
  289.7 6.9 collective-permute-start.7
  300.1 4.9 collective-permute-done.8.refs_11_
  317.3 9.1 shard_map.54
  330.2 7.4 shard_map.55
  340.5 12.7 %shard_map.56 = (bf16[2,4,256,256]{3,2,1,0:T(8,128)(2,1)}, bf16[2,4,256,256]{3,2,1,0:T(8,128)(2,1)}) custom-call(s32[2]{0:T(128)} %pad_add_fusion.pos.refs_0_, bf16[4,2,2048,1024]{3,2,1,0:T(8,128)(2,1)} %refs_1_.31, bf16[16,2,4,64,256]{4,3,2,1,0:T(8,128)(2,1)} %all-to-all-done.1.refs_2_, bf16[1,4,256,256]{3,2,1,0:T(8,128)(2,1)} %get-tuple-element.121.refs_3_.refs_0_), custom_call_target="tpu_custom_call" | custom-call | flops 4294967296 | bytes 23068672 | tf_op jit(solution)/shard_map/pallas_call | solution.py:48
  360.7 11.5 %collective-permute-done.24.refs_10_ = bf16[1,4,64,256]{3,2,1,0:T(8,128)(2,1)} collective-permute-done((bf16[1,4,64,256]{3,2,1,0:T(8,128)(2,1)}, bf16[1,4,64,256]{3,2,1,0:T(8,128)(2,1)}, u32[]{:S(2)}, u32[]{:S(2)}) %collective-permute-start.24) | collective-permute-done | bytes 131104 | tf_op jit(solution)/shard_map/ppermute | solution.py:395
  376.4 8.0 collective-permute-done.26.refs_12_
  395.7 7.4 shard_map.57
  404.2 12.3 %collective-permute-done.32.refs_5_ = bf16[1,4,256,256]{3,2,1,0:T(8,128)(2,1)} collective-permute-done((bf16[1,4,256,256]{3,2,1,0:T(8,128)(2,1)}, bf16[1,4,256,256]{3,2,1,0:T(8,128)(2,1)}, u32[]{:S(2)}, u32[]{:S(2)}) %collective-permute-start.32) | collective-permute-done | bytes 524320 | tf_op jit(solution)/shard_map/ppermute | solution.py:395
  416.5 16.0 %shard_map.58 = (bf16[4,4,256,256]{3,2,1,0:T(8,128)(2,1)}, bf16[4,4,256,256]{3,2,1,0:T(8,128)(2,1)}) custom-call(f32[16,8]{1,0:T(8,128)} %get-tuple-element.202.cosine, f32[16,8]{1,0:T(8,128)} %get-tuple-element.201.sine, s32[1,256]{1,0:T(1,128)} %bitcast.3, bf16[1,4,256,256]{3,2,1,0:T(8,128)(2,1)} %get-tuple-element.121.refs_3_.refs_0_, ...), custom_call_target="tpu_custom_call" | custom-call | flops 67108864 | bytes 8388608 | tf_op jit(solution)/shard_map/pallas_call | solution.py:234
  432.7 46.0 %collective-permute-done.33.refs_1_ = bf16[4,4,256,256]{3,2,1,0:T(8,128)(2,1)} collective-permute-done((bf16[4,4,256,256]{3,2,1,0:T(8,128)(2,1)}, bf16[4,4,256,256]{3,2,1,0:T(8,128)(2,1)}, u32[]{:S(2)}, u32[]{:S(2)}) %collective-permute-start.33) | collective-permute-done | bytes 2097184 | tf_op jit(solution)/shard_map/ppermute | solution.py:395
  478.7 24.5 %shard_map.59.refs_3_ = bf16[16,4,2,128,256]{4,3,2,1,0:T(8,128)(2,1)} custom-call(s32[2]{0:T(128)} %pad_add_fusion.pos.refs_0_, bf16[4,2,2048,1024]{3,2,1,0:T(8,128)(2,1)} %refs_1_.31, bf16[4,4,256,256]{3,2,1,0:T(8,128)(2,1)} %get-tuple-element.142.refs_0_, bf16[4,4,256,256]{3,2,1,0:T(8,128)(2,1)} %collective-permute-done.33.refs_1_), custom_call_target="tpu_custom_call" | custom-call | flops 8589934592 | bytes 46137344 | tf_op jit(solution)/shard_map/pallas_call | solution.py:291
  503.3 12.3 %all-to-all-start.2 = ((bf16[16,4,2,128,256]{4,3,2,1,0:T(8,128)(2,1)}), bf16[16,4,2,128,256]{4,3,2,1,0:T(8,128)(2,1)}, u32[]{:S(2)}, u32[]{:S(2)}) async-start(bf16[16,4,2,128,256]{4,3,2,1,0:T(8,128)(2,1)} %shard_map.59.refs_3_), calls=%async_computation.2 | async-start | bytes 16777216 | tf_op jit(solution)/shard_map/all_to_all | solution.py:400
  515.6 18.2 %shard_map.60 = (bf16[3,4,256,256]{3,2,1,0:T(8,128)(2,1)}, bf16[3,4,256,256]{3,2,1,0:T(8,128)(2,1)}) custom-call(s32[2]{0:T(128)} %pad_add_fusion.pos.refs_0_, bf16[4,2,2048,1024]{3,2,1,0:T(8,128)(2,1)} %refs_1_.31, bf16[16,3,4,64,256]{4,3,2,1,0:T(8,128)(2,1)} %all-to-all-done.refs_2_, bf16[16,4,2,128,256]{4,3,2,1,0:T(8,128)(2,1)} %shard_map.59.refs_3_), custom_call_target="tpu_custom_call" | custom-call | flops 6442450944 | bytes 34603008 | tf_op jit(solution)/shard_map/pallas_call | solution.py:48
  539.1 27.6 %collective-permute-done.36.refs_4_ = bf16[1,4,64,256]{3,2,1,0:T(8,128)(2,1)} collective-permute-done((bf16[1,4,64,256]{3,2,1,0:T(8,128)(2,1)}, bf16[1,4,64,256]{3,2,1,0:T(8,128)(2,1)}, u32[]{:S(2)}, u32[]{:S(2)}) %collective-permute-start.36) | collective-permute-done | bytes 131104 | tf_op jit(solution)/shard_map/ppermute | solution.py:395
  570.7 83.3 %collective-permute-done.38.refs_6_ = bf16[1,4,64,256]{3,2,1,0:T(8,128)(2,1)} collective-permute-done((bf16[1,4,64,256]{3,2,1,0:T(8,128)(2,1)}, bf16[1,4,64,256]{3,2,1,0:T(8,128)(2,1)}, u32[]{:S(2)}, u32[]{:S(2)}) %collective-permute-start.38) | collective-permute-done | bytes 131104 | tf_op jit(solution)/shard_map/ppermute | solution.py:395
  668.4 44.2 %collective-permute-done.42.refs_10_ = bf16[1,4,64,256]{3,2,1,0:T(8,128)(2,1)} collective-permute-done((bf16[1,4,64,256]{3,2,1,0:T(8,128)(2,1)}, bf16[1,4,64,256]{3,2,1,0:T(8,128)(2,1)}, u32[]{:S(2)}, u32[]{:S(2)}) %collective-permute-start.42) | collective-permute-done | bytes 131104 | tf_op jit(solution)/shard_map/ppermute | solution.py:395
  718.0 6.9 collective-permute-done.44.refs_12_
  731.8 5.5 collective-permute-done.49.refs_17_
  737.3 7.4 shard_map.61
  745.0 13.1 %collective-permute-done.50.refs_3_ = bf16[1,4,256,256]{3,2,1,0:T(8,128)(2,1)} collective-permute-done((bf16[1,4,256,256]{3,2,1,0:T(8,128)(2,1)}, bf16[1,4,256,256]{3,2,1,0:T(8,128)(2,1)}, u32[]{:S(2)}, u32[]{:S(2)}) %collective-permute-start.50) | collective-permute-done | bytes 524320 | tf_op jit(solution)/shard_map/ppermute | solution.py:395
  758.1 16.0 %shard_map.62 = (bf16[1,4,256,256]{3,2,1,0:T(8,128)(2,1)}, bf16[1,4,256,256]{3,2,1,0:T(8,128)(2,1)}, bf16[2,4,256,256]{3,2,1,0:T(8,128)(2,1)}, bf16[2,4,256,256]...) custom-call(f32[16,8]{1,0:T(8,128)} %get-tuple-element.202.cosine, ...), custom_call_target="tpu_custom_call" | custom-call | flops 67108864 | bytes 8388608 | tf_op jit(solution)/shard_map/pallas_call | solution.py:234
  775.7 33.5 %collective-permute-done.68.refs_1_ = bf16[1,4,256,256]{3,2,1,0:T(8,128)(2,1)} collective-permute-done((bf16[1,4,256,256]{3,2,1,0:T(8,128)(2,1)}, bf16[1,4,256,256]{3,2,1,0:T(8,128)(2,1)}, u32[]{:S(2)}, u32[]{:S(2)}) %collective-permute-start.68) | collective-permute-done | bytes 524320 | tf_op jit(solution)/shard_map/ppermute | solution.py:395
  809.2 7.9 shard_map.64
  817.1 13.3 %shard_map.65 = bf16[16,2,2,128,256]{4,3,2,1,0:T(8,128)(2,1)} custom-call(s32[2]{0:T(128)} %pad_add_fusion.pos.refs_0_, bf16[4,2,2048,1024]{3,2,1,0:T(8,128)(2,1)} %refs_1_.31, bf16[2,4,256,256]{3,2,1,0:T(8,128)(2,1)} %get-tuple-element.181.refs_2_, bf16[2,4,256,256]{3,2,1,0:T(8,128)(2,1)} %collective-permute-done.67.refs_3_, ...), custom_call_target="tpu_custom_call" | custom-call | flops 4294967296 | bytes 23068672 | tf_op jit(solution)/shard_map/pallas_call | solution.py:48
  830.4 12.4 %all-to-all-start.3 = ((bf16[16,2,2,128,256]{4,3,2,1,0:T(8,128)(2,1)}), bf16[16,2,2,128,256]{4,3,2,1,0:T(8,128)(2,1)}, u32[]{:S(2)}, u32[]{:S(2)}) async-start(bf16[16,2,2,128,256]{4,3,2,1,0:T(8,128)(2,1)} %shard_map.65), calls=%async_computation.3 | async-start | bytes 8388608 | tf_op jit(solution)/shard_map/all_to_all | solution.py:400
  847.9 8.5 collective-permute-done.51.refs_3_
  859.8 11.7 %collective-permute-done.70.refs_2_ = bf16[1,2,128,256]{3,2,1,0:T(8,128)(2,1)} collective-permute-done((bf16[1,2,128,256]{3,2,1,0:T(8,128)(2,1)S(1)}, bf16[1,2,128,256]{3,2,1,0:T(8,128)(2,1)}, u32[]{:S(2)}, u32[]{:S(2)}) %collective-permute-start.70) | collective-permute-done | bytes 131104 | tf_op jit(solution)/shard_map/ppermute | solution.py:395
  875.9 37.9 %collective-permute-done.72.refs_4_ = bf16[1,2,128,256]{3,2,1,0:T(8,128)(2,1)} collective-permute-done((bf16[1,2,128,256]{3,2,1,0:T(8,128)(2,1)S(1)}, bf16[1,2,128,256]{3,2,1,0:T(8,128)(2,1)}, u32[]{:S(2)}, u32[]{:S(2)}) %collective-permute-start.72) | collective-permute-done | bytes 131104 | tf_op jit(solution)/shard_map/ppermute | solution.py:395
  913.8 5.3 collective-permute-start.77
  922.7 5.7 collective-permute-start.79
  928.4 7.9 shard_map.63
  936.4 16.5 %collective-permute-done.76.refs_8_ = bf16[1,2,128,256]{3,2,1,0:T(8,128)(2,1)} collective-permute-done((bf16[1,2,128,256]{3,2,1,0:T(8,128)(2,1)}, bf16[1,2,128,256]{3,2,1,0:T(8,128)(2,1)}, u32[]{:S(2)}, u32[]{:S(2)}) %collective-permute-start.76) | collective-permute-done | bytes 131104 | tf_op jit(solution)/shard_map/ppermute | solution.py:395
  952.9 4.8 collective-permute-start.81
  962.3 7.6 collective-permute-start.83
  969.9 19.3 %shard_map.66.refs_16_ = f32[4,2,1024,256]{3,2,1,0:T(8,128)} custom-call(s32[2]{0:T(128)} %pad_add_fusion.pos.refs_0_, bf16[4,2,1024,2048]{3,2,1,0:T(8,128)(2,1)} %refs_0_.1, bf16[16,4,2,128,256]{4,3,2,1,0:T(8,128)(2,1)} %all-to-all-done.2.refs_4_.refs_2_, bf16[1,2,128,256]{3,2,1,0:T(8,128)(2,1)} %get-tuple-element.169.refs_3_.refs_4_), custom_call_target="tpu_custom_call" | custom-call | flops 8589934592 | bytes 46137344 | tf_op jit(solution)/shard_map/pallas_call | solution.py:48
  992.7 6.7 shard_map.67.refs_1_
  1010.5 11.0 %shard_map.68.refs_16_.refs_6_ = f32[4,2,1024,256]{3,2,1,0:T(8,128)} custom-call(s32[2]{0:T(128)} %pad_add_fusion.pos.refs_0_, bf16[4,2,1024,2048]{3,2,1,0:T(8,128)(2,1)} %refs_0_.1, bf16[16,2,2,128,256]{4,3,2,1,0:T(8,128)(2,1)} %all-to-all-done.3.refs_0_, f32[4,2,1024,256]{3,2,1,0:T(8,128)} %shard_map.67.refs_1_), custom_call_target="tpu_custom_call", output_to_operand_aliasing={{}: (3, {})} | custom-call | flops 4294967296 | bytes 23068672 | tf_op jit(solution)/shard_map/pallas_call | solution.py:322
  1023.8 13.2 %collective-permute-start.55 = (bf16[1,2,128,256]{3,2,1,0:T(8,128)(2,1)}, bf16[1,2,128,256]{3,2,1,0:T(8,128)(2,1)}, u32[]{:S(2)}, u32[]{:S(2)}) collective-permute-start(bf16[1,2,128,256]{3,2,1,0:T(8,128)(2,1)} %get-tuple-element.168), channel_id=1, source_target_pairs={{0,22},{2,20},{4,18},{6,16},{8,30},{10,28},{12,26},{14,24},{16,6},... | collective-permute-start | bytes 393224 | tf_op jit(solution)/shard_map/ppermute | solution.py:395
  1037.0 5.8 shard_map.69.refs_5_
  (192 shorter events, 164.7 us)
Async XLA Ops:
  24.7 85.5 %all-to-all-start.1 = ((bf16[16,2,4,64,256]{4,3,2,1,0:T(8,128)(2,1)}), bf16[16,2,4,64,256]{4,3,2,1,0:T(8,128)(2,1)}, u32[]{:S(2)}, u32[]{:S(2)}) async-start(bf16[16,2,4,64,256]{4,3,2,1,0:T(8,128)(2,1)} %shard_map.49.refs_3_), calls=%async_computation.1 | async-start | bytes 8388608 | tf_op jit(solution)/shard_map/all_to_all | solution.py:400
  110.2 393.1 %all-to-all-start = ((bf16[16,3,4,64,256]{4,3,2,1,0:T(8,128)(2,1)}), bf16[16,3,4,64,256]{4,3,2,1,0:T(8,128)(2,1)}, u32[]{:S(2)}, u32[]{:S(2)}) async-start(bf16[16,3,4,64,256]{4,3,2,1,0:T(8,128)(2,1)} %shard_map.53.refs_3_), calls=%async_computation | async-start | bytes 12582912 | tf_op jit(solution)/shard_map/all_to_all | solution.py:400
  129.3 110.1 %collective-permute-start.14 = (bf16[1,4,64,256]{3,2,1,0:T(8,128)(2,1)S(1)}, bf16[1,4,64,256]{3,2,1,0:T(8,128)(2,1)}, u32[]{:S(2)}, u32[]{:S(2)}) collective-permute-start(bf16[1,4,64,256]{3,2,1,0:T(8,128)(2,1)S(1)} %copy-done.14), channel_id=1, source_target_pairs={{0,30},{2,28},{4,26},{6,24},{8,22},{10,20},{12,18},{14,16},{16,14}... | collective-permute-start | bytes 393224 | tf_op jit(solution)/shard_map/ppermute | solution.py:395
  133.7 152.6 %collective-permute-start.13 = (bf16[1,4,64,256]{3,2,1,0:T(8,128)(2,1)S(1)}, bf16[1,4,64,256]{3,2,1,0:T(8,128)(2,1)}, u32[]{:S(2)}, u32[]{:S(2)}) collective-permute-start(bf16[1,4,64,256]{3,2,1,0:T(8,128)(2,1)S(1)} %copy-done.2), channel_id=1, source_target_pairs={{0,28},{2,30},{4,24},{6,26},{8,20},{10,22},{12,16},{14,18},{16,12}... | collective-permute-start | bytes 393224 | tf_op jit(solution)/shard_map/ppermute | solution.py:395
  133.7 156.0 %collective-permute-start.12 = (bf16[1,4,64,256]{3,2,1,0:T(8,128)(2,1)S(1)}, bf16[1,4,64,256]{3,2,1,0:T(8,128)(2,1)}, u32[]{:S(2)}, u32[]{:S(2)}) collective-permute-start(bf16[1,4,64,256]{3,2,1,0:T(8,128)(2,1)S(1)} %copy-done.11), channel_id=1, source_target_pairs={{0,26},{2,24},{4,30},{6,28},{8,18},{10,16},{12,22},{14,20},{16,10}... | collective-permute-start | bytes 393224 | tf_op jit(solution)/shard_map/ppermute | solution.py:395
  137.2 159.4 %collective-permute-start.11 = (bf16[1,4,64,256]{3,2,1,0:T(8,128)(2,1)S(1)}, bf16[1,4,64,256]{3,2,1,0:T(8,128)(2,1)}, u32[]{:S(2)}, u32[]{:S(2)}) collective-permute-start(bf16[1,4,64,256]{3,2,1,0:T(8,128)(2,1)S(1)} %copy-done.1), channel_id=1, source_target_pairs={{0,24},{2,26},{4,28},{6,30},{8,16},{10,18},{12,20},{14,22},{16,8},... | collective-permute-start | bytes 393224 | tf_op jit(solution)/shard_map/ppermute | solution.py:395
  137.3 167.6 %collective-permute-start.8 = (bf16[1,4,64,256]{3,2,1,0:T(8,128)(2,1)S(1)}, bf16[1,4,64,256]{3,2,1,0:T(8,128)(2,1)}, u32[]{:S(2)}, u32[]{:S(2)}) collective-permute-start(bf16[1,4,64,256]{3,2,1,0:T(8,128)(2,1)S(1)} %copy-done.8), channel_id=1, source_target_pairs={{0,18},{2,16},{4,22},{6,20},{8,26},{10,24},{12,30},{14,28},{16,2},... | collective-permute-start | bytes 393224 | tf_op jit(solution)/shard_map/ppermute | solution.py:395
  239.4 68.3 %collective-permute-start.9 = (bf16[1,4,64,256]{3,2,1,0:T(8,128)(2,1)S(1)}, bf16[1,4,64,256]{3,2,1,0:T(8,128)(2,1)}, u32[]{:S(2)}, u32[]{:S(2)}) collective-permute-start(bf16[1,4,64,256]{3,2,1,0:T(8,128)(2,1)S(1)} %copy-done.7), channel_id=1, source_target_pairs={{0,20},{2,22},{4,16},{6,18},{8,28},{10,30},{12,24},{14,26},{16,4},... | collective-permute-start | bytes 393224 | tf_op jit(solution)/shard_map/ppermute | solution.py:395
  286.3 25.1 %collective-permute-start.10 = (bf16[1,4,64,256]{3,2,1,0:T(8,128)(2,1)S(1)}, bf16[1,4,64,256]{3,2,1,0:T(8,128)(2,1)}, u32[]{:S(2)}, u32[]{:S(2)}) collective-permute-start(bf16[1,4,64,256]{3,2,1,0:T(8,128)(2,1)S(1)} %copy-done.6), channel_id=1, source_target_pairs={{0,22},{2,20},{4,18},{6,16},{8,30},{10,28},{12,26},{14,24},{16,6},... | collective-permute-start | bytes 393224 | tf_op jit(solution)/shard_map/ppermute | solution.py:395
  327.8 25.4 %collective-permute-start.19 = (bf16[1,4,64,256]{3,2,1,0:T(8,128)(2,1)}, bf16[1,4,64,256]{3,2,1,0:T(8,128)(2,1)}, u32[]{:S(2)}, u32[]{:S(2)}) collective-permute-start(bf16[1,4,64,256]{3,2,1,0:T(8,128)(2,1)} %get-tuple-element.127), channel_id=1, source_target_pairs={{0,6},{2,4},{4,2},{6,0},{8,14},{10,12},{12,10},{14,8},{16,22},{18,... | collective-permute-start | bytes 393224 | tf_op jit(solution)/shard_map/ppermute | solution.py:395
  328.7 25.8 %collective-permute-start.20 = (bf16[1,4,64,256]{3,2,1,0:T(8,128)(2,1)}, bf16[1,4,64,256]{3,2,1,0:T(8,128)(2,1)}, u32[]{:S(2)}, u32[]{:S(2)}) collective-permute-start(bf16[1,4,64,256]{3,2,1,0:T(8,128)(2,1)} %get-tuple-element.128), channel_id=1, source_target_pairs={{0,8},{2,10},{4,12},{6,14},{8,0},{10,2},{12,4},{14,6},{16,24},{18,... | collective-permute-start | bytes 393224 | tf_op jit(solution)/shard_map/ppermute | solution.py:395
  328.7 25.8 %collective-permute-start.21 = (bf16[1,4,64,256]{3,2,1,0:T(8,128)(2,1)}, bf16[1,4,64,256]{3,2,1,0:T(8,128)(2,1)}, u32[]{:S(2)}, u32[]{:S(2)}) collective-permute-start(bf16[1,4,64,256]{3,2,1,0:T(8,128)(2,1)} %get-tuple-element.129), channel_id=1, source_target_pairs={{0,10},{2,8},{4,14},{6,12},{8,2},{10,0},{12,6},{14,4},{16,26},{18,... | collective-permute-start | bytes 393224 | tf_op jit(solution)/shard_map/ppermute | solution.py:395
  353.2 63.3 %collective-permute-start.16 = (bf16[2,4,256,256]{3,2,1,0:T(8,128)(2,1)}, bf16[2,4,256,256]{3,2,1,0:T(8,128)(2,1)}, u32[]{:S(2)}, u32[]{:S(2)}) collective-permute-start(bf16[2,4,256,256]{3,2,1,0:T(8,128)(2,1)} %get-tuple-element.124), channel_id=1, source_target_pairs={{0,1},{1,0},{2,3},{3,2},{4,5},{5,4},{6,7},{7,6},{8,9},{9,8},{10,11... | collective-permute-start | bytes 3145736 | tf_op jit(solution)/shard_map/ppermute | solution.py:395
  357.2 27.1 %collective-permute-start.26 = (bf16[1,4,64,256]{3,2,1,0:T(8,128)(2,1)}, bf16[1,4,64,256]{3,2,1,0:T(8,128)(2,1)}, u32[]{:S(2)}, u32[]{:S(2)}) collective-permute-start(bf16[1,4,64,256]{3,2,1,0:T(8,128)(2,1)} %get-tuple-element.134), channel_id=1, source_target_pairs={{0,20},{2,22},{4,16},{6,18},{8,28},{10,30},{12,24},{14,26},{16,4},... | collective-permute-start | bytes 393224 | tf_op jit(solution)/shard_map/ppermute | solution.py:395
  358.0 29.2 %collective-permute-start.27 = (bf16[1,4,64,256]{3,2,1,0:T(8,128)(2,1)}, bf16[1,4,64,256]{3,2,1,0:T(8,128)(2,1)}, u32[]{:S(2)}, u32[]{:S(2)}) collective-permute-start(bf16[1,4,64,256]{3,2,1,0:T(8,128)(2,1)} %get-tuple-element.135), channel_id=1, source_target_pairs={{0,22},{2,20},{4,18},{6,16},{8,30},{10,28},{12,26},{14,24},{16,6},... | collective-permute-start | bytes 393224 | tf_op jit(solution)/shard_map/ppermute | solution.py:395
  432.5 46.3 %collective-permute-start.33 = (bf16[4,4,256,256]{3,2,1,0:T(8,128)(2,1)}, bf16[4,4,256,256]{3,2,1,0:T(8,128)(2,1)}, u32[]{:S(2)}, u32[]{:S(2)}) collective-permute-start(bf16[4,4,256,256]{3,2,1,0:T(8,128)(2,1)} %get-tuple-element.143), channel_id=1, source_target_pairs={{0,1},{1,0},{2,3},{3,2},{4,5},{5,4},{6,7},{7,6},{8,9},{9,8},{10,11... | collective-permute-start | bytes 6291464 | tf_op jit(solution)/shard_map/ppermute | solution.py:395
  503.3 327.2 %all-to-all-start.2 = ((bf16[16,4,2,128,256]{4,3,2,1,0:T(8,128)(2,1)}), bf16[16,4,2,128,256]{4,3,2,1,0:T(8,128)(2,1)}, u32[]{:S(2)}, u32[]{:S(2)}) async-start(bf16[16,4,2,128,256]{4,3,2,1,0:T(8,128)(2,1)} %shard_map.59.refs_3_), calls=%async_computation.2 | async-start | bytes 16777216 | tf_op jit(solution)/shard_map/all_to_all | solution.py:400
  533.7 224.4 %collective-permute-start.34 = (bf16[3,4,256,256]{3,2,1,0:T(8,128)(2,1)}, bf16[3,4,256,256]{3,2,1,0:T(8,128)(2,1)}, u32[]{:S(2)}, u32[]{:S(2)}) collective-permute-start(bf16[3,4,256,256]{3,2,1,0:T(8,128)(2,1)} %get-tuple-element.145), channel_id=1, source_target_pairs={{0,1},{1,0},{2,3},{3,2},{4,5},{5,4},{6,7},{7,6},{8,9},{9,8},{10,11... | collective-permute-start | bytes 4718600 | tf_op jit(solution)/shard_map/ppermute | solution.py:395
  534.4 32.2 %collective-permute-start.36 = (bf16[1,4,64,256]{3,2,1,0:T(8,128)(2,1)}, bf16[1,4,64,256]{3,2,1,0:T(8,128)(2,1)}, u32[]{:S(2)}, u32[]{:S(2)}) collective-permute-start(bf16[1,4,64,256]{3,2,1,0:T(8,128)(2,1)} %get-tuple-element.147), channel_id=1, source_target_pairs={{0,4},{2,6},{4,0},{6,2},{8,12},{10,14},{12,8},{14,10},{16,20},{18,... | collective-permute-start | bytes 393224 | tf_op jit(solution)/shard_map/ppermute | solution.py:395
  536.0 34.0 %collective-permute-start.37 = (bf16[1,4,64,256]{3,2,1,0:T(8,128)(2,1)}, bf16[1,4,64,256]{3,2,1,0:T(8,128)(2,1)}, u32[]{:S(2)}, u32[]{:S(2)}) collective-permute-start(bf16[1,4,64,256]{3,2,1,0:T(8,128)(2,1)} %get-tuple-element.148), channel_id=1, source_target_pairs={{0,6},{2,4},{4,2},{6,0},{8,14},{10,12},{12,10},{14,8},{16,22},{18,... | collective-permute-start | bytes 393224 | tf_op jit(solution)/shard_map/ppermute | solution.py:395
  536.1 117.9 %collective-permute-start.38 = (bf16[1,4,64,256]{3,2,1,0:T(8,128)(2,1)}, bf16[1,4,64,256]{3,2,1,0:T(8,128)(2,1)}, u32[]{:S(2)}, u32[]{:S(2)}) collective-permute-start(bf16[1,4,64,256]{3,2,1,0:T(8,128)(2,1)} %get-tuple-element.149), channel_id=1, source_target_pairs={{0,8},{2,10},{4,12},{6,14},{8,0},{10,2},{12,4},{14,6},{16,24},{18,... | collective-permute-start | bytes 393224 | tf_op jit(solution)/shard_map/ppermute | solution.py:395
  539.0 118.9 %collective-permute-start.39 = (bf16[1,4,64,256]{3,2,1,0:T(8,128)(2,1)}, bf16[1,4,64,256]{3,2,1,0:T(8,128)(2,1)}, u32[]{:S(2)}, u32[]{:S(2)}) collective-permute-start(bf16[1,4,64,256]{3,2,1,0:T(8,128)(2,1)} %get-tuple-element.150), channel_id=1, source_target_pairs={{0,10},{2,8},{4,14},{6,12},{8,2},{10,0},{12,6},{14,4},{16,26},{18,... | collective-permute-start | bytes 393224 | tf_op jit(solution)/shard_map/ppermute | solution.py:395
  566.7 94.3 %collective-permute-start.40 = (bf16[1,4,64,256]{3,2,1,0:T(8,128)(2,1)}, bf16[1,4,64,256]{3,2,1,0:T(8,128)(2,1)}, u32[]{:S(2)}, u32[]{:S(2)}) collective-permute-start(bf16[1,4,64,256]{3,2,1,0:T(8,128)(2,1)} %get-tuple-element.151), channel_id=1, source_target_pairs={{0,12},{2,14},{4,8},{6,10},{8,4},{10,6},{12,0},{14,2},{16,28},{18,... | collective-permute-start | bytes 393224 | tf_op jit(solution)/shard_map/ppermute | solution.py:395
  570.0 94.3 %collective-permute-start.41 = (bf16[1,4,64,256]{3,2,1,0:T(8,128)(2,1)}, bf16[1,4,64,256]{3,2,1,0:T(8,128)(2,1)}, u32[]{:S(2)}, u32[]{:S(2)}) collective-permute-start(bf16[1,4,64,256]{3,2,1,0:T(8,128)(2,1)} %get-tuple-element.152), channel_id=1, source_target_pairs={{0,14},{2,12},{4,10},{6,8},{8,6},{10,4},{12,2},{14,0},{16,30},{18,... | collective-permute-start | bytes 393224 | tf_op jit(solution)/shard_map/ppermute | solution.py:395
  654.1 58.5 %collective-permute-start.42 = (bf16[1,4,64,256]{3,2,1,0:T(8,128)(2,1)}, bf16[1,4,64,256]{3,2,1,0:T(8,128)(2,1)}, u32[]{:S(2)}, u32[]{:S(2)}) collective-permute-start(bf16[1,4,64,256]{3,2,1,0:T(8,128)(2,1)} %get-tuple-element.153), channel_id=1, source_target_pairs={{0,16},{2,18},{4,20},{6,22},{8,24},{10,26},{12,28},{14,30},{16,0},... | collective-permute-start | bytes 393224 | tf_op jit(solution)/shard_map/ppermute | solution.py:395
  657.9 58.8 %collective-permute-start.43 = (bf16[1,4,64,256]{3,2,1,0:T(8,128)(2,1)}, bf16[1,4,64,256]{3,2,1,0:T(8,128)(2,1)}, u32[]{:S(2)}, u32[]{:S(2)}) collective-permute-start(bf16[1,4,64,256]{3,2,1,0:T(8,128)(2,1)} %get-tuple-element.154), channel_id=1, source_target_pairs={{0,18},{2,16},{4,22},{6,20},{8,26},{10,24},{12,30},{14,28},{16,2},... | collective-permute-start | bytes 393224 | tf_op jit(solution)/shard_map/ppermute | solution.py:395
  661.0 63.9 %collective-permute-start.44 = (bf16[1,4,64,256]{3,2,1,0:T(8,128)(2,1)}, bf16[1,4,64,256]{3,2,1,0:T(8,128)(2,1)}, u32[]{:S(2)}, u32[]{:S(2)}) collective-permute-start(bf16[1,4,64,256]{3,2,1,0:T(8,128)(2,1)} %get-tuple-element.155), channel_id=1, source_target_pairs={{0,20},{2,22},{4,16},{6,18},{8,28},{10,30},{12,24},{14,26},{16,4},... | collective-permute-start | bytes 393224 | tf_op jit(solution)/shard_map/ppermute | solution.py:395
  664.4 64.2 %collective-permute-start.45 = (bf16[1,4,64,256]{3,2,1,0:T(8,128)(2,1)}, bf16[1,4,64,256]{3,2,1,0:T(8,128)(2,1)}, u32[]{:S(2)}, u32[]{:S(2)}) collective-permute-start(bf16[1,4,64,256]{3,2,1,0:T(8,128)(2,1)} %get-tuple-element.156), channel_id=1, source_target_pairs={{0,22},{2,20},{4,18},{6,16},{8,30},{10,28},{12,26},{14,24},{16,6},... | collective-permute-start | bytes 393224 | tf_op jit(solution)/shard_map/ppermute | solution.py:395
  774.2 42.9 %collective-permute-start.67 = (bf16[2,4,256,256]{3,2,1,0:T(8,128)(2,1)}, bf16[2,4,256,256]{3,2,1,0:T(8,128)(2,1)}, u32[]{:S(2)}, u32[]{:S(2)}) collective-permute-start(bf16[2,4,256,256]{3,2,1,0:T(8,128)(2,1)} %get-tuple-element.182), channel_id=1, source_target_pairs={{0,1},{1,0},{2,3},{3,2},{4,5},{5,4},{6,7},{7,6},{8,9},{9,8},{10,11... | collective-permute-start | bytes 3145736 | tf_op jit(solution)/shard_map/ppermute | solution.py:395
  774.5 34.7 %collective-permute-start.68 = (bf16[1,4,256,256]{3,2,1,0:T(8,128)(2,1)}, bf16[1,4,256,256]{3,2,1,0:T(8,128)(2,1)}, u32[]{:S(2)}, u32[]{:S(2)}) collective-permute-start(bf16[1,4,256,256]{3,2,1,0:T(8,128)(2,1)} %get-tuple-element.184), channel_id=1, source_target_pairs={{0,1},{1,0},{2,3},{3,2},{4,5},{5,4},{6,7},{7,6},{8,9},{9,8},{10,11... | collective-permute-start | bytes 1572872 | tf_op jit(solution)/shard_map/ppermute | solution.py:395
  830.4 180.1 %all-to-all-start.3 = ((bf16[16,2,2,128,256]{4,3,2,1,0:T(8,128)(2,1)}), bf16[16,2,2,128,256]{4,3,2,1,0:T(8,128)(2,1)}, u32[]{:S(2)}, u32[]{:S(2)}) async-start(bf16[16,2,2,128,256]{4,3,2,1,0:T(8,128)(2,1)} %shard_map.65), calls=%async_computation.3 | async-start | bytes 8388608 | tf_op jit(solution)/shard_map/all_to_all | solution.py:400
  843.6 27.9 %collective-permute-start.70 = (bf16[1,2,128,256]{3,2,1,0:T(8,128)(2,1)S(1)}, bf16[1,2,128,256]{3,2,1,0:T(8,128)(2,1)}, u32[]{:S(2)}, u32[]{:S(2)}) collective-permute-start(bf16[1,2,128,256]{3,2,1,0:T(8,128)(2,1)S(1)} %copy-done.15), channel_id=1, source_target_pairs={{0,4},{2,6},{4,0},{6,2},{8,12},{10,14},{12,8},{14,10},{16,20},{18,... | collective-permute-start | bytes 393224 | tf_op jit(solution)/shard_map/ppermute | solution.py:395
  845.2 29.6 %collective-permute-start.71 = (bf16[1,2,128,256]{3,2,1,0:T(8,128)(2,1)S(1)}, bf16[1,2,128,256]{3,2,1,0:T(8,128)(2,1)}, u32[]{:S(2)}, u32[]{:S(2)}) collective-permute-start(bf16[1,2,128,256]{3,2,1,0:T(8,128)(2,1)S(1)} %copy-done.13), channel_id=1, source_target_pairs={{0,6},{2,4},{4,2},{6,0},{8,14},{10,12},{12,10},{14,8},{16,22},{18,... | collective-permute-start | bytes 393224 | tf_op jit(solution)/shard_map/ppermute | solution.py:395
  845.3 68.5 %collective-permute-start.72 = (bf16[1,2,128,256]{3,2,1,0:T(8,128)(2,1)S(1)}, bf16[1,2,128,256]{3,2,1,0:T(8,128)(2,1)}, u32[]{:S(2)}, u32[]{:S(2)}) collective-permute-start(bf16[1,2,128,256]{3,2,1,0:T(8,128)(2,1)S(1)} %copy-done.12), channel_id=1, source_target_pairs={{0,8},{2,10},{4,12},{6,14},{8,0},{10,2},{12,4},{14,6},{16,24},{18,... | collective-permute-start | bytes 393224 | tf_op jit(solution)/shard_map/ppermute | solution.py:395
  856.4 62.8 %collective-permute-start.73 = (bf16[1,2,128,256]{3,2,1,0:T(8,128)(2,1)S(1)}, bf16[1,2,128,256]{3,2,1,0:T(8,128)(2,1)}, u32[]{:S(2)}, u32[]{:S(2)}) collective-permute-start(bf16[1,2,128,256]{3,2,1,0:T(8,128)(2,1)S(1)} %copy-done.10), channel_id=1, source_target_pairs={{0,10},{2,8},{4,14},{6,12},{8,2},{10,0},{12,6},{14,4},{16,26},{18,... | collective-permute-start | bytes 393224 | tf_op jit(solution)/shard_map/ppermute | solution.py:395
  858.6 64.1 %collective-permute-start.74 = (bf16[1,2,128,256]{3,2,1,0:T(8,128)(2,1)S(1)}, bf16[1,2,128,256]{3,2,1,0:T(8,128)(2,1)}, u32[]{:S(2)}, u32[]{:S(2)}) collective-permute-start(bf16[1,2,128,256]{3,2,1,0:T(8,128)(2,1)S(1)} %copy-done.9), channel_id=1, source_target_pairs={{0,12},{2,14},{4,8},{6,10},{8,4},{10,6},{12,0},{14,2},{16,28},{18,... | collective-permute-start | bytes 393224 | tf_op jit(solution)/shard_map/ppermute | solution.py:395
  871.5 64.9 %collective-permute-start.75 = (bf16[1,2,128,256]{3,2,1,0:T(8,128)(2,1)}, bf16[1,2,128,256]{3,2,1,0:T(8,128)(2,1)}, u32[]{:S(2)}, u32[]{:S(2)}) collective-permute-start(bf16[1,2,128,256]{3,2,1,0:T(8,128)(2,1)} %get-tuple-element.192), channel_id=1, source_target_pairs={{0,14},{2,12},{4,10},{6,8},{8,6},{10,4},{12,2},{14,0},{16,30},{18,... | collective-permute-start | bytes 393224 | tf_op jit(solution)/shard_map/ppermute | solution.py:395
  874.9 78.1 %collective-permute-start.76 = (bf16[1,2,128,256]{3,2,1,0:T(8,128)(2,1)}, bf16[1,2,128,256]{3,2,1,0:T(8,128)(2,1)}, u32[]{:S(2)}, u32[]{:S(2)}) collective-permute-start(bf16[1,2,128,256]{3,2,1,0:T(8,128)(2,1)} %get-tuple-element.193), channel_id=1, source_target_pairs={{0,16},{2,18},{4,20},{6,22},{8,24},{10,26},{12,28},{14,30},{16,0},... | collective-permute-start | bytes 393224 | tf_op jit(solution)/shard_map/ppermute | solution.py:395
  913.8 44.0 %collective-permute-start.77 = (bf16[1,2,128,256]{3,2,1,0:T(8,128)(2,1)}, bf16[1,2,128,256]{3,2,1,0:T(8,128)(2,1)}, u32[]{:S(2)}, u32[]{:S(2)}) collective-permute-start(bf16[1,2,128,256]{3,2,1,0:T(8,128)(2,1)} %get-tuple-element.194), channel_id=1, source_target_pairs={{0,18},{2,16},{4,22},{6,20},{8,26},{10,24},{12,30},{14,28},{16,2},... | collective-permute-start | bytes 393224 | tf_op jit(solution)/shard_map/ppermute | solution.py:395
  919.2 43.1 %collective-permute-start.78 = (bf16[1,2,128,256]{3,2,1,0:T(8,128)(2,1)}, bf16[1,2,128,256]{3,2,1,0:T(8,128)(2,1)}, u32[]{:S(2)}, u32[]{:S(2)}) collective-permute-start(bf16[1,2,128,256]{3,2,1,0:T(8,128)(2,1)} %get-tuple-element.195), channel_id=1, source_target_pairs={{0,20},{2,22},{4,16},{6,18},{8,28},{10,30},{12,24},{14,26},{16,4},... | collective-permute-start | bytes 393224 | tf_op jit(solution)/shard_map/ppermute | solution.py:395
  922.7 47.2 %collective-permute-start.79 = (bf16[1,2,128,256]{3,2,1,0:T(8,128)(2,1)}, bf16[1,2,128,256]{3,2,1,0:T(8,128)(2,1)}, u32[]{:S(2)}, u32[]{:S(2)}) collective-permute-start(bf16[1,2,128,256]{3,2,1,0:T(8,128)(2,1)} %get-tuple-element.196), channel_id=1, source_target_pairs={{0,22},{2,20},{4,18},{6,16},{8,30},{10,28},{12,26},{14,24},{16,6},... | collective-permute-start | bytes 393224 | tf_op jit(solution)/shard_map/ppermute | solution.py:395
  936.3 52.8 %collective-permute-start.80 = (bf16[1,2,128,256]{3,2,1,0:T(8,128)(2,1)}, bf16[1,2,128,256]{3,2,1,0:T(8,128)(2,1)}, u32[]{:S(2)}, u32[]{:S(2)}) collective-permute-start(bf16[1,2,128,256]{3,2,1,0:T(8,128)(2,1)} %get-tuple-element.197), channel_id=1, source_target_pairs={{0,24},{2,26},{4,28},{6,30},{8,16},{10,18},{12,20},{14,22},{16,8},... | collective-permute-start | bytes 393224 | tf_op jit(solution)/shard_map/ppermute | solution.py:395
  952.9 36.2 %collective-permute-start.81 = (bf16[1,2,128,256]{3,2,1,0:T(8,128)(2,1)}, bf16[1,2,128,256]{3,2,1,0:T(8,128)(2,1)}, u32[]{:S(2)}, u32[]{:S(2)}) collective-permute-start(bf16[1,2,128,256]{3,2,1,0:T(8,128)(2,1)} %get-tuple-element.198), channel_id=1, source_target_pairs={{0,26},{2,24},{4,30},{6,28},{8,18},{10,16},{12,22},{14,20},{16,10}... | collective-permute-start | bytes 393224 | tf_op jit(solution)/shard_map/ppermute | solution.py:395
  957.8 33.5 %collective-permute-start.82 = (bf16[1,2,128,256]{3,2,1,0:T(8,128)(2,1)}, bf16[1,2,128,256]{3,2,1,0:T(8,128)(2,1)}, u32[]{:S(2)}, u32[]{:S(2)}) collective-permute-start(bf16[1,2,128,256]{3,2,1,0:T(8,128)(2,1)} %get-tuple-element.199), channel_id=1, source_target_pairs={{0,28},{2,30},{4,24},{6,26},{8,20},{10,22},{12,16},{14,18},{16,12}... | collective-permute-start | bytes 393224 | tf_op jit(solution)/shard_map/ppermute | solution.py:395
  962.3 29.0 %collective-permute-start.83 = (bf16[1,2,128,256]{3,2,1,0:T(8,128)(2,1)}, bf16[1,2,128,256]{3,2,1,0:T(8,128)(2,1)}, u32[]{:S(2)}, u32[]{:S(2)}) collective-permute-start(bf16[1,2,128,256]{3,2,1,0:T(8,128)(2,1)} %get-tuple-element.200), channel_id=1, source_target_pairs={{0,30},{2,28},{4,26},{6,24},{8,22},{10,20},{12,18},{14,16},{16,14}... | collective-permute-start | bytes 393224 | tf_op jit(solution)/shard_map/ppermute | solution.py:395
  1007.9 29.1 %collective-permute-start.66 = (bf16[1,2,128,256]{3,2,1,0:T(8,128)(2,1)}, bf16[1,2,128,256]{3,2,1,0:T(8,128)(2,1)}, u32[]{:S(2)}, u32[]{:S(2)}) collective-permute-start(bf16[1,2,128,256]{3,2,1,0:T(8,128)(2,1)} %get-tuple-element.180), channel_id=1, source_target_pairs={{0,30},{2,28},{4,26},{6,24},{8,22},{10,20},{12,18},{14,16},{16,14}... | collective-permute-start | bytes 393224 | tf_op jit(solution)/shard_map/ppermute | solution.py:395
  1021.5 23.1 %collective-permute-start.53 = (bf16[1,2,128,256]{3,2,1,0:T(8,128)(2,1)}, bf16[1,2,128,256]{3,2,1,0:T(8,128)(2,1)}, u32[]{:S(2)}, u32[]{:S(2)}) collective-permute-start(bf16[1,2,128,256]{3,2,1,0:T(8,128)(2,1)} %get-tuple-element.166), channel_id=1, source_target_pairs={{0,18},{2,16},{4,22},{6,20},{8,26},{10,24},{12,30},{14,28},{16,2},... | collective-permute-start | bytes 393224 | tf_op jit(solution)/shard_map/ppermute | solution.py:395
  1023.8 26.0 %collective-permute-start.55 = (bf16[1,2,128,256]{3,2,1,0:T(8,128)(2,1)}, bf16[1,2,128,256]{3,2,1,0:T(8,128)(2,1)}, u32[]{:S(2)}, u32[]{:S(2)}) collective-permute-start(bf16[1,2,128,256]{3,2,1,0:T(8,128)(2,1)} %get-tuple-element.168), channel_id=1, source_target_pairs={{0,22},{2,20},{4,18},{6,16},{8,30},{10,28},{12,26},{14,24},{16,6},... | collective-permute-start | bytes 393224 | tf_op jit(solution)/shard_map/ppermute | solution.py:395
  (57 other events, 2139.8 us)
